TPU v7x, 32 devices: a whole 2x2x4 slice. The times are simulated.
32 devices in a mesh: grp: 2 (over x), src: 8 (over z, y), tgt: 2 (over core).
Axes of the slice: x: 2, y: 2, z: 4, core: 2. Of those that a mesh axis runs over, the one named last changes fastest.
Arguments:
- densities: bfloat16 [512, 32768], P('grp', ('src', 'tgt')), parts along dimension 0, may hold values from -6 to 6
- compress: bfloat16 [65536, 2, 256], P(('grp', 'src', 'tgt')), parts along dimension 0, may hold values from -0.0625 to 0.0625
- level_a: bfloat16 [6, 2048, 2, 256], P('grp', 'src', None, 'tgt'), parts along dimension 0, may hold values from -0.1875 to 0.1875
- level_b: bfloat16 [6, 2048, 2, 256], P('grp', 'src', None, 'tgt'), parts along dimension 0, may hold values from -0.1875 to 0.1875
- expand: bfloat16 [4096, 2, 4096], P(('grp', 'src'), None, 'tgt'), parts along dimension 0, may hold values from -0.25 to 0.25
- near_tiles: bfloat16 [2048, 128, 2, 128], P(('grp', 'src', 'tgt')), parts along dimension 0, may hold values from -0.375 to 0.375
- tile_pairs: int32 [2048, 2], P(('grp', 'src', 'tgt')), parts along dimension 0, may hold values from 0 to 15
- tile_count: int32 [32], P(('grp', 'src', 'tgt')), parts along dimension 0, may hold values from 1 to 63, as said below
- cluster_order: int32 [32, 16], P(('grp', 'src', 'tgt')), parts along dimension 0, may hold values from 0 to 15, each once within a row
Outputs:
- potential: bfloat16 [512, 32768], P('grp', ('src', 'tgt')), parts along dimension 0
There are 2 independent parts, one for each index of `grp`. A program takes and returns all parts, laid end to end along the dimension named above; each array names one. Nothing has to cross between parts.
Inputs may be any that keep to these rules, and one draw needn't show every extreme that they name: For every i below 8, tile_count[i] + tile_count[i + 8] == 64; slots at or beyond a device's count are unused. `cluster_order`: each row is a permutation.
All inputs are finite; a program needn't handle non-finite values.
Results may differ from a plain program's by a relative error of at most 0.007.
Values may be sent and summed in bfloat16 or wider, within the bound.
No kernel may reach another device: no remote copies, remote signals or barrier semaphores. Data moves between devices by JAX's collectives and lax.ppermute only.
A program may use at most 128 MiB of HBM per device.

v0:
```python
import jax
import jax.numpy as jnp
from jax import lax
from jax.sharding import PartitionSpec as P


def swapped(value, axis, bit):
    mask = 2**bit
    pairs = [(source, source ^ mask) for source in range(lax.axis_size(axis))]
    return lax.ppermute(value, axis, pairs)


def complex_product(operand, matrix):
    product = jnp.dot(operand, matrix, preferred_element_type=jnp.float32)
    half_rows = operand.shape[0] // 2
    half_cols = matrix.shape[1] // 2
    real_part = product[:half_rows, :half_cols] - product[half_rows:, half_cols:]
    imag_part = product[:half_rows, half_cols:] + product[half_rows:, :half_cols]
    return jnp.concatenate([real_part, imag_part], axis=0)


def near_sum(sources, tile_blocks, source_ids, target_ids, active, targets):
    half_rows = sources.shape[0] // 2
    cluster_size = tile_blocks.shape[1]
    picked = jnp.take(sources, source_ids, axis=1)
    product = jnp.einsum("rjp,jpq->rjq", picked, tile_blocks, preferred_element_type=jnp.float32)
    real_part = product[:half_rows, :, :cluster_size] - product[half_rows:, :, cluster_size:]
    imag_part = product[:half_rows, :, cluster_size:] + product[half_rows:, :, :cluster_size]
    joined = jnp.concatenate([real_part, imag_part], axis=0)
    chooser = (
        (target_ids[:, None] == jnp.arange(targets, dtype=jnp.int32)[None, :]) & active[:, None]
    ).astype(jnp.float32)
    return jnp.einsum("rjq,jc->rcq", joined, chooser, precision=lax.Precision.HIGHEST)


def shards(
    densities, compress, level_a, level_b, expand, near_tiles, tile_pairs, tile_count, cluster_order
):
    row_count, points = densities.shape
    rank = compress.shape[2]
    sections = level_a.shape[0]
    partial_value = complex_product(densities, compress.reshape(points, 2 * rank))
    matrices_a = level_a.reshape(sections, rank, -1)
    matrices_b = level_b.reshape(sections, rank, -1)
    coefficients = lax.psum(partial_value, "tgt").astype(jnp.bfloat16)
    for section in range(sections):
        partner_coeff = swapped(coefficients, "src", section)
        updated = complex_product(coefficients, matrices_a[section]) + complex_product(
            partner_coeff, matrices_b[section]
        )
        coefficients = lax.all_gather(updated.astype(jnp.bfloat16), "tgt", axis=1, tiled=True)
    far_field = complex_product(coefficients, expand.reshape(rank, 2 * points))
    clusters = cluster_order.shape[1]
    cluster_size = points // clusters
    placed = (
        jnp.zeros((row_count, clusters, cluster_size), jnp.float32)
        .at[:, cluster_order[0], :]
        .set(far_field.reshape(row_count, clusters, cluster_size))
    )
    slots = near_tiles.shape[0]
    blocks = near_tiles.reshape(slots, cluster_size, 2 * cluster_size)
    sources = densities.reshape(row_count, clusters, cluster_size)
    count = tile_count[0]
    active = jnp.arange(slots, dtype=jnp.int32) < count
    near_field = near_sum(sources, blocks, tile_pairs[:, 1], tile_pairs[:, 0], active, clusters)
    return (placed + near_field).reshape(row_count, points).astype(jnp.bfloat16)


def solution(mesh):
    placed = (
        P("grp", ("src", "tgt")),
        P(("grp", "src", "tgt"), None, None),
        P("grp", "src", None, "tgt"),
        P("grp", "src", None, "tgt"),
        P(("grp", "src"), None, "tgt"),
        P(("grp", "src", "tgt"), None, None, None),
        P(("grp", "src", "tgt"), None),
        P(("grp", "src", "tgt")),
        P(("grp", "src", "tgt"), None),
    )
    return jax.shard_map(
        shards, mesh=mesh, in_specs=placed, out_specs=P("grp", ("src", "tgt")), check_vma=False
    )
```

profile of v0, /device:TPU:0, one launch (start us, length us, event | category | flops | bytes accessed | tf_op | source)
XLA Modules:
  0.0 93.4 jit_solution(9930778493908321840)
XLA Ops:
  0.0 2.1 %copy.22 = bf16[256,8,2,256]{3,1,2,0:T(8,128)(2,1)S(1)} copy(bf16[256,8,2,256]{3,2,1,0:T(2,128)(2,1)} %bitcast.84) | data formatting | bytes 4194304
  2.2 0.7 fusion.40
  2.9 4.5 %all-reduce.1 = bf16[256,256]{1,0:T(8,128)(2,1)S(1)} all-reduce(f32[256,256]{1,0:T(8,128)S(1)} %pad_maximum_fusion.1), channel_id=1, replica_groups=mesh['grp'=2,'src'=8,'tgt'=2] {'tgt'}, use_global_device_ids=true, to_apply=%region_0.0 | all-reduce | flops 65536 | bytes 393216 | tf_op jit(solution)/shard_map/psum | solution.py:45
  7.5 2.7 %collective-permute-start = (bf16[256,256]{1,0:T(8,128)(2,1)S(1)}, bf16[256,256]{1,0:T(8,128)(2,1)S(1)}, u32[]{:S(2)}, u32[]{:S(2)}) collective-permute-start(bf16[256,256]{1,0:T(8,128)(2,1)S(1)} %all-reduce.1), channel_id=1, source_target_pairs={{0,2},{2,0},{4,6},{6,4},{8,10},{10,8},{12,14},{14,12},{1,3},{3,1},... | collective-permute-start | bytes 393224 | tf_op jit(solution)/shard_map/ppermute | solution.py:10
  10.2 0.5 copy.17
  10.7 0.3 fusion.38
  11.0 1.3 %fusion.39 = (bf16[1,256,2,128]{3,2,1,0:T(2,128)(2,1)S(1)}, bf16[1,256,2,128]{3,2,1,0:T(2,128)(2,1)S(1)}, bf16[1,256,2,128]{3,2,1,0:T(2,128)(2,1)S(1)}) fusion(bf16[3,256,2,128]{3,2,1,0:T(2,128)(2,1)} %param.11), kind=kLoop, calls=%fused_computation.73 | loop fusion | bytes 786432 | tf_op jit(solution)/shard_map/slice | solution.py:48
  12.3 0.2 fusion.24
  12.6 0.7 copy.18
  13.2 7.6 %reshape.71 = bf16[64,128,256]{2,1,0:T(8,128)(2,1)} reshape(bf16[64,128,2,128]{3,2,1,0:T(2,128)(2,1)} %param.14) | data formatting | bytes 8388608 | tf_op jit(solution)/shard_map/reshape | solution.py:61
  20.8 3.0 %gather_fusion = bf16[64,256,128]{2,1,0:T(8,128)(2,1)} fusion(bf16[256,16,128]{2,0,1:T(8,128)(2,1)S(1)} %copy.18, s32[1024]{0:T(1024)S(1)} %pad_clamp_fusion), kind=kCustom, calls=%fused_computation | custom fusion | bytes 8388864 | tf_op jit(solution)/shard_map/jit(_take)/gather | solution.py:25
  23.9 11.6 %convolution_bitcast_fusion = f32[256,64,256]{2,0,1:T(8,128)} fusion(bf16[64,128,256]{2,1,0:T(8,128)(2,1)} %reshape.71, bf16[64,256,128]{2,1,0:T(8,128)(2,1)} %gather_fusion, pred[64]{0:T(512)(128)(4,1)S(1)} %and_bitcast_fusion), kind=kOutput, calls=%fused_computation.2 | convolution fusion | flops 1075838976 | bytes 25165888 | tf_op jit(solution)/shard_map/rjp,jpq->rjq/dot_general | solution.py:26
  35.5 10.1 %slice_subtract_fusion = (f32[128,64,128]{2,0,1:T(8,128)S(1)}, f32[128,64,128]{2,0,1:T(8,128)}) fusion(f32[256,64,256]{2,0,1:T(8,128)} %convolution_bitcast_fusion), kind=kLoop, calls=%fused_computation.7 | loop fusion | flops 2097152 | bytes 25165824 | tf_op jit(solution)/shard_map/sub | solution.py:27
  45.6 6.3 %pad_maximum_fusion = f32[256,64,128]{2,0,1:T(8,128)} fusion(f32[128,64,128]{2,0,1:T(8,128)} %get-tuple-element.6, f32[128,64,128]{2,0,1:T(8,128)S(1)} %get-tuple-element.5), kind=kLoop, calls=%fused_computation.3 | loop fusion | flops 2097152 | bytes 16777216 | tf_op jit(solution)/shard_map/concatenate | solution.py:29
  51.9 0.9 copy.29
  53.5 0.2 fusion.21
  53.8 1.9 %all_gather.9 = bf16[256,256]{1,0:T(8,128)(2,1)S(1)} all-gather(bf16[256,128]{1,0:T(8,128)(2,1)S(1)} %fusion.27), channel_id=1, replica_groups=mesh['grp'=2,'src'=8,'tgt'=2] {'tgt'}, dimensions={1}, use_global_device_ids=true | all-gather | bytes 196608 | tf_op jit(solution)/shard_map/all_gather | solution.py:51
  55.7 1.6 %collective-permute-start.1 = (bf16[256,256]{1,0:T(8,128)(2,1)S(1)}, bf16[256,256]{1,0:T(8,128)(2,1)S(1)}, u32[]{:S(2)}, u32[]{:S(2)}) collective-permute-start(bf16[256,256]{1,0:T(8,128)(2,1)S(1)} %all_gather.9), channel_id=1, source_target_pairs={{0,4},{2,6},{4,0},{6,2},{8,12},{10,14},{12,8},{14,10},{1,5},{3,7},... | collective-permute-start | bytes 393224 | tf_op jit(solution)/shard_map/ppermute | solution.py:10
  57.5 3.8 %collective-permute-done.1 = bf16[256,256]{1,0:T(8,128)(2,1)S(1)} collective-permute-done((bf16[256,256]{1,0:T(8,128)(2,1)S(1)}, bf16[256,256]{1,0:T(8,128)(2,1)S(1)}, u32[]{:S(2)}, u32[]{:S(2)}) %collective-permute-start.1) | collective-permute-done | bytes 131104 | tf_op jit(solution)/shard_map/ppermute | solution.py:10
  61.2 0.2 fusion.15
  61.5 1.9 %all_gather.10 = bf16[256,256]{1,0:T(8,128)(2,1)S(1)} all-gather(bf16[256,128]{1,0:T(8,128)(2,1)S(1)} %fusion.28), channel_id=1, replica_groups=mesh['grp'=2,'src'=8,'tgt'=2] {'tgt'}, dimensions={1}, use_global_device_ids=true | all-gather | bytes 196608 | tf_op jit(solution)/shard_map/all_gather | solution.py:51
  63.4 2.6 %collective-permute-start.2 = (bf16[256,256]{1,0:T(8,128)(2,1)S(1)}, bf16[256,256]{1,0:T(8,128)(2,1)S(1)}, u32[]{:S(2)}, u32[]{:S(2)}) collective-permute-start(bf16[256,256]{1,0:T(8,128)(2,1)S(1)} %all_gather.10), channel_id=1, source_target_pairs={{0,8},{2,10},{4,12},{6,14},{8,0},{10,2},{12,4},{14,6},{1,9},{3,11}... | collective-permute-start | bytes 393224 | tf_op jit(solution)/shard_map/ppermute | solution.py:10
  66.2 6.5 %collective-permute-done.2 = bf16[256,256]{1,0:T(8,128)(2,1)S(1)} collective-permute-done((bf16[256,256]{1,0:T(8,128)(2,1)S(1)}, bf16[256,256]{1,0:T(8,128)(2,1)S(1)}, u32[]{:S(2)}, u32[]{:S(2)}) %collective-permute-start.2) | collective-permute-done | bytes 131104 | tf_op jit(solution)/shard_map/ppermute | solution.py:10
  72.7 0.2 fusion.9
  72.9 2.1 %all_gather.11 = bf16[256,256]{1,0:T(8,128)(2,1)S(1)} all-gather(bf16[256,128]{1,0:T(8,128)(2,1)S(1)} %fusion.29), channel_id=1, replica_groups=mesh['grp'=2,'src'=8,'tgt'=2] {'tgt'}, dimensions={1}, use_global_device_ids=true | all-gather | bytes 196608 | tf_op jit(solution)/shard_map/all_gather | solution.py:51
  75.0 0.7 fusion.41
  75.8 0.3 slice_subtract_fusion.1
  76.1 1.6 %bitcast_bitcast_fusion = f32[16,256,128]{2,1,0:T(8,128)} fusion(f32[128,2048]{1,0:T(8,128)S(1)} %get-tuple-element.8, f32[128,2048]{1,0:T(8,128)S(1)} %get-tuple-element.7), kind=kLoop, calls=%fused_computation.11 | loop fusion | flops 524288 | bytes 4194304 | tf_op jit(solution)/shard_map/reshape | solution.py:58
  77.7 0.2 broadcast_in_dim.16
  77.9 2.7 %scatter_fusion = f32[256,16,128]{2,0,1:T(8,128)S(1)} fusion(f32[256,16,128]{2,0,1:T(8,128)S(1)} %broadcast_in_dim.16, s32[16]{0:T(128)S(1)} %fusion.35, f32[16,256,128]{2,1,0:T(8,128)} %bitcast_bitcast_fusion), kind=kCustom, calls=%fused_computation.1 | custom fusion | bytes 6291520 | tf_op jit(solution)/shard_map/scatter | solution.py:58
  80.6 11.6 %fusion.5 = bf16[256,16,128]{2,1,0:T(8,128)(2,1)S(1)} fusion(f32[256,16,128]{2,0,1:T(8,128)S(1)} %scatter_fusion, f32[256,64,128]{2,0,1:T(8,128)} %pad_maximum_fusion, s32[64]{0:T(128)S(1)} %get-tuple-element.29, pred[64]{0:T(512)(128)(4,1)S(1)} %iota_compare_fusion.1), kind=kOutput, calls=%fused_computation.14 | convolution fusion | flops 403703808 | bytes 11534656 | tf_op jit(solution)/shard_map/rjq,jc->rcq/dot_general | solution.py:33
  92.2 1.2 %copy.62 = bf16[32,8,16,128]{3,1,2,0:T(8,128)(2,1)} copy(bf16[32,8,16,128]{3,2,1,0:T(8,128)(2,1)S(1)} %bitcast.82) | data formatting | bytes 2097152
  (29 shorter events, 0.6 us)
Async XLA Ops:
  0.0 2.2 %copy-start.1 = (bf16[256,2048]{1,0:T(8,128)(2,1)S(1)}, bf16[256,2048]{1,0:T(8,128)(2,1)}, u32[]{:S(2)}) copy-start(bf16[256,2048]{1,0:T(8,128)(2,1)} %param.9) | copy-start | bytes 3145732
  2.1 8.6 %copy-start.3 = (s32[64,2]{0,1:T(2,128)S(1)}, s32[64,2]{0,1:T(2,128)}, u32[]{:S(2)}) copy-start(s32[64,2]{0,1:T(2,128)} %param.15) | copy-start | bytes 1540
  2.1 8.6 %copy-start.2 = (bf16[3,256,2,128]{3,2,1,0:T(2,128)(2,1)S(1)}, bf16[3,256,2,128]{3,2,1,0:T(2,128)(2,1)}, u32[]{:S(2)}) copy-start(bf16[3,256,2,128]{3,2,1,0:T(2,128)(2,1)} %param.12) | copy-start | bytes 1179652
  7.5 46.0 %collective-permute-start = (bf16[256,256]{1,0:T(8,128)(2,1)S(1)}, bf16[256,256]{1,0:T(8,128)(2,1)S(1)}, u32[]{:S(2)}, u32[]{:S(2)}) collective-permute-start(bf16[256,256]{1,0:T(8,128)(2,1)S(1)} %all-reduce.1), channel_id=1, source_target_pairs={{0,2},{2,0},{4,6},{6,4},{8,10},{10,8},{12,14},{14,12},{1,3},{3,1},... | collective-permute-start | bytes 393224 | tf_op jit(solution)/shard_map/ppermute | solution.py:10
  45.6 6.3 %copy-start.4 = (s32[1,16]{1,0:T(1,128)S(1)}, s32[1,16]{1,0:T(1,128)}, u32[]{:S(2)}) copy-start(s32[1,16]{1,0:T(1,128)} %param.17) | copy-start | bytes 196
  45.6 6.3 %copy-start = (bf16[256,2,2048]{2,1,0:T(2,128)(2,1)S(1)}, bf16[256,2,2048]{2,1,0:T(2,128)(2,1)}, u32[]{:S(2)}) copy-start(bf16[256,2,2048]{2,1,0:T(2,128)(2,1)} %param.13) | copy-start | bytes 6291460
  55.7 5.6 %collective-permute-start.1 = (bf16[256,256]{1,0:T(8,128)(2,1)S(1)}, bf16[256,256]{1,0:T(8,128)(2,1)S(1)}, u32[]{:S(2)}, u32[]{:S(2)}) collective-permute-start(bf16[256,256]{1,0:T(8,128)(2,1)S(1)} %all_gather.9), channel_id=1, source_target_pairs={{0,4},{2,6},{4,0},{6,2},{8,12},{10,14},{12,8},{14,10},{1,5},{3,7},... | collective-permute-start | bytes 393224 | tf_op jit(solution)/shard_map/ppermute | solution.py:10
  63.4 9.3 %collective-permute-start.2 = (bf16[256,256]{1,0:T(8,128)(2,1)S(1)}, bf16[256,256]{1,0:T(8,128)(2,1)S(1)}, u32[]{:S(2)}, u32[]{:S(2)}) collective-permute-start(bf16[256,256]{1,0:T(8,128)(2,1)S(1)} %all_gather.10), channel_id=1, source_target_pairs={{0,8},{2,10},{4,12},{6,14},{8,0},{10,2},{12,4},{14,6},{1,9},{3,11}... | collective-permute-start | bytes 393224 | tf_op jit(solution)/shard_map/ppermute | solution.py:10
where the time goes:
time: 93.8 us; the launch traced here: 93.4 us
  matrix products  25.7 us (27%)
  local copies, waits for them, and re-layouts  20.6 us (22%)
  other arithmetic  18.6 us (20%)
  blocking collectives  10.5 us (11%)
  waiting for transfers between devices  10.2 us (11%)
  starting transfers between devices  6.88 us (7%)
  between operations  0.95 us (1%)
    dot_general x1, matrix products, near_sum(): jnp.einsum('rjp,jpq->rjq', picked, tile_blocks, preferred_element_type=jn...  11.6 us
    dot_general x1, matrix products, near_sum(): jnp.einsum('rjq,jc->rcq', joined, chooser, precision=lax.Precision.HIGHEST)  11.6 us
    ppermute x3, waiting for transfers between devices, swapped(): return lax.ppermute(value, axis, pairs)  10.2 us
    sub x1, other arithmetic, near_sum(): product[:half_rows, :, :cluster_size]  10.1 us
    reshape x1, local copies, waits for them, and re-layouts, shards(): blocks = near_tiles.reshape(slots, cluster_size, 2 * cluster_size)  7.59 us
    ppermute x3, starting transfers between devices, swapped(): return lax.ppermute(value, axis, pairs)  6.88 us
    concatenate x1, other arithmetic, near_sum(): joined = jnp.concatenate([real_part, imag_part], axis=0)  6.32 us
    all_gather x3, blocking collectives, shards(): lax.all_gather(updated.astype(jnp.bfloat16), 'tgt', axis=1, tiled=True)  5.97 us
  transfers between devices with their start and end apart: 3, of which 2 were waited for; matrix products, arithmetic and copies ran while one was open for 46% of the time, Pallas kernels for 0%

commit v1 on v0

v1 whole, which is shorter than its diff:
```python
import functools

import jax
import jax.numpy as jnp
from jax import lax
from jax.experimental import pallas as pl
from jax.experimental.pallas import tpu as pltpu
from jax.sharding import PartitionSpec as P

VMEM = pltpu.VMEM
CHUNKS = 4
NEAR_CALLS = 3
UNROLL = 4


def in_vmem():
    return pl.BlockSpec(memory_space=pltpu.VMEM)


def in_smem():
    return pl.BlockSpec(memory_space=pltpu.SMEM)


def in_hbm():
    return pl.BlockSpec(memory_space=pltpu.HBM)


def swapped(value, axis, bit):
    mask = 2**bit
    pairs = [(source, source ^ mask) for source in range(lax.axis_size(axis))]
    return lax.ppermute(value, axis, pairs)


def paired(block):
    half = block.shape[0] // 2
    upper, lower = block[:half], block[half:]
    return jnp.concatenate(
        [jnp.concatenate([upper, -lower], axis=1), jnp.concatenate([lower, upper], axis=1)], axis=0
    )


def compress_kernel(clusters, core_ref, dens_hbm, comp_hbm, mixed_ref, keep_ref, send_ref, dens, comp, weave, total, sems):
    rows, points = dens.shape
    width = points // clusters
    rank = comp.shape[1]
    comp_flat = comp_hbm.reshape(2 * points, rank)
    step = points // CHUNKS
    copies = []
    for chunk in range(CHUNKS):
        columns = pl.ds(chunk * step, step)
        planes = pl.ds(2 * chunk * step, 2 * step)
        pair = (
            pltpu.make_async_copy(dens_hbm.at[:, columns], dens.at[:, columns], sems.at[chunk, 0]),
            pltpu.make_async_copy(comp_flat.at[planes, :], comp.at[planes, :], sems.at[chunk, 1]),
        )
        for copy in pair:
            copy.start()
        copies.append(pair)
    row_id = lax.broadcasted_iota(jnp.int32, (2 * width, 2 * width), 0)
    col_id = lax.broadcasted_iota(jnp.int32, (2 * width, 2 * width), 1)
    goal = jnp.where(row_id < width, 2 * row_id, 2 * (row_id - width) + 1)
    weave[...] = jnp.where(col_id == goal, 1.0, 0.0).astype(jnp.bfloat16)
    for chunk in range(CHUNKS):
        copies[chunk][0].wait()
        pieces = []
        for cluster in range(chunk * clusters // CHUNKS, (chunk + 1) * clusters // CHUNKS):
            block = paired(dens[:, cluster * width : (cluster + 1) * width])
            woven = jnp.dot(block, weave[...], preferred_element_type=jnp.float32).astype(jnp.bfloat16)
            mixed_ref[cluster] = woven
            pieces.append(woven)
        copies[chunk][1].wait()
        product = jnp.dot(
            jnp.concatenate(pieces, axis=1),
            comp[2 * chunk * step : 2 * (chunk + 1) * step, :],
            preferred_element_type=jnp.float32,
        )
        if chunk == 0:
            total[...] = product
        else:
            total[...] += product
    quarter = rows // 4
    core = core_ref[0]
    for part in range(2):
        mine = pl.ds(pl.multiple_of(2 * part * quarter + core * quarter, quarter), quarter)
        other = pl.ds(pl.multiple_of(2 * part * quarter + (1 - core) * quarter, quarter), quarter)
        keep_ref[part * quarter : (part + 1) * quarter, :] = total[mine, :]
        send_ref[part * quarter : (part + 1) * quarter, :] = total[other, :].astype(jnp.bfloat16)


def compress_call(core, densities, compress, clusters):
    rows, points = densities.shape
    rank = compress.shape[2]
    width = points // clusters
    return pl.pallas_call(
        functools.partial(compress_kernel, clusters),
        out_shape=(
            jax.ShapeDtypeStruct((clusters, rows, 2 * width), jnp.bfloat16),
            jax.ShapeDtypeStruct((rows // 2, rank), jnp.float32),
            jax.ShapeDtypeStruct((rows // 2, rank), jnp.bfloat16),
        ),
        in_specs=[in_smem(), in_hbm(), in_hbm()],
        out_specs=(in_vmem(), in_vmem(), in_vmem()),
        scratch_shapes=[
            VMEM((rows, points), jnp.bfloat16),
            VMEM((2 * points, rank), jnp.bfloat16),
            VMEM((2 * width, 2 * width), jnp.bfloat16),
            VMEM((rows, rank), jnp.float32),
            pltpu.SemaphoreType.DMA((CHUNKS, 2)),
        ],
        compiler_params=pltpu.CompilerParams(vmem_limit_bytes=16 << 20),
        name="compress",
    )(core, densities, compress)


def near_kernel(call, pairs_ref, count_ref, mixed_ref, tiles_ref, *refs):
    total = refs[-1]
    if call == 0:
        total[...] = jnp.zeros_like(total)
    clusters = total.shape[0] - 1
    slots = tiles_ref.shape[0]
    count = count_ref[0]
    first = (count * call) // NEAR_CALLS
    last = (count * (call + 1)) // NEAR_CALLS

    def body(trip, carry):
        base = first + trip * UNROLL
        for lane in range(UNROLL):
            slot = jnp.minimum(base + lane, slots - 1)
            target = jnp.where(base + lane < last, pairs_ref[slot, 0], clusters)
            total[target] += jnp.dot(
                mixed_ref[pairs_ref[slot, 1]], tiles_ref[slot], preferred_element_type=jnp.float32
            )
        return carry

    lax.fori_loop(0, (last - first + UNROLL - 1) // UNROLL, body, 0)


def near_call(call, pairs, count, mixed, tiles, total):
    clusters, rows, depth = mixed.shape
    width = tiles.shape[2]
    operands = [pairs, count, mixed, tiles]
    specs = [in_smem(), in_smem(), in_vmem(), in_vmem()]
    aliases = {}
    if total is not None:
        operands.append(total)
        specs.append(in_vmem())
        aliases = {4: 0}
    return pl.pallas_call(
        functools.partial(near_kernel, call),
        out_shape=jax.ShapeDtypeStruct((clusters + 1, rows, width), jnp.float32),
        in_specs=specs,
        out_specs=in_vmem(),
        input_output_aliases=aliases,
        cost_estimate=pl.CostEstimate(
            flops=2 * rows * depth * width * tiles.shape[0] // NEAR_CALLS, bytes_accessed=0, transcendentals=0
        ),
        compiler_params=pltpu.CompilerParams(vmem_limit_bytes=16 << 20),
        name=f"near{call}",
    )(*operands)


def expand_kernel(half_ref, order_ref, coeff_ref, matrix_ref, near_ref, *refs):
    out_hbm, rows_out, inverse, sems = refs[-4:]
    clusters = order_ref.shape[1]
    points = matrix_ref.shape[1]
    width = points // clusters
    rows = near_ref.shape[1]
    quarter = rows // 4
    half = half_ref[0]

    def note(cluster, carry):
        inverse[order_ref[0, cluster]] = cluster
        return carry

    lax.fori_loop(0, clusters, note, 0)
    lhs = paired(coeff_ref[...])
    group = clusters // CHUNKS
    copies = []
    for chunk in range(CHUNKS):
        blocks = []
        for place in range(chunk * group, (chunk + 1) * group):
            start = pl.multiple_of(inverse[place] * width, width)
            blocks.append(matrix_ref[:, pl.ds(start, width)])
        far = jnp.dot(lhs, jnp.concatenate(blocks, axis=1), preferred_element_type=jnp.float32)
        for part in range(2):
            source = pl.ds(pl.multiple_of(2 * part * quarter + half * quarter, quarter), quarter)
            for item in range(group):
                place = chunk * group + item
                value = far[part * quarter : (part + 1) * quarter, item * width : (item + 1) * width]
                rows_out[part * quarter : (part + 1) * quarter, place * width : (place + 1) * width] = (
                    value + near_ref[place, source, :]
                ).astype(jnp.bfloat16)
            columns = pl.ds(chunk * group * width, group * width)
            copy = pltpu.make_async_copy(
                rows_out.at[part * quarter : (part + 1) * quarter, columns],
                out_hbm.at[source, columns],
                sems.at[chunk, part],
            )
            copy.start()
            copies.append(copy)
    for copy in copies:
        copy.wait()


def expand_call(half, order, coefficients, matrix, near, result):
    clusters = order.shape[1]
    points = matrix.shape[1]
    rows = near.shape[1]
    operands = [half, order, coefficients, matrix, near]
    specs = [in_smem(), in_smem(), in_vmem(), in_vmem(), in_vmem()]
    aliases = {}
    if result is not None:
        operands.append(result)
        specs.append(in_hbm())
        aliases = {5: 0}
    return pl.pallas_call(
        expand_kernel,
        out_shape=jax.ShapeDtypeStruct((rows, points), jnp.bfloat16),
        in_specs=specs,
        out_specs=in_hbm(),
        input_output_aliases=aliases,
        scratch_shapes=[
            VMEM((rows // 2, points), jnp.bfloat16),
            pltpu.SMEM((clusters,), jnp.int32),
            pltpu.SemaphoreType.DMA((CHUNKS, 2)),
        ],
        compiler_params=pltpu.CompilerParams(vmem_limit_bytes=16 << 20),
        name="expand",
    )(*operands)


def shards(
    densities, compress, level_a, level_b, expand, near_tiles, tile_pairs, tile_count, cluster_order
):
    rows, points = densities.shape
    rank = compress.shape[2]
    sections = level_a.shape[0]
    clusters = cluster_order.shape[1]
    width = points // clusters
    slots = near_tiles.shape[0]
    core = lax.axis_index("tgt").astype(jnp.int32)
    mine = core.reshape(1)
    tiles = near_tiles.reshape(slots, 2 * width, width)

    mixed, keep, send = compress_call(mine, densities, compress, clusters)
    arrived = swapped(send, "tgt", 0)
    coefficients = (keep + arrived.astype(jnp.float32)).astype(jnp.bfloat16)

    def whole(matrix):
        other = swapped(matrix, "tgt", 0)
        first = jnp.where(core == 0, matrix, other)
        second = jnp.where(core == 0, other, matrix)
        joined = jnp.concatenate([first, second], axis=3)
        return joined.transpose(0, 2, 1, 3).reshape(sections, 2 * rank, rank)

    own_matrices, partner_matrices = whole(level_a), whole(level_b)
    matrix = expand.transpose(1, 0, 2).reshape(2 * rank, points)
    near = None
    for section in range(sections):
        partner = swapped(coefficients, "src", section)
        if section < NEAR_CALLS:
            near = near_call(section, tile_pairs, tile_count, mixed, tiles, near)
        updated = jnp.dot(
            paired(coefficients), own_matrices[section], preferred_element_type=jnp.float32
        ) + jnp.dot(paired(partner), partner_matrices[section], preferred_element_type=jnp.float32)
        coefficients = updated.astype(jnp.bfloat16)
    others = swapped(coefficients, "tgt", 0)
    result = expand_call(mine, cluster_order, coefficients, matrix, near, None)
    return expand_call(1 - mine, cluster_order, others, matrix, near, result)


def solution(mesh):
    placed = (
        P("grp", ("src", "tgt")),
        P(("grp", "src", "tgt"), None, None),
        P("grp", "src", None, "tgt"),
        P("grp", "src", None, "tgt"),
        P(("grp", "src"), None, "tgt"),
        P(("grp", "src", "tgt"), None, None, None),
        P(("grp", "src", "tgt"), None),
        P(("grp", "src", "tgt")),
        P(("grp", "src", "tgt"), None),
    )
    return jax.shard_map(
        shards, mesh=mesh, in_specs=placed, out_specs=P("grp", ("src", "tgt")), check_vma=False
    )
```

time: 93.8 us -> 44.4 us (0.47)
  matrix products: 25.7 us -> 1.14 us
  Pallas kernels: 0 us -> 18 us
  other arithmetic: 18.6 us -> 2.34 us
  local copies, waits for them, and re-layouts: 20.6 us -> 6.69 us
  blocking collectives: 10.5 us -> 0 us
  waiting for transfers between devices: 10.2 us -> 7.54 us
    dot_general x10 -> x6, matrix products: 25.7 us -> 1.14 us  [the longest x3 0.58 us: shards(): jnp.dot(paired(partner), partner_matrices[section], preferred_element_typ...]
    pallas_call x0 -> x6, Pallas kernels: none -> 18 us  [the longest x3 8.85 us: near_call(): pl.pallas_call(functools.partial(near_kernel, call), out_shape=jax.ShapeD...]
    sub x9 -> x0, other arithmetic: 10.6 us -> none  [the longest x1 10.1 us: near_sum(): product[:half_rows, :, :cluster_size]]
    reshape x2 -> x0, local copies, waits for them, and re-layouts: 8.25 us -> none  [the longest x1 7.59 us: shards(): blocks = near_tiles.reshape(slots, cluster_size, 2 * cluster_size)]
    concatenate x2 -> x0, other arithmetic: 6.34 us -> none  [the longest x1 6.32 us: near_sum(): joined = jnp.concatenate([real_part, imag_part], axis=0)]
    all_gather x3 -> x0, blocking collectives: 5.97 us -> none  [shards(): lax.all_gather(updated.astype(jnp.bfloat16), 'tgt', axis=1, tiled=True)]
    psum x1 -> x0, blocking collectives: 4.51 us -> none  [shards(): coefficients = lax.psum(partial_value, 'tgt').astype(jnp.bfloat16)]
    gather x1 -> x0, local copies, waits for them, and re-layouts: 3.05 us -> none  [near_sum(): picked = jnp.take(sources, source_ids, axis=1)]
  transfers between devices with their start and end apart: 3 -> 7, of which waited for: 2 -> 3; matrix products, arithmetic and copies ran while one was open for 46% -> 11% of each run, Pallas kernels for 0% -> 25%
where the time goes in v1:
time: 44.4 us; the launch traced here: 44.1 us
  Pallas kernels  18 us (41%)
  starting transfers between devices  7.57 us (17%)
  waiting for transfers between devices  7.54 us (17%)
  local copies, waits for them, and re-layouts  6.69 us (15%)
  other arithmetic  2.34 us (5%)
  matrix products  1.14 us (3%)
  between operations  0.89 us (2%)
    pallas_call x3, Pallas kernels, near_call(): pl.pallas_call(functools.partial(near_kernel, call), out_shape=jax.ShapeD...  8.85 us
    ppermute x7, starting transfers between devices, swapped(): return lax.ppermute(value, axis, pairs)  7.57 us
    ppermute x7, waiting for transfers between devices, swapped(): return lax.ppermute(value, axis, pairs)  7.54 us
    pallas_call x2, Pallas kernels, expand_call(): pl.pallas_call(expand_kernel, out_shape=jax.ShapeDtypeStruct((rows, point...  4.6 us
    pallas_call x1, Pallas kernels, compress_call(): pl.pallas_call(functools.partial(compress_kernel, clusters), out_shape=(j...  4.51 us
    unnamed x17, local copies, waits for them, and re-layouts  3.95 us
    transpose x1, local copies, waits for them, and re-layouts, shards(): matrix = expand.transpose(1, 0, 2).reshape(2 * rank, points)  2.63 us
    select_n x1, other arithmetic, whole(): first = jnp.where(core == 0, matrix, other)  1.25 us
  transfers between devices with their start and end apart: 7, of which 3 were waited for; matrix products, arithmetic and copies ran while one was open for 11% of the time, Pallas kernels for 25%

profile of v1, /device:TPU:0, one launch (start us, length us, event | category | flops | bytes accessed | tf_op | source)
XLA Modules:
  0.0 44.1 jit_solution(488805385203532541)
XLA Ops:
  0.0 1.6 %copy-done.1 = bf16[2048,2,256]{2,1,0:T(2,128)(2,1)S(1)} copy-done((bf16[2048,2,256]{2,1,0:T(2,128)(2,1)S(1)}, bf16[2048,2,256]{2,1,0:T(2,128)(2,1)}, u32[]{:S(2)}) %copy-start.1) | copy-done | bytes 2097176
  1.6 1.2 %copy-done.2 = bf16[256,2048]{1,0:T(8,128)(2,1)S(1)} copy-done((bf16[256,2048]{1,0:T(8,128)(2,1)S(1)}, bf16[256,2048]{1,0:T(8,128)(2,1)}, u32[]{:S(2)}) %copy-start.2) | copy-done | bytes 1048600
  2.8 4.5 %compress.1 = (bf16[16,256,256]{2,1,0:T(8,128)(2,1)S(1)}, f32[128,256]{1,0:T(8,128)S(1)}, bf16[128,256]{1,0:T(8,128)(2,1)S(1)}) custom-call(s32[1]{0:T(128)} %bitcast.core_ref.half_ref, bf16[256,2048]{1,0:T(8,128)(2,1)S(1)} %copy-done.2, bf16[2048,2,256]{2,1,0:T(2,128)(2,1)S(1)} %copy-done.1), custom_call_target="tpu_custom_call" | custom-call | tf_op jit(solution)/shard_map/compress/pallas_call | solution.py:94
  7.3 0.6 %collective-permute-start = (bf16[128,256]{1,0:T(8,128)(2,1)S(1)}, bf16[128,256]{1,0:T(8,128)(2,1)}, u32[]{:S(2)}, u32[]{:S(2)}) collective-permute-start(bf16[128,256]{1,0:T(8,128)(2,1)S(1)} %get-tuple-element.9), channel_id=1, source_target_pairs={{0,1},{1,0},{2,3},{3,2},{4,5},{5,4},{6,7},{7,6},{8,9},{9,8},{10,11... | collective-permute-start | bytes 196616 | tf_op jit(solution)/shard_map/ppermute | solution.py:31
  8.0 0.1 collective-permute-start.1
  8.1 0.8 %copy.21 = bf16[3,256,2,128]{3,1,2,0:T(8,128)(2,1)} copy(bf16[3,256,2,128]{3,2,1,0:T(2,128)(2,1)S(1)} %copy-done.4) | data formatting | bytes 786432 | tf_op args[3]
  8.9 0.5 %collective-permute-start.3 = (bf16[3,256,2,128]{3,1,2,0:T(8,128)(2,1)}, bf16[3,256,2,128]{3,1,2,0:T(8,128)(2,1)}, u32[]{:S(2)}, u32[]{:S(2)}) collective-permute-start(bf16[3,256,2,128]{3,1,2,0:T(8,128)(2,1)} %copy.21), channel_id=1, source_target_pairs={{0,1},{1,0},{2,3},{3,2},{4,5},{5,4},{6,7},{7,6},{8,9},{9,8},{10,11... | collective-permute-start | bytes 1179656 | tf_op jit(solution)/shard_map/ppermute | solution.py:31
  9.3 0.1 copy.26.pairs_ref
  10.1 2.6 %copy.23 = bf16[2,256,2048]{2,1,0:T(8,128)(2,1)S(1)} copy(bf16[2,256,2048]{2,0,1:T(2,128)(2,1)} %bitcast.25) | data formatting | bytes 4194304 | tf_op jit(solution)/shard_map/transpose | solution.py:257
  12.7 0.2 copy-done
  12.9 3.0 %near0.1.refs_0_ = f32[17,256,128]{2,1,0:T(8,128)S(1)} custom-call(s32[64,2]{1,0:T(8,128)S(1)} %copy.26.pairs_ref, s32[1]{0:T(128)S(6)} %copy.34.count_ref, bf16[16,256,256]{2,1,0:T(8,128)(2,1)S(1)} %get-tuple-element.10.mixed_ref, bf16[64,256,128]{2,1,0:T(8,128)(2,1)S(1)} %bitcast.20), custom_call_target="tpu_custom_call" | custom-call | flops 357913952 | tf_op jit(solution)/shard_map/near0/pallas_call | solution.py:148
  16.0 0.9 %add_convert_fusion = bf16[128,256]{1,0:T(8,128)(2,1)S(1)} fusion(f32[128,256]{1,0:T(8,128)S(1)} %get-tuple-element.8, bf16[128,256]{1,0:T(8,128)(2,1)} %collective-permute-done), kind=kLoop, calls=%fused_computation.57 | loop fusion | flops 98304 | bytes 262144 | tf_op jit(solution)/shard_map/convert_element_type | solution.py:247
  16.8 2.3 %collective-permute-start.2 = (bf16[128,256]{1,0:T(8,128)(2,1)S(1)}, bf16[128,256]{1,0:T(8,128)(2,1)S(1)}, u32[]{:S(2)}, u32[]{:S(2)}) collective-permute-start(bf16[128,256]{1,0:T(8,128)(2,1)S(1)} %add_convert_fusion), channel_id=1, source_target_pairs={{0,2},{2,0},{4,6},{6,4},{8,10},{10,8},{12,14},{14,12},{1,3},{3,1},... | collective-permute-start | bytes 196616 | tf_op jit(solution)/shard_map/ppermute | solution.py:31
  19.1 2.4 %collective-permute-done.2 = bf16[128,256]{1,0:T(8,128)(2,1)S(1)} collective-permute-done((bf16[128,256]{1,0:T(8,128)(2,1)S(1)}, bf16[128,256]{1,0:T(8,128)(2,1)S(1)}, u32[]{:S(2)}, u32[]{:S(2)}) %collective-permute-start.2) | collective-permute-done | bytes 65568 | tf_op jit(solution)/shard_map/ppermute | solution.py:31
  21.6 1.3 %broadcast_select_fusion.1 = (bf16[3,256,2,128]{3,1,2,0:T(8,128)(2,1)S(1)}, bf16[3,256,2,128]{3,1,2,0:T(8,128)(2,1)S(1)}, bf16[3,256,2,128]{3,1,2,0:T(8,128)(2,1)S(1)}, bf16[3,256,2,128]{3,1,2,0:T(8,128)(2,1)S(1)}) fusion(bf16[3,256,2,128]{3,1,2,0:T(8,128)(2,1)} %collective-permute-done.3, pred[]{:T(512)S(6)} %eq.2, ...), kind=kLoop, calls=%fused_computation.9 | loop fusion | flops 786432 | bytes 3145729 | tf_op jit(solution)/shard_map/jit(_where)/select_n | solution.py:251
  22.8 0.1 maximum_bitcast_fusion
  23.0 0.1 maximum_bitcast_fusion.1
  23.2 0.2 fusion.3
  23.4 0.2 fusion
  23.6 1.6 %collective-permute-start.4 = (bf16[128,256]{1,0:T(8,128)(2,1)S(1)}, bf16[128,256]{1,0:T(8,128)(2,1)S(1)}, u32[]{:S(2)}, u32[]{:S(2)}) collective-permute-start(bf16[128,256]{1,0:T(8,128)(2,1)S(1)} %fusion), channel_id=1, source_target_pairs={{0,4},{2,6},{4,0},{6,2},{8,12},{10,14},{12,8},{14,10},{1,5},{3,7},... | collective-permute-start | bytes 196616 | tf_op jit(solution)/shard_map/ppermute | solution.py:31
  25.2 0.2 fusion.18
  25.4 2.5 %collective-permute-done.4 = bf16[128,256]{1,0:T(8,128)(2,1)S(1)} collective-permute-done((bf16[128,256]{1,0:T(8,128)(2,1)S(1)}, bf16[128,256]{1,0:T(8,128)(2,1)S(1)}, u32[]{:S(2)}, u32[]{:S(2)}) %collective-permute-start.4) | collective-permute-done | bytes 65568 | tf_op jit(solution)/shard_map/ppermute | solution.py:31
  27.9 0.2 fusion.1
  28.1 2.4 %collective-permute-start.5 = (bf16[128,256]{1,0:T(8,128)(2,1)S(1)}, bf16[128,256]{1,0:T(8,128)(2,1)S(1)}, u32[]{:S(2)}, u32[]{:S(2)}) collective-permute-start(bf16[128,256]{1,0:T(8,128)(2,1)S(1)} %fusion.1), channel_id=1, source_target_pairs={{0,8},{2,10},{4,12},{6,14},{8,0},{10,2},{12,4},{14,6},{1,9},{3,11}... | collective-permute-start | bytes 196616 | tf_op jit(solution)/shard_map/ppermute | solution.py:31
  30.6 0.2 fusion.33
  30.8 2.6 %collective-permute-done.5 = bf16[128,256]{1,0:T(8,128)(2,1)S(1)} collective-permute-done((bf16[128,256]{1,0:T(8,128)(2,1)S(1)}, bf16[128,256]{1,0:T(8,128)(2,1)S(1)}, u32[]{:S(2)}, u32[]{:S(2)}) %collective-permute-start.5) | collective-permute-done | bytes 65568 | tf_op jit(solution)/shard_map/ppermute | solution.py:31
  33.4 0.2 fusion.2.coeff_ref
  33.6 0.1 collective-permute-start.6
  33.7 2.9 %near1.1.refs_0_ = f32[17,256,128]{2,1,0:T(8,128)S(1)} custom-call(s32[64,2]{1,0:T(8,128)S(1)} %copy.26.pairs_ref, s32[1]{0:T(128)S(6)} %copy.34.count_ref, bf16[16,256,256]{2,1,0:T(8,128)(2,1)S(1)} %get-tuple-element.10.mixed_ref, bf16[64,256,128]{2,1,0:T(8,128)(2,1)S(1)} %bitcast.21, f32[17,256,128]{2,1,0:T(8,128)S(1)} %near0.1.refs_0_), custom_call_target="tpu_custom_call", output_to_operand_aliasing={{}: (4, {})} | custom-call | flops 357913952 | tf_op jit(solution)/shard_map/near1/pallas_call | solution.py:148
  36.6 2.9 %near2.1.near_ref = f32[17,256,128]{2,1,0:T(8,128)S(1)} custom-call(s32[64,2]{1,0:T(8,128)S(1)} %copy.26.pairs_ref, s32[1]{0:T(128)S(6)} %copy.34.count_ref, bf16[16,256,256]{2,1,0:T(8,128)(2,1)S(1)} %get-tuple-element.10.mixed_ref, bf16[64,256,128]{2,1,0:T(8,128)(2,1)S(1)} %bitcast.22, f32[17,256,128]{2,1,0:T(8,128)S(1)} %near1.1.refs_0_), custom_call_target="tpu_custom_call", output_to_operand_aliasing={{}: (4, {})} | custom-call | flops 357913952 | tf_op jit(solution)/shard_map/near2/pallas_call | solution.py:148
  39.5 2.3 %expand.2.refs_0_ = bf16[256,2048]{1,0:T(8,128)(2,1)} custom-call(s32[1]{0:T(128)} %bitcast.core_ref.half_ref, s32[1,16]{1,0:T(1,128)S(1)} %copy-done.3, bf16[128,256]{1,0:T(8,128)(2,1)S(1)} %fusion.2.coeff_ref, bf16[512,2048]{1,0:T(8,128)(2,1)S(1)} %bitcast.23, f32[17,256,128]{2,1,0:T(8,128)S(1)} %near2.1.near_ref), custom_call_target="tpu_custom_call" | custom-call | tf_op jit(solution)/shard_map/expand/pallas_call | solution.py:216
  41.8 2.3 %expand.3 = bf16[256,2048]{1,0:T(8,128)(2,1)} custom-call(s32[1]{0:T(128)S(6)} %sub.3.half_ref, s32[1,16]{1,0:T(1,128)S(1)} %copy-done.3, bf16[128,256]{1,0:T(8,128)(2,1)S(1)} %collective-permute-done.6.coeff_ref, bf16[512,2048]{1,0:T(8,128)(2,1)S(1)} %bitcast.24, f32[17,256,128]{2,1,0:T(8,128)S(1)} %near2.1.near_ref, ...), custom_call_target="tpu_custom_call", output_to_operand_aliasing={{}: (5, {})} | custom-call | tf_op jit(solution)/shard_map/expand/pallas_call | solution.py:216
  (24 shorter events, 0.2 us)
Async XLA Ops:
  0.0 1.6 %copy-start.1 = (bf16[2048,2,256]{2,1,0:T(2,128)(2,1)S(1)}, bf16[2048,2,256]{2,1,0:T(2,128)(2,1)}, u32[]{:S(2)}) copy-start(bf16[2048,2,256]{2,1,0:T(2,128)(2,1)} %comp_hbm.1) | copy-start | bytes 6291460
  1.6 1.2 %copy-start.2 = (bf16[256,2048]{1,0:T(8,128)(2,1)S(1)}, bf16[256,2048]{1,0:T(8,128)(2,1)}, u32[]{:S(2)}) copy-start(bf16[256,2048]{1,0:T(8,128)(2,1)} %dens_hbm.1) | copy-start | bytes 3145732
  2.8 5.1 %copy-start.5 = (bf16[3,256,2,128]{3,2,1,0:T(2,128)(2,1)S(1)}, bf16[3,256,2,128]{3,2,1,0:T(2,128)(2,1)}, u32[]{:S(2)}) copy-start(bf16[3,256,2,128]{3,2,1,0:T(2,128)(2,1)} %param.11) | copy-start | bytes 1179652
  2.8 5.2 %copy-start.4 = (bf16[3,256,2,128]{3,2,1,0:T(2,128)(2,1)S(1)}, bf16[3,256,2,128]{3,2,1,0:T(2,128)(2,1)}, u32[]{:S(2)}) copy-start(bf16[3,256,2,128]{3,2,1,0:T(2,128)(2,1)} %param.12) | copy-start | bytes 1179652
  2.8 6.5 %copy-start.6 = (s32[64,2]{0,1:T(2,128)S(1)}, s32[64,2]{0,1:T(2,128)}, u32[]{:S(2)}) copy-start(s32[64,2]{0,1:T(2,128)} %param.15) | copy-start | bytes 1540
  7.3 8.6 %collective-permute-start = (bf16[128,256]{1,0:T(8,128)(2,1)S(1)}, bf16[128,256]{1,0:T(8,128)(2,1)}, u32[]{:S(2)}, u32[]{:S(2)}) collective-permute-start(bf16[128,256]{1,0:T(8,128)(2,1)S(1)} %get-tuple-element.9), channel_id=1, source_target_pairs={{0,1},{1,0},{2,3},{3,2},{4,5},{5,4},{6,7},{7,6},{8,9},{9,8},{10,11... | collective-permute-start | bytes 196616 | tf_op jit(solution)/shard_map/ppermute | solution.py:31
  8.0 13.6 %collective-permute-start.1 = (bf16[3,256,2,128]{3,1,2,0:T(8,128)(2,1)S(1)}, bf16[3,256,2,128]{3,1,2,0:T(8,128)(2,1)}, u32[]{:S(2)}, u32[]{:S(2)}) collective-permute-start(bf16[3,256,2,128]{3,1,2,0:T(8,128)(2,1)S(1)} %copy.18), channel_id=1, source_target_pairs={{0,1},{1,0},{2,3},{3,2},{4,5},{5,4},{6,7},{7,6},{8,9},{9,8},{10,11... | collective-permute-start | bytes 1179656 | tf_op jit(solution)/shard_map/ppermute | solution.py:31
  8.9 12.7 %collective-permute-start.3 = (bf16[3,256,2,128]{3,1,2,0:T(8,128)(2,1)}, bf16[3,256,2,128]{3,1,2,0:T(8,128)(2,1)}, u32[]{:S(2)}, u32[]{:S(2)}) collective-permute-start(bf16[3,256,2,128]{3,1,2,0:T(8,128)(2,1)} %copy.21), channel_id=1, source_target_pairs={{0,1},{1,0},{2,3},{3,2},{4,5},{5,4},{6,7},{7,6},{8,9},{9,8},{10,11... | collective-permute-start | bytes 1179656 | tf_op jit(solution)/shard_map/ppermute | solution.py:31
  10.1 2.8 %copy-start = (bf16[64,128,2,128]{3,2,1,0:T(2,128)(2,1)S(1)}, bf16[64,128,2,128]{3,2,1,0:T(2,128)(2,1)}, u32[]{:S(2)}) copy-start(bf16[64,128,2,128]{3,2,1,0:T(2,128)(2,1)} %param.14) | copy-start | bytes 12582916
  16.8 4.7 %collective-permute-start.2 = (bf16[128,256]{1,0:T(8,128)(2,1)S(1)}, bf16[128,256]{1,0:T(8,128)(2,1)S(1)}, u32[]{:S(2)}, u32[]{:S(2)}) collective-permute-start(bf16[128,256]{1,0:T(8,128)(2,1)S(1)} %add_convert_fusion), channel_id=1, source_target_pairs={{0,2},{2,0},{4,6},{6,4},{8,10},{10,8},{12,14},{14,12},{1,3},{3,1},... | collective-permute-start | bytes 196616 | tf_op jit(solution)/shard_map/ppermute | solution.py:31
  23.6 4.3 %collective-permute-start.4 = (bf16[128,256]{1,0:T(8,128)(2,1)S(1)}, bf16[128,256]{1,0:T(8,128)(2,1)S(1)}, u32[]{:S(2)}, u32[]{:S(2)}) collective-permute-start(bf16[128,256]{1,0:T(8,128)(2,1)S(1)} %fusion), channel_id=1, source_target_pairs={{0,4},{2,6},{4,0},{6,2},{8,12},{10,14},{12,8},{14,10},{1,5},{3,7},... | collective-permute-start | bytes 196616 | tf_op jit(solution)/shard_map/ppermute | solution.py:31
  28.1 5.2 %collective-permute-start.5 = (bf16[128,256]{1,0:T(8,128)(2,1)S(1)}, bf16[128,256]{1,0:T(8,128)(2,1)S(1)}, u32[]{:S(2)}, u32[]{:S(2)}) collective-permute-start(bf16[128,256]{1,0:T(8,128)(2,1)S(1)} %fusion.1), channel_id=1, source_target_pairs={{0,8},{2,10},{4,12},{6,14},{8,0},{10,2},{12,4},{14,6},{1,9},{3,11}... | collective-permute-start | bytes 196616 | tf_op jit(solution)/shard_map/ppermute | solution.py:31
  33.6 8.2 %collective-permute-start.6 = (bf16[128,256]{1,0:T(8,128)(2,1)S(1)}, bf16[128,256]{1,0:T(8,128)(2,1)S(1)}, u32[]{:S(2)}, u32[]{:S(2)}) collective-permute-start(bf16[128,256]{1,0:T(8,128)(2,1)S(1)} %fusion.2.coeff_ref), channel_id=1, source_target_pairs={{0,1},{1,0},{2,3},{3,2},{4,5},{5,4},{6,7},{7,6},{8,9},{9,8},{10,11... | collective-permute-start | bytes 196616 | tf_op jit(solution)/shard_map/ppermute | solution.py:31
  36.6 2.9 %copy-start.3 = (s32[1,16]{1,0:T(1,128)S(1)}, s32[1,16]{1,0:T(1,128)}, u32[]{:S(2)}) copy-start(s32[1,16]{1,0:T(1,128)} %order_ref.3) | copy-start | bytes 196

commit v2 on v1

--- a/solution.py
+++ b/solution.py
@@ -7,10 +7,11 @@
 from jax.experimental.pallas import tpu as pltpu
 from jax.sharding import PartitionSpec as P
 
+
 VMEM = pltpu.VMEM
 CHUNKS = 4
 NEAR_CALLS = 3
-UNROLL = 4
+UNROLL = 8
 
 
 def in_vmem():
@@ -39,77 +40,40 @@
     )
 
 
-def compress_kernel(clusters, core_ref, dens_hbm, comp_hbm, mixed_ref, keep_ref, send_ref, dens, comp, weave, total, sems):
-    rows, points = dens.shape
-    width = points // clusters
-    rank = comp.shape[1]
-    comp_flat = comp_hbm.reshape(2 * points, rank)
-    step = points // CHUNKS
-    copies = []
-    for chunk in range(CHUNKS):
-        columns = pl.ds(chunk * step, step)
-        planes = pl.ds(2 * chunk * step, 2 * step)
-        pair = (
-            pltpu.make_async_copy(dens_hbm.at[:, columns], dens.at[:, columns], sems.at[chunk, 0]),
-            pltpu.make_async_copy(comp_flat.at[planes, :], comp.at[planes, :], sems.at[chunk, 1]),
-        )
-        for copy in pair:
-            copy.start()
-        copies.append(pair)
+def weave_kernel(dens_ref, mixed_ref, weave):
+    clusters = mixed_ref.shape[0]
+    width = dens_ref.shape[1] // clusters
     row_id = lax.broadcasted_iota(jnp.int32, (2 * width, 2 * width), 0)
     col_id = lax.broadcasted_iota(jnp.int32, (2 * width, 2 * width), 1)
     goal = jnp.where(row_id < width, 2 * row_id, 2 * (row_id - width) + 1)
     weave[...] = jnp.where(col_id == goal, 1.0, 0.0).astype(jnp.bfloat16)
-    for chunk in range(CHUNKS):
-        copies[chunk][0].wait()
-        pieces = []
-        for cluster in range(chunk * clusters // CHUNKS, (chunk + 1) * clusters // CHUNKS):
-            block = paired(dens[:, cluster * width : (cluster + 1) * width])
-            woven = jnp.dot(block, weave[...], preferred_element_type=jnp.float32).astype(jnp.bfloat16)
-            mixed_ref[cluster] = woven
-            pieces.append(woven)
-        copies[chunk][1].wait()
-        product = jnp.dot(
-            jnp.concatenate(pieces, axis=1),
-            comp[2 * chunk * step : 2 * (chunk + 1) * step, :],
-            preferred_element_type=jnp.float32,
-        )
-        if chunk == 0:
-            total[...] = product
-        else:
-            total[...] += product
-    quarter = rows // 4
-    core = core_ref[0]
-    for part in range(2):
-        mine = pl.ds(pl.multiple_of(2 * part * quarter + core * quarter, quarter), quarter)
-        other = pl.ds(pl.multiple_of(2 * part * quarter + (1 - core) * quarter, quarter), quarter)
-        keep_ref[part * quarter : (part + 1) * quarter, :] = total[mine, :]
-        send_ref[part * quarter : (part + 1) * quarter, :] = total[other, :].astype(jnp.bfloat16)
-
-
-def compress_call(core, densities, compress, clusters):
+
+    def body(trip, carry):
+        for lane in range(2):
+            cluster = 2 * trip + lane
+            block = paired(dens_ref[:, pl.ds(pl.multiple_of(cluster * width, width), width)])
+            woven = jnp.dot(block, weave[...], preferred_element_type=jnp.float32)
+            mixed_ref[cluster] = woven.astype(jnp.bfloat16)
+        return carry
+
+    lax.fori_loop(0, clusters // 2, body, 0)
+
+
+def weave_call(densities, clusters):
     rows, points = densities.shape
-    rank = compress.shape[2]
     width = points // clusters
     return pl.pallas_call(
-        functools.partial(compress_kernel, clusters),
-        out_shape=(
-            jax.ShapeDtypeStruct((clusters, rows, 2 * width), jnp.bfloat16),
-            jax.ShapeDtypeStruct((rows // 2, rank), jnp.float32),
-            jax.ShapeDtypeStruct((rows // 2, rank), jnp.bfloat16),
+        weave_kernel,
+        out_shape=jax.ShapeDtypeStruct((clusters, rows, 2 * width), jnp.bfloat16),
+        in_specs=[in_vmem()],
+        out_specs=in_vmem(),
+        scratch_shapes=[VMEM((2 * width, 2 * width), jnp.bfloat16)],
+        cost_estimate=pl.CostEstimate(
+            flops=4 * rows * points * width, bytes_accessed=0, transcendentals=0
         ),
-        in_specs=[in_smem(), in_hbm(), in_hbm()],
-        out_specs=(in_vmem(), in_vmem(), in_vmem()),
-        scratch_shapes=[
-            VMEM((rows, points), jnp.bfloat16),
-            VMEM((2 * points, rank), jnp.bfloat16),
-            VMEM((2 * width, 2 * width), jnp.bfloat16),
-            VMEM((rows, rank), jnp.float32),
-            pltpu.SemaphoreType.DMA((CHUNKS, 2)),
-        ],
         compiler_params=pltpu.CompilerParams(vmem_limit_bytes=16 << 20),
-        name="compress",
-    )(core, densities, compress)
+        name="weave",
+    )(densities)
 
 
 def near_kernel(call, pairs_ref, count_ref, mixed_ref, tiles_ref, *refs):
@@ -119,20 +83,18 @@
     clusters = total.shape[0] - 1
     slots = tiles_ref.shape[0]
     count = count_ref[0]
-    first = (count * call) // NEAR_CALLS
-    last = (count * (call + 1)) // NEAR_CALLS
+    trips = (count + UNROLL - 1) // UNROLL
 
     def body(trip, carry):
-        base = first + trip * UNROLL
         for lane in range(UNROLL):
-            slot = jnp.minimum(base + lane, slots - 1)
-            target = jnp.where(base + lane < last, pairs_ref[slot, 0], clusters)
+            slot = jnp.minimum(trip * UNROLL + lane, slots - 1)
+            target = jnp.where(trip * UNROLL + lane < count, pairs_ref[0, slot], clusters)
             total[target] += jnp.dot(
-                mixed_ref[pairs_ref[slot, 1]], tiles_ref[slot], preferred_element_type=jnp.float32
+                mixed_ref[pairs_ref[1, slot]], tiles_ref[slot], preferred_element_type=jnp.float32
             )
         return carry
 
-    lax.fori_loop(0, (last - first + UNROLL - 1) // UNROLL, body, 0)
+    lax.fori_loop((trips * call) // NEAR_CALLS, (trips * (call + 1)) // NEAR_CALLS, body, 0)
 
 
 def near_call(call, pairs, count, mixed, tiles, total):
@@ -155,7 +117,6 @@
             flops=2 * rows * depth * width * tiles.shape[0] // NEAR_CALLS, bytes_accessed=0, transcendentals=0
         ),
         compiler_params=pltpu.CompilerParams(vmem_limit_bytes=16 << 20),
-        name=f"near{call}",
     )(*operands)
 
 
@@ -241,29 +202,42 @@
     core = lax.axis_index("tgt").astype(jnp.int32)
     mine = core.reshape(1)
     tiles = near_tiles.reshape(slots, 2 * width, width)
-
-    mixed, keep, send = compress_call(mine, densities, compress, clusters)
-    arrived = swapped(send, "tgt", 0)
+    pairs = tile_pairs.T
+    half_rows = rows // 2
+
+    product = jnp.dot(
+        densities, compress.reshape(points, 2 * rank), preferred_element_type=jnp.float32
+    )
+    upper, lower = product[:half_rows], product[half_rows:]
+    quarter = half_rows // 2
+    first_core = core == 0
+    keep, send = [], []
+    for value in (upper[:, :rank] - lower[:, rank:], upper[:, rank:] + lower[:, :rank]):
+        keep.append(jnp.where(first_core, value[:quarter], value[quarter:]))
+        send.append(jnp.where(first_core, value[quarter:], value[:quarter]))
+    keep = jnp.concatenate(keep, axis=0)
+    arrived = swapped(jnp.concatenate(send, axis=0).astype(jnp.bfloat16), "tgt", 0)
+    mixed = weave_call(densities, clusters)
     coefficients = (keep + arrived.astype(jnp.float32)).astype(jnp.bfloat16)
 
-    def whole(matrix):
-        other = swapped(matrix, "tgt", 0)
-        first = jnp.where(core == 0, matrix, other)
-        second = jnp.where(core == 0, other, matrix)
-        joined = jnp.concatenate([first, second], axis=3)
-        return joined.transpose(0, 2, 1, 3).reshape(sections, 2 * rank, rank)
-
-    own_matrices, partner_matrices = whole(level_a), whole(level_b)
+    def both(matrix):
+        planes = matrix.transpose(0, 2, 1, 3)
+        joined = jnp.concatenate([planes, swapped(planes, "tgt", 0)], axis=3)
+        return joined.reshape(sections, 2 * rank, rank)
+
+    own_matrices, partner_matrices = both(level_a), both(level_b)
     matrix = expand.transpose(1, 0, 2).reshape(2 * rank, points)
     near = None
     for section in range(sections):
         partner = swapped(coefficients, "src", section)
         if section < NEAR_CALLS:
-            near = near_call(section, tile_pairs, tile_count, mixed, tiles, near)
+            near = near_call(section, pairs, tile_count, mixed, tiles, near)
         updated = jnp.dot(
             paired(coefficients), own_matrices[section], preferred_element_type=jnp.float32
         ) + jnp.dot(paired(partner), partner_matrices[section], preferred_element_type=jnp.float32)
-        coefficients = updated.astype(jnp.bfloat16)
+        updated = updated.astype(jnp.bfloat16)
+        turned = jnp.concatenate([updated[:, rank // 2 :], updated[:, : rank // 2]], axis=1)
+        coefficients = jnp.where(first_core, updated, turned)
     others = swapped(coefficients, "tgt", 0)
     result = expand_call(mine, cluster_order, coefficients, matrix, near, None)
     return expand_call(1 - mine, cluster_order, others, matrix, near, result)

time: 44.4 us -> 36.1 us (0.81)
  the two profiles are of different devices: /device:TPU:0 before, /device:TPU:25 now
where the time goes in v2:
time: 36.1 us; the launch traced here: 35.9 us
  Pallas kernels  11.4 us (32%)
  waiting for transfers between devices  9.78 us (27%)
  starting transfers between devices  6.36 us (18%)
  local copies, waits for them, and re-layouts  5.16 us (14%)
  matrix products  1.85 us (5%)
  between operations  1 us (3%)
  other arithmetic  0.39 us (1%)
    ppermute x7, waiting for transfers between devices, swapped(): return lax.ppermute(value, axis, pairs)  9.78 us
    ppermute x7, starting transfers between devices, swapped(): return lax.ppermute(value, axis, pairs)  6.36 us
    pallas_call x3, Pallas kernels, near_call(): pl.pallas_call(functools.partial(near_kernel, call), out_shape=jax.ShapeD...  4.88 us
    pallas_call x2, Pallas kernels, expand_call(): pl.pallas_call(expand_kernel, out_shape=jax.ShapeDtypeStruct((rows, point...  4.59 us
    unnamed x13, local copies, waits for them, and re-layouts  4.25 us
    pallas_call x1, Pallas kernels, weave_call(): pl.pallas_call(weave_kernel, out_shape=jax.ShapeDtypeStruct((clusters, ro...  1.91 us
    transpose x1, local copies, waits for them, and re-layouts, shards(): matrix = expand.transpose(1, 0, 2).reshape(2 * rank, points)  0.89 us
  transfers between devices with their start and end apart: 7, of which 3 were waited for; matrix products, arithmetic and copies ran while one was open for 9% of the time, Pallas kernels for 25%

profile of v2, /device:TPU:25, one launch (start us, length us, event | category | flops | bytes accessed | tf_op | source)
XLA Modules:
  0.0 35.9 jit_solution(12446412936736393493)
XLA Ops:
  0.0 2.1 %copy.17 = bf16[256,8,2,256]{3,1,2,0:T(8,128)(2,1)S(1)} copy(bf16[256,8,2,256]{3,2,1,0:T(2,128)(2,1)} %bitcast.35) | data formatting | bytes 4194304
  2.1 0.7 %fusion.62 = f32[256,512]{1,0:T(8,128)S(1)} fusion(bf16[256,2048]{1,0:T(8,128)(2,1)S(1)} %copy-done.1, bf16[2048,512]{1,0:T(8,128)(2,1)S(1)} %bitcast.37), kind=kOutput, calls=%fused_computation.94 | convolution fusion | flops 536870912 | bytes 3670016 | tf_op jit(solution)/shard_map/dot_general | solution.py:208
  2.9 0.7 %collective-permute-start = (bf16[128,256]{1,0:T(8,128)(2,1)S(1)}, bf16[128,256]{1,0:T(8,128)(2,1)S(1)}, u32[]{:S(2)}, u32[]{:S(2)}) collective-permute-start(bf16[128,256]{1,0:T(8,128)(2,1)S(1)} %pad_maximum_fusion.2), channel_id=1, source_target_pairs={{0,1},{1,0},{2,3},{3,2},{4,5},{5,4},{6,7},{7,6},{8,9},{9,8},{10,11... | collective-permute-start | bytes 196616 | tf_op jit(solution)/shard_map/ppermute | solution.py:32
  3.7 1.0 %copy.20 = bf16[3,256,2,128]{3,1,2,0:T(8,128)(2,1)S(1)} copy(bf16[3,256,2,128]{3,2,1,0:T(2,128)(2,1)} %param.12) | data formatting | bytes 786432 | tf_op args[3]
  4.7 0.2 collective-permute-start.3
  4.9 1.0 %copy.21 = bf16[3,256,2,128]{3,1,2,0:T(8,128)(2,1)S(1)} copy(bf16[3,256,2,128]{3,2,1,0:T(2,128)(2,1)} %param.11) | data formatting | bytes 786432 | tf_op args[2]
  6.0 0.4 %collective-permute-start.1 = (bf16[3,2,256,128]{3,2,1,0:T(8,128)(2,1)S(1)}, bf16[3,2,256,128]{3,2,1,0:T(8,128)(2,1)S(1)}, u32[]{:S(2)}, u32[]{:S(2)}) collective-permute-start(bf16[3,2,256,128]{3,2,1,0:T(8,128)(2,1)S(1)} %bitcast.38), channel_id=1, source_target_pairs={{0,1},{1,0},{2,3},{3,2},{4,5},{5,4},{6,7},{7,6},{8,9},{9,8},{10,11... | collective-permute-start | bytes 1179656 | tf_op jit(solution)/shard_map/ppermute | solution.py:32
  7.1 0.0 copy-start
  7.1 0.9 %copy.16 = bf16[2,256,2048]{2,1,0:T(8,128)(2,1)S(1)} copy(bf16[2,256,2048]{2,0,1:T(2,128)(2,1)S(1)} %bitcast.36) | data formatting | bytes 4194304 | tf_op jit(solution)/shard_map/transpose | solution.py:229
  8.0 0.0 copy-start.2
  8.0 1.9 %weave.1.mixed_ref = bf16[16,256,256]{2,1,0:T(8,128)(2,1)S(1)} custom-call(bf16[256,2048]{1,0:T(8,128)(2,1)S(1)} %copy-done.1), custom_call_target="tpu_custom_call" | custom-call | flops 268435456 | tf_op jit(solution)/shard_map/weave/pallas_call | solution.py:65
  10.0 1.6 %shard_map.91.refs_0_ = f32[17,256,128]{2,1,0:T(8,128)S(1)} custom-call(s32[2,64]{1,0:T(2,128)S(1)} %bitcast.32, s32[1]{0:T(128)S(6)} %copy.25.count_ref, bf16[16,256,256]{2,1,0:T(8,128)(2,1)S(1)} %weave.1.mixed_ref, bf16[64,256,128]{2,1,0:T(8,128)(2,1)S(1)} %bitcast.27), custom_call_target="tpu_custom_call" | custom-call | flops 357913952 | tf_op jit(solution)/shard_map/pallas_call | solution.py:110
  11.6 1.3 %collective-permute-start.2 = (bf16[128,256]{1,0:T(8,128)(2,1)S(1)}, bf16[128,256]{1,0:T(8,128)(2,1)S(1)}, u32[]{:S(2)}, u32[]{:S(2)}) collective-permute-start(bf16[128,256]{1,0:T(8,128)(2,1)S(1)} %fusion.7), channel_id=1, source_target_pairs={{0,2},{2,0},{4,6},{6,4},{8,10},{10,8},{12,14},{14,12},{1,3},{3,1},... | collective-permute-start | bytes 196616 | tf_op jit(solution)/shard_map/ppermute | solution.py:32
  12.9 2.3 %collective-permute-done.2 = bf16[128,256]{1,0:T(8,128)(2,1)S(1)} collective-permute-done((bf16[128,256]{1,0:T(8,128)(2,1)S(1)}, bf16[128,256]{1,0:T(8,128)(2,1)S(1)}, u32[]{:S(2)}, u32[]{:S(2)}) %collective-permute-start.2) | collective-permute-done | bytes 65568 | tf_op jit(solution)/shard_map/ppermute | solution.py:32
  15.2 0.1 fusion.4
  15.3 0.2 fusion.15
  15.5 0.1 pad_maximum_fusion.1
  15.6 0.2 fusion
  15.8 0.2 collective-permute-start.4
  16.1 2.9 %collective-permute-done.4 = bf16[128,256]{1,0:T(8,128)(2,1)S(1)} collective-permute-done((bf16[128,256]{1,0:T(8,128)(2,1)S(1)}, bf16[128,256]{1,0:T(8,128)(2,1)S(1)}, u32[]{:S(2)}, u32[]{:S(2)}) %collective-permute-start.4) | collective-permute-done | bytes 65568 | tf_op jit(solution)/shard_map/ppermute | solution.py:32
  19.0 0.2 fusion.30
  19.2 0.2 fusion.1
  19.5 0.1 collective-permute-start.5
  19.6 4.6 %collective-permute-done.5 = bf16[128,256]{1,0:T(8,128)(2,1)S(1)} collective-permute-done((bf16[128,256]{1,0:T(8,128)(2,1)S(1)}, bf16[128,256]{1,0:T(8,128)(2,1)S(1)}, u32[]{:S(2)}, u32[]{:S(2)}) %collective-permute-start.5) | collective-permute-done | bytes 65568 | tf_op jit(solution)/shard_map/ppermute | solution.py:32
  24.1 0.2 fusion.45
  24.3 0.2 fusion.2
  24.6 3.4 %collective-permute-start.6 = (bf16[128,256]{1,0:T(8,128)(2,1)S(1)}, bf16[128,256]{1,0:T(8,128)(2,1)S(1)}, u32[]{:S(2)}, u32[]{:S(2)}) collective-permute-start(bf16[128,256]{1,0:T(8,128)(2,1)S(1)} %maximum_select_fusion.2.coeff_ref), channel_id=1, source_target_pairs={{0,1},{1,0},{2,3},{3,2},{4,5},{5,4},{6,7},{7,6},{8,9},{9,8},{10,11... | collective-permute-start | bytes 196616 | tf_op jit(solution)/shard_map/ppermute | solution.py:32
  27.9 1.4 %shard_map.92.refs_0_ = f32[17,256,128]{2,1,0:T(8,128)S(1)} custom-call(s32[2,64]{1,0:T(2,128)S(1)} %bitcast.33, s32[1]{0:T(128)S(6)} %copy.25.count_ref, bf16[16,256,256]{2,1,0:T(8,128)(2,1)S(1)} %weave.1.mixed_ref, bf16[64,256,128]{2,1,0:T(8,128)(2,1)S(1)} %bitcast.28, f32[17,256,128]{2,1,0:T(8,128)S(1)} %shard_map.91.refs_0_), custom_call_target="tpu_custom_call", output_to_operand_aliasing={{}: (4, {})} | custom-call | flops 357913952 | tf_op jit(solution)/shard_map/pallas_call | solution.py:110
  29.4 0.0 copy-start.3
  29.4 1.9 %shard_map.93.near_ref = f32[17,256,128]{2,1,0:T(8,128)S(1)} custom-call(s32[2,64]{1,0:T(2,128)S(1)} %bitcast.34, s32[1]{0:T(128)S(6)} %copy.25.count_ref, bf16[16,256,256]{2,1,0:T(8,128)(2,1)S(1)} %weave.1.mixed_ref, bf16[64,256,128]{2,1,0:T(8,128)(2,1)S(1)} %bitcast.29, f32[17,256,128]{2,1,0:T(8,128)S(1)} %shard_map.92.refs_0_), custom_call_target="tpu_custom_call", output_to_operand_aliasing={{}: (4, {})} | custom-call | flops 357913952 | tf_op jit(solution)/shard_map/pallas_call | solution.py:110
  31.3 2.3 %expand.2.refs_0_ = bf16[256,2048]{1,0:T(8,128)(2,1)} custom-call(s32[1]{0:T(128)} %bitcast.half_ref, s32[1,16]{1,0:T(1,128)S(1)} %copy-done.3, bf16[128,256]{1,0:T(8,128)(2,1)S(1)} %maximum_select_fusion.2.coeff_ref, bf16[512,2048]{1,0:T(8,128)(2,1)S(1)} %bitcast.30, f32[17,256,128]{2,1,0:T(8,128)S(1)} %shard_map.93.near_ref), custom_call_target="tpu_custom_call" | custom-call | tf_op jit(solution)/shard_map/expand/pallas_call | solution.py:177
  33.6 2.3 %expand.3 = bf16[256,2048]{1,0:T(8,128)(2,1)} custom-call(s32[1]{0:T(128)S(6)} %sub.6.half_ref, s32[1,16]{1,0:T(1,128)S(1)} %copy-done.3, bf16[128,256]{1,0:T(8,128)(2,1)S(1)} %collective-permute-done.6.coeff_ref, bf16[512,2048]{1,0:T(8,128)(2,1)S(1)} %bitcast.31, f32[17,256,128]{2,1,0:T(8,128)S(1)} %shard_map.93.near_ref, ...), custom_call_target="tpu_custom_call", output_to_operand_aliasing={{}: (5, {})} | custom-call | tf_op jit(solution)/shard_map/expand/pallas_call | solution.py:177
  (28 shorter events, 0.2 us)
Async XLA Ops:
  0.0 2.1 %copy-start.1 = (bf16[256,2048]{1,0:T(8,128)(2,1)S(1)}, bf16[256,2048]{1,0:T(8,128)(2,1)}, u32[]{:S(2)}) copy-start(bf16[256,2048]{1,0:T(8,128)(2,1)} %dens_ref.1) | copy-start | bytes 3145732
  2.8 4.3 %copy-start.4 = (bf16[256,2,2048]{2,1,0:T(2,128)(2,1)S(1)}, bf16[256,2,2048]{2,1,0:T(2,128)(2,1)}, u32[]{:S(2)}) copy-start(bf16[256,2,2048]{2,1,0:T(2,128)(2,1)} %param.13) | copy-start | bytes 6291460
  2.9 8.6 %collective-permute-start = (bf16[128,256]{1,0:T(8,128)(2,1)S(1)}, bf16[128,256]{1,0:T(8,128)(2,1)S(1)}, u32[]{:S(2)}, u32[]{:S(2)}) collective-permute-start(bf16[128,256]{1,0:T(8,128)(2,1)S(1)} %pad_maximum_fusion.2), channel_id=1, source_target_pairs={{0,1},{1,0},{2,3},{3,2},{4,5},{5,4},{6,7},{7,6},{8,9},{9,8},{10,11... | collective-permute-start | bytes 196616 | tf_op jit(solution)/shard_map/ppermute | solution.py:32
  4.7 10.4 %collective-permute-start.3 = (bf16[3,2,256,128]{3,2,1,0:T(8,128)(2,1)S(1)}, bf16[3,2,256,128]{3,2,1,0:T(8,128)(2,1)S(1)}, u32[]{:S(2)}, u32[]{:S(2)}) collective-permute-start(bf16[3,2,256,128]{3,2,1,0:T(8,128)(2,1)S(1)} %bitcast.40), channel_id=1, source_target_pairs={{0,1},{1,0},{2,3},{3,2},{4,5},{5,4},{6,7},{7,6},{8,9},{9,8},{10,11... | collective-permute-start | bytes 1179656 | tf_op jit(solution)/shard_map/ppermute | solution.py:32
  6.0 9.5 %collective-permute-start.1 = (bf16[3,2,256,128]{3,2,1,0:T(8,128)(2,1)S(1)}, bf16[3,2,256,128]{3,2,1,0:T(8,128)(2,1)S(1)}, u32[]{:S(2)}, u32[]{:S(2)}) collective-permute-start(bf16[3,2,256,128]{3,2,1,0:T(8,128)(2,1)S(1)} %bitcast.38), channel_id=1, source_target_pairs={{0,1},{1,0},{2,3},{3,2},{4,5},{5,4},{6,7},{7,6},{8,9},{9,8},{10,11... | collective-permute-start | bytes 1179656 | tf_op jit(solution)/shard_map/ppermute | solution.py:32
  7.1 2.8 %copy-start = (bf16[64,128,2,128]{3,2,1,0:T(2,128)(2,1)S(1)}, bf16[64,128,2,128]{3,2,1,0:T(2,128)(2,1)}, u32[]{:S(2)}) copy-start(bf16[64,128,2,128]{3,2,1,0:T(2,128)(2,1)} %param.14) | copy-start | bytes 12582916
  8.0 1.9 %copy-start.2 = (s32[64,2]{0,1:T(2,128)S(1)}, s32[64,2]{0,1:T(2,128)}, u32[]{:S(2)}) copy-start(s32[64,2]{0,1:T(2,128)} %param.15) | copy-start | bytes 1540
  11.6 3.6 %collective-permute-start.2 = (bf16[128,256]{1,0:T(8,128)(2,1)S(1)}, bf16[128,256]{1,0:T(8,128)(2,1)S(1)}, u32[]{:S(2)}, u32[]{:S(2)}) collective-permute-start(bf16[128,256]{1,0:T(8,128)(2,1)S(1)} %fusion.7), channel_id=1, source_target_pairs={{0,2},{2,0},{4,6},{6,4},{8,10},{10,8},{12,14},{14,12},{1,3},{3,1},... | collective-permute-start | bytes 196616 | tf_op jit(solution)/shard_map/ppermute | solution.py:32
  15.8 3.2 %collective-permute-start.4 = (bf16[128,256]{1,0:T(8,128)(2,1)S(1)}, bf16[128,256]{1,0:T(8,128)(2,1)S(1)}, u32[]{:S(2)}, u32[]{:S(2)}) collective-permute-start(bf16[128,256]{1,0:T(8,128)(2,1)S(1)} %maximum_select_fusion), channel_id=1, source_target_pairs={{0,4},{2,6},{4,0},{6,2},{8,12},{10,14},{12,8},{14,10},{1,5},{3,7},... | collective-permute-start | bytes 196616 | tf_op jit(solution)/shard_map/ppermute | solution.py:32
  19.5 4.7 %collective-permute-start.5 = (bf16[128,256]{1,0:T(8,128)(2,1)S(1)}, bf16[128,256]{1,0:T(8,128)(2,1)S(1)}, u32[]{:S(2)}, u32[]{:S(2)}) collective-permute-start(bf16[128,256]{1,0:T(8,128)(2,1)S(1)} %maximum_select_fusion.1), channel_id=1, source_target_pairs={{0,8},{2,10},{4,12},{6,14},{8,0},{10,2},{12,4},{14,6},{1,9},{3,11}... | collective-permute-start | bytes 196616 | tf_op jit(solution)/shard_map/ppermute | solution.py:32
  24.6 9.0 %collective-permute-start.6 = (bf16[128,256]{1,0:T(8,128)(2,1)S(1)}, bf16[128,256]{1,0:T(8,128)(2,1)S(1)}, u32[]{:S(2)}, u32[]{:S(2)}) collective-permute-start(bf16[128,256]{1,0:T(8,128)(2,1)S(1)} %maximum_select_fusion.2.coeff_ref), channel_id=1, source_target_pairs={{0,1},{1,0},{2,3},{3,2},{4,5},{5,4},{6,7},{7,6},{8,9},{9,8},{10,11... | collective-permute-start | bytes 196616 | tf_op jit(solution)/shard_map/ppermute | solution.py:32
  29.4 1.9 %copy-start.3 = (s32[1,16]{1,0:T(1,128)S(1)}, s32[1,16]{1,0:T(1,128)}, u32[]{:S(2)}) copy-start(s32[1,16]{1,0:T(1,128)} %order_ref.3) | copy-start | bytes 196

commit v3 on v0

v3 whole, which is shorter than its diff:
```python
import jax
import jax.numpy as jnp
from jax import lax
from jax.experimental import pallas as pl
from jax.experimental.pallas import tpu as pltpu
from jax.sharding import PartitionSpec as P


NEAR_SHARES = (0, 2, 5, 8)
UNROLL = 8


def in_vmem():
    return pl.BlockSpec(memory_space=pltpu.VMEM)


def in_hbm():
    return pl.BlockSpec(memory_space=pltpu.HBM)


def anywhere():
    return pl.BlockSpec(memory_space=pl.ANY)


def swapped(value, axis, bit):
    mask = 2**bit
    pairs = [(source, source ^ mask) for source in range(lax.axis_size(axis))]
    return lax.ppermute(value, axis, pairs)


def paired(block):
    half = block.shape[0] // 2
    upper, lower = block[:half], block[half:]
    return jnp.concatenate(
        [jnp.concatenate([upper, -lower], axis=1), jnp.concatenate([lower, upper], axis=1)], axis=0
    )


def weave_into(mixed_ref, dens_ref, weave):
    clusters = mixed_ref.shape[0]
    width = dens_ref.shape[1] // clusters
    row_id = lax.broadcasted_iota(jnp.int32, (2 * width, 2 * width), 0)
    col_id = lax.broadcasted_iota(jnp.int32, (2 * width, 2 * width), 1)
    goal = jnp.where(row_id < width, 2 * row_id, 2 * (row_id - width) + 1)
    weave[...] = jnp.where(col_id == goal, 1.0, 0.0).astype(jnp.bfloat16)
    lanes = min(UNROLL, clusters)

    def body(trip, carry):
        for lane in range(lanes):
            cluster = lanes * trip + lane
            block = paired(dens_ref[:, pl.ds(pl.multiple_of(cluster * width, width), width)])
            woven = jnp.dot(block, weave[...], preferred_element_type=jnp.float32)
            mixed_ref[cluster] = woven.astype(jnp.bfloat16)
        return carry

    lax.fori_loop(0, clusters // lanes, body, 0)


def bounds(count, call):
    trips = (count + UNROLL - 1) // UNROLL
    return (trips * NEAR_SHARES[call]) // NEAR_SHARES[-1]


def tile_copy(tiles_hbm, tiles_ref, sems, trip):
    span = pl.ds(pl.multiple_of(trip * UNROLL, UNROLL), UNROLL)
    return pltpu.make_async_copy(tiles_hbm.at[span], tiles_ref.at[span], sems.at[trip])


def start_tiles(tiles_hbm, tiles_ref, sems, first, last):
    def body(trip, carry):
        tile_copy(tiles_hbm, tiles_ref, sems, trip).start()
        return carry

    lax.fori_loop(first, last, body, 0)


def wait_tiles(tiles_hbm, tiles_ref, sems, first, last):
    def body(trip, carry):
        tile_copy(tiles_hbm, tiles_ref, sems, trip).wait()
        return carry

    lax.fori_loop(first, last, body, 0)


def add_tiles(first, last, pairs_ref, count, mixed_ref, tiles_ref, total, ready):
    clusters = mixed_ref.shape[0]
    width = tiles_ref.shape[2]

    def body(trip, carry):
        ready(trip)
        for lane in range(UNROLL):
            slot = trip * UNROLL + lane
            target = jnp.where(slot < count, pairs_ref[0, slot], clusters)
            columns = pl.ds(pl.multiple_of(target * width, width), width)
            total[:, columns] += jnp.dot(
                mixed_ref[pairs_ref[1, slot]], tiles_ref[slot], preferred_element_type=jnp.float32
            )
        return carry

    lax.fori_loop(first, last, body, 0)


def fetch(sources, targets, sems):
    copies = []
    for item, (source, target) in enumerate(zip(sources, targets)):
        copies.append(pltpu.make_async_copy(source, target, sems.at[item]))
    for copy in copies:
        copy.start()
    for copy in copies:
        copy.wait()


def first_kernel(
    pairs_hbm,
    count_hbm,
    dens_ref,
    tiles_hbm,
    mixed_ref,
    tiles_ref,
    total,
    weave,
    pairs_ref,
    count_ref,
    table_sems,
    tile_sems,
):
    fetch((pairs_hbm, count_hbm), (pairs_ref, count_ref), table_sems)
    count = count_ref[0]
    middle, last = bounds(count, 1), bounds(count, 2)
    start_tiles(tiles_hbm, tiles_ref, tile_sems, 0, last)
    weave_into(mixed_ref, dens_ref, weave)
    total[...] = jnp.zeros_like(total)

    def ready(trip):
        tile_copy(tiles_hbm, tiles_ref, tile_sems, trip).wait()

    add_tiles(0, middle, pairs_ref, count, mixed_ref, tiles_ref, total, ready)
    wait_tiles(tiles_hbm, tiles_ref, tile_sems, middle, last)


def in_place(value):
    return pltpu.with_memory_space_constraint(value, pltpu.HBM)


def near_cost(rows, tiles):
    slots, depth, width = tiles.shape
    return pl.CostEstimate(
        flops=2 * rows * depth * width * slots // 2, bytes_accessed=0, transcendentals=0
    )


def first_call(pairs, count, densities, tiles, clusters):
    rows = densities.shape[0]
    slots, depth, width = tiles.shape
    return pl.pallas_call(
        first_kernel,
        out_shape=(
            jax.ShapeDtypeStruct((clusters, rows, depth), jnp.bfloat16),
            jax.ShapeDtypeStruct(tiles.shape, tiles.dtype),
            jax.ShapeDtypeStruct((rows, (clusters + 1) * width), jnp.float32),
        ),
        in_specs=[in_hbm(), anywhere(), in_vmem(), in_hbm()],
        out_specs=(in_vmem(), in_vmem(), in_vmem()),
        scratch_shapes=[
            pltpu.VMEM((depth, depth), jnp.bfloat16),
            pltpu.SMEM(pairs.shape, pairs.dtype),
            pltpu.SMEM(count.shape, count.dtype),
            pltpu.SemaphoreType.DMA((2,)),
            pltpu.SemaphoreType.DMA((slots // UNROLL,)),
        ],
        cost_estimate=near_cost(rows, tiles),
        compiler_params=pltpu.CompilerParams(vmem_limit_bytes=16 << 20),
        name="near0",
    )(in_place(pairs), count, densities, in_place(tiles))


def second_kernel(
    pairs_hbm,
    count_hbm,
    order_hbm,
    mixed_ref,
    tiles_hbm,
    expand_hbm,
    tiles_before,
    total_before,
    tiles_ref,
    total,
    placed_ref,
    pairs_ref,
    count_ref,
    order_ref,
    table_sems,
    tile_sems,
    place_sems,
):
    clusters = mixed_ref.shape[0]
    width = tiles_ref.shape[2]
    fetch((pairs_hbm, count_hbm, order_hbm), (pairs_ref, count_ref, order_ref), table_sems)
    count = count_ref[0]
    first, middle, last = bounds(count, 1), bounds(count, 2), bounds(count, 3)
    start_tiles(tiles_hbm, tiles_ref, tile_sems, middle, last)
    copies = []
    for cluster in range(clusters):
        place = pl.multiple_of(order_ref[0, cluster] * width, width)
        copies.append(
            pltpu.make_async_copy(
                expand_hbm.at[:, :, pl.ds(cluster * width, width)],
                placed_ref.at[:, :, pl.ds(place, width)],
                place_sems.at[cluster],
            )
        )
    for copy in copies:
        copy.start()
    add_tiles(first, middle, pairs_ref, count, mixed_ref, tiles_ref, total, lambda trip: None)
    for copy in copies:
        copy.wait()
    wait_tiles(tiles_hbm, tiles_ref, tile_sems, middle, last)


def second_call(pairs, count, order, mixed, tiles, expand, fetched, total):
    clusters = mixed.shape[0]
    slots = tiles.shape[0]
    return pl.pallas_call(
        second_kernel,
        out_shape=(
            jax.ShapeDtypeStruct(fetched.shape, fetched.dtype),
            jax.ShapeDtypeStruct(total.shape, total.dtype),
            jax.ShapeDtypeStruct(expand.shape, expand.dtype),
        ),
        in_specs=[
            in_hbm(),
            anywhere(),
            in_hbm(),
            in_vmem(),
            in_hbm(),
            in_hbm(),
            in_vmem(),
            in_vmem(),
        ],
        out_specs=(in_vmem(), in_vmem(), in_vmem()),
        input_output_aliases={6: 0, 7: 1},
        scratch_shapes=[
            pltpu.SMEM(pairs.shape, pairs.dtype),
            pltpu.SMEM(count.shape, count.dtype),
            pltpu.SMEM(order.shape, order.dtype),
            pltpu.SemaphoreType.DMA((3,)),
            pltpu.SemaphoreType.DMA((slots // UNROLL,)),
            pltpu.SemaphoreType.DMA((clusters,)),
        ],
        cost_estimate=near_cost(total.shape[0], tiles),
        compiler_params=pltpu.CompilerParams(vmem_limit_bytes=16 << 20),
        name="near1",
    )(
        in_place(pairs), count, in_place(order), mixed, in_place(tiles), in_place(expand), fetched, total
    )


def third_kernel(
    pairs_hbm, count_hbm, mixed_ref, tiles_ref, before, total, pairs_ref, count_ref, table_sems
):
    fetch((pairs_hbm, count_hbm), (pairs_ref, count_ref), table_sems)
    count = count_ref[0]
    first, last = bounds(count, 2), bounds(count, 3)
    add_tiles(first, last, pairs_ref, count, mixed_ref, tiles_ref, total, lambda trip: None)


def third_call(pairs, count, mixed, fetched, total):
    return pl.pallas_call(
        third_kernel,
        out_shape=jax.ShapeDtypeStruct(total.shape, total.dtype),
        in_specs=[in_hbm(), anywhere(), in_vmem(), in_vmem(), in_vmem()],
        out_specs=in_vmem(),
        input_output_aliases={4: 0},
        scratch_shapes=[
            pltpu.SMEM(pairs.shape, pairs.dtype),
            pltpu.SMEM(count.shape, count.dtype),
            pltpu.SemaphoreType.DMA((2,)),
        ],
        cost_estimate=near_cost(total.shape[0], fetched),
        compiler_params=pltpu.CompilerParams(vmem_limit_bytes=16 << 20),
        name="near2",
    )(in_place(pairs), count, mixed, fetched, total)


def shards(
    densities, compress, level_a, level_b, expand, near_tiles, tile_pairs, tile_count, cluster_order
):
    rows, points = densities.shape
    rank = compress.shape[2]
    sections = level_a.shape[0]
    clusters = cluster_order.shape[1]
    width = points // clusters
    slots = near_tiles.shape[0]
    core = lax.axis_index("tgt").astype(jnp.int32)
    tiles = near_tiles.reshape(slots, 2 * width, width)
    pairs = tile_pairs.T
    half_rows = rows // 2

    product = jnp.dot(
        densities, compress.reshape(points, 2 * rank), preferred_element_type=jnp.float32
    )
    upper, lower = product[:half_rows], product[half_rows:]
    quarter = half_rows // 2
    first_core = core == 0
    keep, send = [], []
    for value in (upper[:, :rank] - lower[:, rank:], upper[:, rank:] + lower[:, :rank]):
        keep.append(jnp.where(first_core, value[:quarter], value[quarter:]))
        send.append(jnp.where(first_core, value[quarter:], value[:quarter]))
    keep = jnp.concatenate(keep, axis=0)
    arrived = swapped(jnp.concatenate(send, axis=0).astype(jnp.bfloat16), "tgt", 0)
    count, arrived = lax.optimization_barrier((tile_count, arrived))
    coefficients = (keep + arrived.astype(jnp.float32)).astype(jnp.bfloat16)

    def both(matrix):
        planes = matrix.transpose(0, 2, 1, 3)
        other = swapped(planes, "tgt", 0)
        joined = jnp.concatenate([planes, other], axis=3)
        return joined.reshape(sections, 2 * rank, rank)

    own_matrices, partner_matrices = both(level_a), both(level_b)
    for section in range(sections):
        partner = swapped(coefficients, "src", section)
        if section == 0:
            mixed, fetched, near = first_call(pairs, count, densities, tiles, clusters)
        elif section == 1:
            fetched, near, placed = second_call(
                pairs, count, cluster_order, mixed, tiles, expand, fetched, near
            )
        elif section == 2:
            near = third_call(pairs, count, mixed, fetched, near)
        own = jnp.dot(
            paired(coefficients), own_matrices[section], preferred_element_type=jnp.float32
        )
        updated = own + jnp.dot(
            paired(partner), partner_matrices[section], preferred_element_type=jnp.float32
        )
        updated = updated.astype(jnp.bfloat16)
        turned = jnp.concatenate([updated[:, rank // 2 :], updated[:, : rank // 2]], axis=1)
        coefficients = jnp.where(first_core, updated, turned)
    others = swapped(coefficients, "tgt", 0)
    pieces = []
    for part in range(2):
        own = coefficients[part * quarter : (part + 1) * quarter]
        other = others[part * quarter : (part + 1) * quarter]
        pieces += [jnp.where(first_core, own, other), jnp.where(first_core, other, own)]
    matrix = placed.transpose(1, 0, 2).reshape(2 * rank, points)
    far = jnp.dot(
        paired(jnp.concatenate(pieces, axis=0)), matrix, preferred_element_type=jnp.float32
    )
    return (far + near[:, :points]).astype(jnp.bfloat16)


def solution(mesh):
    placed = (
        P("grp", ("src", "tgt")),
        P(("grp", "src", "tgt"), None, None),
        P("grp", "src", None, "tgt"),
        P("grp", "src", None, "tgt"),
        P(("grp", "src"), None, "tgt"),
        P(("grp", "src", "tgt"), None, None, None),
        P(("grp", "src", "tgt"), None),
        P(("grp", "src", "tgt")),
        P(("grp", "src", "tgt"), None),
    )
    return jax.shard_map(
        shards, mesh=mesh, in_specs=placed, out_specs=P("grp", ("src", "tgt")), check_vma=False
    )
```

time: 93.8 us -> 34.3 us (0.37)
  the two profiles are of different devices: /device:TPU:0 before, /device:TPU:25 now
where the time goes in v3:
time: 34.3 us; the launch traced here: 34.1 us
  waiting for transfers between devices  9.34 us (27%)
  Pallas kernels  7.65 us (22%)
  starting transfers between devices  7.04 us (21%)
  local copies, waits for them, and re-layouts  5.13 us (15%)
  matrix products  3.55 us (10%)
  between operations  0.92 us (3%)
  other arithmetic  0.43 us (1%)
    ppermute x7, waiting for transfers between devices, swapped(): return lax.ppermute(value, axis, pairs)  9.34 us
    ppermute x7, starting transfers between devices, swapped(): return lax.ppermute(value, axis, pairs)  7.04 us
    unnamed x5, local copies, waits for them, and re-layouts  4.23 us
    pallas_call x1, Pallas kernels, second_call(): pl.pallas_call(second_kernel, out_shape=(jax.ShapeDtypeStruct(fetched.sha...  3.19 us
    pallas_call x1, Pallas kernels, first_call(): pl.pallas_call(first_kernel, out_shape=(jax.ShapeDtypeStruct((clusters, r...  2.38 us
    pallas_call x1, Pallas kernels, third_call(): pl.pallas_call(third_kernel, out_shape=jax.ShapeDtypeStruct(total.shape,...  2.08 us
    dot_general x1, matrix products, shards(): jnp.dot(paired(jnp.concatenate(pieces, axis=0)), matrix, preferred_elemen...  1.7 us
    transpose x1, local copies, waits for them, and re-layouts, shards(): matrix = placed.transpose(1, 0, 2).reshape(2 * rank, points)  0.88 us
  transfers between devices with their start and end apart: 7, of which 3 were waited for; matrix products, arithmetic and copies ran while one was open for 15% of the time, Pallas kernels for 22%

profile of v3, /device:TPU:25, one launch (start us, length us, event | category | flops | bytes accessed | tf_op | source)
XLA Modules:
  0.0 34.1 jit_solution(7210187116733305923)
XLA Ops:
  0.0 1.0 %copy.19 = bf16[3,256,2,128]{3,1,2,0:T(8,128)(2,1)S(1)} copy(bf16[3,256,2,128]{3,2,1,0:T(2,128)(2,1)} %param.12) | data formatting | bytes 786432 | tf_op args[3]
  1.1 0.7 %collective-permute-start.3 = (bf16[3,2,256,128]{3,2,1,0:T(8,128)(2,1)S(1)}, bf16[3,2,256,128]{3,2,1,0:T(8,128)(2,1)S(1)}, u32[]{:S(2)}, u32[]{:S(2)}) collective-permute-start(bf16[3,2,256,128]{3,2,1,0:T(8,128)(2,1)S(1)} %bitcast.35), channel_id=1, source_target_pairs={{0,1},{1,0},{2,3},{3,2},{4,5},{5,4},{6,7},{7,6},{8,9},{9,8},{10,11... | collective-permute-start | bytes 1179656 | tf_op jit(solution)/shard_map/ppermute | solution.py:28
  1.8 1.0 %copy.20 = bf16[3,256,2,128]{3,1,2,0:T(8,128)(2,1)S(1)} copy(bf16[3,256,2,128]{3,2,1,0:T(2,128)(2,1)} %param.11) | data formatting | bytes 786432 | tf_op args[2]
  2.8 0.1 collective-permute-start.1
  2.9 0.0 copy-start
  2.9 2.1 %copy.16 = bf16[256,8,2,256]{3,1,2,0:T(8,128)(2,1)S(1)} copy(bf16[256,8,2,256]{3,2,1,0:T(2,128)(2,1)} %bitcast.31) | data formatting | bytes 4194304
  5.1 0.7 %fusion.80 = f32[256,512]{1,0:T(8,128)S(1)} fusion(bf16[256,2048]{1,0:T(8,128)(2,1)S(1)} %copy-done, bf16[2048,512]{1,0:T(8,128)(2,1)S(1)} %bitcast.32), kind=kOutput, calls=%fused_computation.116 | convolution fusion | flops 536870912 | bytes 3670016 | tf_op jit(solution)/shard_map/dot_general | solution.py:299
  5.9 0.5 %collective-permute-start = (bf16[128,256]{1,0:T(8,128)(2,1)S(1)}, bf16[128,256]{1,0:T(8,128)(2,1)S(1)}, u32[]{:S(2)}, u32[]{:S(2)}) collective-permute-start(bf16[128,256]{1,0:T(8,128)(2,1)S(1)} %pad_maximum_fusion.2), channel_id=1, source_target_pairs={{0,1},{1,0},{2,3},{3,2},{4,5},{5,4},{6,7},{7,6},{8,9},{9,8},{10,11... | collective-permute-start | bytes 196616 | tf_op jit(solution)/shard_map/ppermute | solution.py:28
  7.1 2.4 %near0.1 = (bf16[16,256,256]{2,1,0:T(8,128)(2,1)S(1)}, bf16[64,256,128]{2,1,0:T(8,128)(2,1)S(1)}, f32[256,2176]{1,0:T(8,128)S(1)}) custom-call(s32[2,64]{1,0:T(2,128)} %bitcast.43, s32[1]{0:T(128)S(6)} %copy.24.count_hbm, bf16[256,2048]{1,0:T(8,128)(2,1)S(1)} %copy-done, bf16[64,256,128]{2,1,0:T(8,128)(2,1)} %bitcast.28), custom_call_target="tpu_custom_call" | custom-call | flops 536870912 | tf_op jit(solution)/shard_map/near0/pallas_call | solution.py:155
  9.5 0.0 collective-permute-done
  9.5 1.3 %collective-permute-start.2 = (bf16[128,256]{1,0:T(8,128)(2,1)S(1)}, bf16[128,256]{1,0:T(8,128)(2,1)S(1)}, u32[]{:S(2)}, u32[]{:S(2)}) collective-permute-start(bf16[128,256]{1,0:T(8,128)(2,1)S(1)} %fusion.24), channel_id=1, source_target_pairs={{0,2},{2,0},{4,6},{6,4},{8,10},{10,8},{12,14},{14,12},{1,3},{3,1},... | collective-permute-start | bytes 196616 | tf_op jit(solution)/shard_map/ppermute | solution.py:28
  10.8 1.9 %collective-permute-done.2 = bf16[128,256]{1,0:T(8,128)(2,1)S(1)} collective-permute-done((bf16[128,256]{1,0:T(8,128)(2,1)S(1)}, bf16[128,256]{1,0:T(8,128)(2,1)S(1)}, u32[]{:S(2)}, u32[]{:S(2)}) %collective-permute-start.2) | collective-permute-done | bytes 65568 | tf_op jit(solution)/shard_map/ppermute | solution.py:28
  12.7 0.0 collective-permute-done.3
  12.7 0.1 fusion.5
  12.8 0.2 fusion.32
  13.0 0.0 collective-permute-done.1
  13.0 0.1 pad_maximum_fusion.1
  13.1 0.2 fusion.1
  13.4 0.2 collective-permute-start.4
  13.6 3.0 %collective-permute-done.4 = bf16[128,256]{1,0:T(8,128)(2,1)S(1)} collective-permute-done((bf16[128,256]{1,0:T(8,128)(2,1)S(1)}, bf16[128,256]{1,0:T(8,128)(2,1)S(1)}, u32[]{:S(2)}, u32[]{:S(2)}) %collective-permute-start.4) | collective-permute-done | bytes 65568 | tf_op jit(solution)/shard_map/ppermute | solution.py:28
  16.6 0.2 fusion.47
  16.8 0.2 fusion.2
  17.0 0.1 collective-permute-start.5
  17.1 4.5 %collective-permute-done.5 = bf16[128,256]{1,0:T(8,128)(2,1)S(1)} collective-permute-done((bf16[128,256]{1,0:T(8,128)(2,1)S(1)}, bf16[128,256]{1,0:T(8,128)(2,1)S(1)}, u32[]{:S(2)}, u32[]{:S(2)}) %collective-permute-start.5) | collective-permute-done | bytes 65568 | tf_op jit(solution)/shard_map/ppermute | solution.py:28
  21.7 0.2 fusion.62
  21.9 0.2 fusion.3
  22.1 4.0 %collective-permute-start.6 = (bf16[128,256]{1,0:T(8,128)(2,1)S(1)}, bf16[128,256]{1,0:T(8,128)(2,1)S(1)}, u32[]{:S(2)}, u32[]{:S(2)}) collective-permute-start(bf16[128,256]{1,0:T(8,128)(2,1)S(1)} %maximum_select_fusion.2), channel_id=1, source_target_pairs={{0,1},{1,0},{2,3},{3,2},{4,5},{5,4},{6,7},{7,6},{8,9},{9,8},{10,11... | collective-permute-start | bytes 196616 | tf_op jit(solution)/shard_map/ppermute | solution.py:28
  26.1 3.2 %near1.1 = (bf16[64,256,128]{2,1,0:T(8,128)(2,1)S(1)}, f32[256,2176]{1,0:T(8,128)S(1)}, bf16[256,2,2048]{2,1,0:T(2,128)(2,1)S(1)}) custom-call(s32[2,64]{1,0:T(2,128)} %bitcast.44, s32[1]{0:T(128)S(6)} %copy.24.count_hbm, s32[1,16]{1,0:T(1,128)} %order_hbm.1, ...), custom_call_target="tpu_custom_call", output_to_operand_aliasing={{0}: (6, {}), {1}: (7, {})} | custom-call | flops 536870912 | tf_op jit(solution)/shard_map/near1/pallas_call | solution.py:223
  29.3 0.9 %copy.15 = bf16[2,256,2048]{2,1,0:T(8,128)(2,1)S(1)} copy(bf16[2,256,2048]{2,0,1:T(2,128)(2,1)S(1)} %bitcast.27) | data formatting | bytes 4194304 | tf_op jit(solution)/shard_map/transpose | solution.py:346
  30.2 2.1 %near2.1 = f32[256,2176]{1,0:T(8,128)S(1)} custom-call(s32[2,64]{1,0:T(2,128)} %bitcast.45, s32[1]{0:T(128)S(6)} %copy.24.count_hbm, bf16[16,256,256]{2,1,0:T(8,128)(2,1)S(1)} %get-tuple-element.15.mixed_ref, bf16[64,256,128]{2,1,0:T(8,128)(2,1)S(1)} %get-tuple-element.19.tiles_ref, ...), custom_call_target="tpu_custom_call", output_to_operand_aliasing={{}: (4, {})} | custom-call | flops 536870912 | tf_op jit(solution)/shard_map/near2/pallas_call | solution.py:268
  32.3 0.0 collective-permute-done.6
  32.3 1.7 %fusion = bf16[256,2048]{1,0:T(8,128)(2,1)} fusion(f32[256,2176]{1,0:T(8,128)S(1)} %near2.1, bf16[512,2048]{1,0:T(8,128)(2,1)S(1)} %bitcast.30, bf16[64,256]{1,0:T(8,128)(2,1)S(1)} %get-tuple-element.31, bf16[64,256]{1,0:T(8,128)(2,1)S(1)} %get-tuple-element.30, bf16[64,256]{1,0:T(8,128)(2,1)S(1)} %get-tuple-element.32, ...), kind=kOutput, calls=%fused_computation.1 | convolution fusion | flops 539754496 | bytes 5439488 | tf_op jit(solution)/shard_map/dot_general | solution.py:347
  (20 shorter events, 0.3 us)
Async XLA Ops:
  1.1 11.6 %collective-permute-start.3 = (bf16[3,2,256,128]{3,2,1,0:T(8,128)(2,1)S(1)}, bf16[3,2,256,128]{3,2,1,0:T(8,128)(2,1)S(1)}, u32[]{:S(2)}, u32[]{:S(2)}) collective-permute-start(bf16[3,2,256,128]{3,2,1,0:T(8,128)(2,1)S(1)} %bitcast.35), channel_id=1, source_target_pairs={{0,1},{1,0},{2,3},{3,2},{4,5},{5,4},{6,7},{7,6},{8,9},{9,8},{10,11... | collective-permute-start | bytes 1179656 | tf_op jit(solution)/shard_map/ppermute | solution.py:28
  2.8 10.2 %collective-permute-start.1 = (bf16[3,2,256,128]{3,2,1,0:T(8,128)(2,1)S(1)}, bf16[3,2,256,128]{3,2,1,0:T(8,128)(2,1)S(1)}, u32[]{:S(2)}, u32[]{:S(2)}) collective-permute-start(bf16[3,2,256,128]{3,2,1,0:T(8,128)(2,1)S(1)} %bitcast.33), channel_id=1, source_target_pairs={{0,1},{1,0},{2,3},{3,2},{4,5},{5,4},{6,7},{7,6},{8,9},{9,8},{10,11... | collective-permute-start | bytes 1179656 | tf_op jit(solution)/shard_map/ppermute | solution.py:28
  2.9 2.1 %copy-start = (bf16[256,2048]{1,0:T(8,128)(2,1)S(1)}, bf16[256,2048]{1,0:T(8,128)(2,1)}, u32[]{:S(2)}) copy-start(bf16[256,2048]{1,0:T(8,128)(2,1)} %dens_ref.1) | copy-start | bytes 3145732
  5.9 3.6 %collective-permute-start = (bf16[128,256]{1,0:T(8,128)(2,1)S(1)}, bf16[128,256]{1,0:T(8,128)(2,1)S(1)}, u32[]{:S(2)}, u32[]{:S(2)}) collective-permute-start(bf16[128,256]{1,0:T(8,128)(2,1)S(1)} %pad_maximum_fusion.2), channel_id=1, source_target_pairs={{0,1},{1,0},{2,3},{3,2},{4,5},{5,4},{6,7},{7,6},{8,9},{9,8},{10,11... | collective-permute-start | bytes 196616 | tf_op jit(solution)/shard_map/ppermute | solution.py:28
  9.5 3.2 %collective-permute-start.2 = (bf16[128,256]{1,0:T(8,128)(2,1)S(1)}, bf16[128,256]{1,0:T(8,128)(2,1)S(1)}, u32[]{:S(2)}, u32[]{:S(2)}) collective-permute-start(bf16[128,256]{1,0:T(8,128)(2,1)S(1)} %fusion.24), channel_id=1, source_target_pairs={{0,2},{2,0},{4,6},{6,4},{8,10},{10,8},{12,14},{14,12},{1,3},{3,1},... | collective-permute-start | bytes 196616 | tf_op jit(solution)/shard_map/ppermute | solution.py:28
  13.4 3.2 %collective-permute-start.4 = (bf16[128,256]{1,0:T(8,128)(2,1)S(1)}, bf16[128,256]{1,0:T(8,128)(2,1)S(1)}, u32[]{:S(2)}, u32[]{:S(2)}) collective-permute-start(bf16[128,256]{1,0:T(8,128)(2,1)S(1)} %maximum_select_fusion), channel_id=1, source_target_pairs={{0,4},{2,6},{4,0},{6,2},{8,12},{10,14},{12,8},{14,10},{1,5},{3,7},... | collective-permute-start | bytes 196616 | tf_op jit(solution)/shard_map/ppermute | solution.py:28
  17.0 4.7 %collective-permute-start.5 = (bf16[128,256]{1,0:T(8,128)(2,1)S(1)}, bf16[128,256]{1,0:T(8,128)(2,1)S(1)}, u32[]{:S(2)}, u32[]{:S(2)}) collective-permute-start(bf16[128,256]{1,0:T(8,128)(2,1)S(1)} %maximum_select_fusion.1), channel_id=1, source_target_pairs={{0,8},{2,10},{4,12},{6,14},{8,0},{10,2},{12,4},{14,6},{1,9},{3,11}... | collective-permute-start | bytes 196616 | tf_op jit(solution)/shard_map/ppermute | solution.py:28
  22.1 10.2 %collective-permute-start.6 = (bf16[128,256]{1,0:T(8,128)(2,1)S(1)}, bf16[128,256]{1,0:T(8,128)(2,1)S(1)}, u32[]{:S(2)}, u32[]{:S(2)}) collective-permute-start(bf16[128,256]{1,0:T(8,128)(2,1)S(1)} %maximum_select_fusion.2), channel_id=1, source_target_pairs={{0,1},{1,0},{2,3},{3,2},{4,5},{5,4},{6,7},{7,6},{8,9},{9,8},{10,11... | collective-permute-start | bytes 196616 | tf_op jit(solution)/shard_map/ppermute | solution.py:28

commit v4 on v3

v4 whole, which is shorter than its diff:
```python
import functools

import jax
import jax.numpy as jnp
from jax import lax
from jax.experimental import pallas as pl
from jax.experimental.pallas import tpu as pltpu
from jax.sharding import PartitionSpec as P


NEAR_SHARES = (0, 1, 4, 8)
EXPAND_CHUNKS = 4
UNROLL = 8


def in_vmem():
    return pl.BlockSpec(memory_space=pltpu.VMEM)


def in_hbm():
    return pl.BlockSpec(memory_space=pltpu.HBM)


def anywhere():
    return pl.BlockSpec(memory_space=pl.ANY)


def swapped(value, axis, bit):
    mask = 2**bit
    pairs = [(source, source ^ mask) for source in range(lax.axis_size(axis))]
    return lax.ppermute(value, axis, pairs)


def paired(block):
    half = block.shape[0] // 2
    upper, lower = block[:half], block[half:]
    return jnp.concatenate(
        [jnp.concatenate([upper, -lower], axis=1), jnp.concatenate([lower, upper], axis=1)], axis=0
    )


def prepare_weave(weave):
    width = weave.shape[0] // 2
    row_id = lax.broadcasted_iota(jnp.int32, weave.shape, 0)
    col_id = lax.broadcasted_iota(jnp.int32, weave.shape, 1)
    goal = jnp.where(row_id < width, 2 * row_id, 2 * (row_id - width) + 1)
    weave[...] = jnp.where(col_id == goal, 1.0, 0.0).astype(jnp.bfloat16)


def weave_into(mixed_ref, dens_ref, weave, first, last):
    width = dens_ref.shape[1] // mixed_ref.shape[0]
    for cluster in range(first, last):
        block = paired(dens_ref[:, cluster * width : (cluster + 1) * width])
        woven = jnp.dot(block, weave[...], preferred_element_type=jnp.float32)
        mixed_ref[cluster] = woven.astype(jnp.bfloat16)


def bounds(count, call):
    trips = (count + UNROLL - 1) // UNROLL
    return (trips * NEAR_SHARES[call]) // NEAR_SHARES[-1]


def tile_copy(tiles_hbm, tiles_ref, sems, trip):
    span = pl.ds(pl.multiple_of(trip * UNROLL, UNROLL), UNROLL)
    return pltpu.make_async_copy(tiles_hbm.at[span], tiles_ref.at[span], sems.at[trip])


def start_tiles(tiles_hbm, tiles_ref, sems, first, last):
    def body(trip, carry):
        tile_copy(tiles_hbm, tiles_ref, sems, trip).start()
        return carry

    lax.fori_loop(first, last, body, 0)


def wait_tiles(tiles_hbm, tiles_ref, sems, first, last):
    def body(trip, carry):
        tile_copy(tiles_hbm, tiles_ref, sems, trip).wait()
        return carry

    lax.fori_loop(first, last, body, 0)


def invert(order_ref, inverse_ref):
    def body(cluster, carry):
        inverse_ref[order_ref[0, cluster]] = cluster
        return carry

    lax.fori_loop(0, order_ref.shape[1], body, 0)


def add_tiles(first, last, pairs_ref, inverse_ref, count, mixed_ref, tiles_ref, total, ready):
    clusters = mixed_ref.shape[0]
    width = tiles_ref.shape[2]

    def body(trip, carry):
        ready(trip)
        for lane in range(UNROLL):
            slot = trip * UNROLL + lane
            target = jnp.where(slot < count, inverse_ref[pairs_ref[0, slot]], clusters)
            columns = pl.ds(pl.multiple_of(target * width, width), width)
            total[:, columns] += jnp.dot(
                mixed_ref[pairs_ref[1, slot]], tiles_ref[slot], preferred_element_type=jnp.float32
            )
        return carry

    lax.fori_loop(first, last, body, 0)


def fetch(sources, targets, sems):
    copies = []
    for item, (source, target) in enumerate(zip(sources, targets)):
        copies.append(pltpu.make_async_copy(source, target, sems.at[item]))
    for copy in copies:
        copy.start()

    def finish():
        for copy in copies:
            copy.wait()

    return finish


def first_kernel(
    pairs_hbm,
    count_hbm,
    order_hbm,
    dens_ref,
    tiles_hbm,
    mixed_ref,
    tiles_ref,
    total,
    weave,
    pairs_ref,
    count_ref,
    order_ref,
    inverse_ref,
    table_sems,
    tile_sems,
):
    finish = fetch(
        (pairs_hbm, count_hbm, order_hbm), (pairs_ref, count_ref, order_ref), table_sems
    )
    clusters = mixed_ref.shape[0]
    prepare_weave(weave)
    weave_into(mixed_ref, dens_ref, weave, 0, clusters // 2)
    finish()
    count = count_ref[0]
    middle, last = bounds(count, 1), bounds(count, 2)
    start_tiles(tiles_hbm, tiles_ref, tile_sems, 0, last)
    invert(order_ref, inverse_ref)
    weave_into(mixed_ref, dens_ref, weave, clusters // 2, clusters)
    total[...] = jnp.zeros_like(total)

    def ready(trip):
        tile_copy(tiles_hbm, tiles_ref, tile_sems, trip).wait()

    add_tiles(0, middle, pairs_ref, inverse_ref, count, mixed_ref, tiles_ref, total, ready)
    wait_tiles(tiles_hbm, tiles_ref, tile_sems, middle, last)


def in_place(value):
    return pltpu.with_memory_space_constraint(value, pltpu.HBM)


def near_cost(rows, tiles):
    slots, depth, width = tiles.shape
    return pl.CostEstimate(
        flops=2 * rows * depth * width * slots // 2, bytes_accessed=0, transcendentals=0
    )


def tables(*arrays):
    return [pltpu.SMEM(array.shape, array.dtype) for array in arrays]


def first_call(pairs, count, order, densities, tiles):
    rows = densities.shape[0]
    clusters = order.shape[1]
    slots, depth, width = tiles.shape
    return pl.pallas_call(
        first_kernel,
        out_shape=(
            jax.ShapeDtypeStruct((clusters, rows, depth), jnp.bfloat16),
            jax.ShapeDtypeStruct(tiles.shape, tiles.dtype),
            jax.ShapeDtypeStruct((rows, (clusters + 1) * width), jnp.float32),
        ),
        in_specs=[in_hbm(), anywhere(), in_hbm(), in_vmem(), in_hbm()],
        out_specs=(in_vmem(), in_vmem(), in_vmem()),
        scratch_shapes=[
            pltpu.VMEM((depth, depth), jnp.bfloat16),
            *tables(pairs, count, order),
            pltpu.SMEM((clusters,), jnp.int32),
            pltpu.SemaphoreType.DMA((3,)),
            pltpu.SemaphoreType.DMA((slots // UNROLL,)),
        ],
        cost_estimate=near_cost(rows, tiles),
        compiler_params=pltpu.CompilerParams(vmem_limit_bytes=16 << 20),
        name="near0",
    )(in_place(pairs), count, in_place(order), densities, in_place(tiles))


def second_kernel(
    pairs_hbm,
    count_hbm,
    order_hbm,
    mixed_ref,
    tiles_hbm,
    tiles_before,
    total_before,
    tiles_ref,
    total,
    pairs_ref,
    count_ref,
    order_ref,
    inverse_ref,
    table_sems,
    tile_sems,
):
    fetch((pairs_hbm, count_hbm, order_hbm), (pairs_ref, count_ref, order_ref), table_sems)()
    count = count_ref[0]
    first, middle, last = bounds(count, 1), bounds(count, 2), bounds(count, 3)
    start_tiles(tiles_hbm, tiles_ref, tile_sems, middle, last)
    invert(order_ref, inverse_ref)
    add_tiles(
        first, middle, pairs_ref, inverse_ref, count, mixed_ref, tiles_ref, total, lambda trip: None
    )
    wait_tiles(tiles_hbm, tiles_ref, tile_sems, middle, last)


def second_call(pairs, count, order, mixed, tiles, fetched, total):
    clusters = mixed.shape[0]
    slots = tiles.shape[0]
    return pl.pallas_call(
        second_kernel,
        out_shape=(
            jax.ShapeDtypeStruct(fetched.shape, fetched.dtype),
            jax.ShapeDtypeStruct(total.shape, total.dtype),
        ),
        in_specs=[in_hbm(), anywhere(), in_hbm(), in_vmem(), in_hbm(), in_vmem(), in_vmem()],
        out_specs=(in_vmem(), in_vmem()),
        input_output_aliases={5: 0, 6: 1},
        scratch_shapes=[
            *tables(pairs, count, order),
            pltpu.SMEM((clusters,), jnp.int32),
            pltpu.SemaphoreType.DMA((3,)),
            pltpu.SemaphoreType.DMA((slots // UNROLL,)),
        ],
        cost_estimate=near_cost(total.shape[0], tiles),
        compiler_params=pltpu.CompilerParams(vmem_limit_bytes=16 << 20),
        name="near1",
    )(in_place(pairs), count, in_place(order), mixed, in_place(tiles), fetched, total)


def third_kernel(
    pairs_hbm,
    count_hbm,
    order_hbm,
    mixed_ref,
    tiles_ref,
    before,
    total,
    pairs_ref,
    count_ref,
    order_ref,
    inverse_ref,
    table_sems,
):
    fetch((pairs_hbm, count_hbm, order_hbm), (pairs_ref, count_ref, order_ref), table_sems)()
    count = count_ref[0]
    first, last = bounds(count, 2), bounds(count, 3)
    invert(order_ref, inverse_ref)
    add_tiles(
        first, last, pairs_ref, inverse_ref, count, mixed_ref, tiles_ref, total, lambda trip: None
    )


def third_call(pairs, count, order, mixed, fetched, total):
    clusters = mixed.shape[0]
    return pl.pallas_call(
        third_kernel,
        out_shape=jax.ShapeDtypeStruct(total.shape, total.dtype),
        in_specs=[in_hbm(), anywhere(), in_hbm(), in_vmem(), in_vmem(), in_vmem()],
        out_specs=in_vmem(),
        input_output_aliases={5: 0},
        scratch_shapes=[
            *tables(pairs, count, order),
            pltpu.SMEM((clusters,), jnp.int32),
            pltpu.SemaphoreType.DMA((3,)),
        ],
        cost_estimate=near_cost(total.shape[0], fetched),
        compiler_params=pltpu.CompilerParams(vmem_limit_bytes=16 << 20),
        name="near2",
    )(in_place(pairs), count, in_place(order), mixed, fetched, total)


def expand_kernel(axis, flip, order_hbm, coeff_ref, matrix_ref, near_ref, *refs):
    out_hbm, rows_out, order_ref, table_sem, sems = refs[-5:]
    rows = near_ref.shape[0]
    quarter = rows // 4
    points = matrix_ref.shape[1]
    clusters = order_ref.shape[1]
    width = points // clusters
    finish = fetch((order_hbm,), (order_ref,), table_sem)
    core = lax.axis_index(axis)
    half = 1 - core if flip else core
    left = paired(coeff_ref[...])
    span = points // EXPAND_CHUNKS
    copies = []
    for chunk in range(EXPAND_CHUNKS):
        columns = slice(chunk * span, (chunk + 1) * span)
        far = jnp.dot(left, matrix_ref[:, columns], preferred_element_type=jnp.float32)
        for part in range(2):
            source = pl.ds(pl.multiple_of((2 * part + half) * quarter, quarter), quarter)
            inner = slice(part * quarter, (part + 1) * quarter)
            rows_out[inner, columns] = (far[inner] + near_ref[source, columns]).astype(jnp.bfloat16)
        if chunk == 0:
            finish()
        for cluster in range(chunk * clusters // EXPAND_CHUNKS, (chunk + 1) * clusters // EXPAND_CHUNKS):
            place = pl.multiple_of(order_ref[0, cluster] * width, width)
            for part in range(2):
                target = pl.ds(pl.multiple_of((2 * part + half) * quarter, quarter), quarter)
                copy = pltpu.make_async_copy(
                    rows_out.at[part * quarter : (part + 1) * quarter, cluster * width : (cluster + 1) * width],
                    out_hbm.at[target, pl.ds(place, width)],
                    sems.at[2 * cluster + part],
                )
                copy.start()
                copies.append(copy)
    for copy in copies:
        copy.wait()


def expand_call(flip, order, coefficients, matrix, near, result):
    clusters = order.shape[1]
    rows = near.shape[0]
    points = matrix.shape[1]
    operands = [in_place(order), coefficients, matrix, near]
    specs = [in_hbm(), in_vmem(), in_vmem(), in_vmem()]
    aliases = {}
    if result is not None:
        operands.append(result)
        specs.append(in_hbm())
        aliases = {4: 0}
    return pl.pallas_call(
        functools.partial(expand_kernel, "tgt", flip),
        out_shape=jax.ShapeDtypeStruct((rows, points), jnp.bfloat16),
        in_specs=specs,
        out_specs=in_hbm(),
        input_output_aliases=aliases,
        scratch_shapes=[
            pltpu.VMEM((rows // 2, points), jnp.bfloat16),
            pltpu.SMEM(order.shape, order.dtype),
            pltpu.SemaphoreType.DMA((1,)),
            pltpu.SemaphoreType.DMA((2 * clusters,)),
        ],
        cost_estimate=pl.CostEstimate(
            flops=4 * rows * matrix.shape[0] * points // 4, bytes_accessed=0, transcendentals=0
        ),
        compiler_params=pltpu.CompilerParams(vmem_limit_bytes=16 << 20),
        name="expand1" if flip else "expand0",
    )(*operands)


def shards(
    densities, compress, level_a, level_b, expand, near_tiles, tile_pairs, tile_count, cluster_order
):
    rows, points = densities.shape
    rank = compress.shape[2]
    sections = level_a.shape[0]
    clusters = cluster_order.shape[1]
    width = points // clusters
    slots = near_tiles.shape[0]
    core = lax.axis_index("tgt").astype(jnp.int32)
    tiles = near_tiles.reshape(slots, 2 * width, width)
    pairs = tile_pairs.T
    half_rows = rows // 2

    product = jnp.dot(
        densities, compress.reshape(points, 2 * rank), preferred_element_type=jnp.float32
    )
    upper, lower = product[:half_rows], product[half_rows:]
    quarter = half_rows // 2
    first_core = core == 0
    keep, send = [], []
    for value in (upper[:, :rank] - lower[:, rank:], upper[:, rank:] + lower[:, :rank]):
        keep.append(jnp.where(first_core, value[:quarter], value[quarter:]))
        send.append(jnp.where(first_core, value[quarter:], value[:quarter]))
    keep = jnp.concatenate(keep, axis=0)
    arrived = swapped(jnp.concatenate(send, axis=0).astype(jnp.bfloat16), "tgt", 0)
    count = tile_count
    coefficients = (keep + arrived.astype(jnp.float32)).astype(jnp.bfloat16)

    def both(matrix):
        planes = matrix.transpose(0, 2, 1, 3)
        other = swapped(planes, "tgt", 0)
        joined = jnp.concatenate([planes, other], axis=3)
        return joined.reshape(sections, 2 * rank, rank)

    own_matrices, partner_matrices = both(level_a), both(level_b)
    for section in range(sections):
        partner = swapped(coefficients, "src", section)
        if section == 0:
            mixed, fetched, near = first_call(pairs, count, cluster_order, densities, tiles)
        elif section == 1:
            fetched, near = second_call(pairs, count, cluster_order, mixed, tiles, fetched, near)
        elif section == 2:
            near = third_call(pairs, count, cluster_order, mixed, fetched, near)
        own = jnp.dot(
            paired(coefficients), own_matrices[section], preferred_element_type=jnp.float32
        )
        own = lax.optimization_barrier(own)
        updated = own + jnp.dot(
            paired(partner), partner_matrices[section], preferred_element_type=jnp.float32
        )
        updated = updated.astype(jnp.bfloat16)
        turned = jnp.concatenate([updated[:, rank // 2 :], updated[:, : rank // 2]], axis=1)
        coefficients = jnp.where(first_core, updated, turned)
    others = swapped(coefficients, "tgt", 0)
    matrix = expand.transpose(1, 0, 2).reshape(2 * rank, points)
    result = expand_call(False, cluster_order, coefficients, matrix, near, None)
    return expand_call(True, cluster_order, others, matrix, near, result)


def solution(mesh):
    placed = (
        P("grp", ("src", "tgt")),
        P(("grp", "src", "tgt"), None, None),
        P("grp", "src", None, "tgt"),
        P("grp", "src", None, "tgt"),
        P(("grp", "src"), None, "tgt"),
        P(("grp", "src", "tgt"), None, None, None),
        P(("grp", "src", "tgt"), None),
        P(("grp", "src", "tgt")),
        P(("grp", "src", "tgt"), None),
    )
    return jax.shard_map(
        shards, mesh=mesh, in_specs=placed, out_specs=P("grp", ("src", "tgt")), check_vma=False
    )
```

time: 34.3 us -> 34 us (level)
  Pallas kernels: 7.65 us -> 11.6 us
  local copies, waits for them, and re-layouts: 5.13 us -> 3.16 us
  matrix products: 3.55 us -> 1.85 us
  waiting for transfers between devices: 9.34 us -> 8.99 us
    pallas_call x0 -> x2, Pallas kernels: none -> 3.97 us  [expand_call(): pl.pallas_call(functools.partial(expand_kernel, 'tgt', flip), out_shape=j...]
    unnamed x5 -> x11, local copies, waits for them, and re-layouts: 4.23 us -> 2.25 us
    dot_general x1 -> x0, matrix products: 1.7 us -> none  [shards(): jnp.dot(paired(jnp.concatenate(pieces, axis=0)), matrix, preferred_elemen...]
    pallas_call x1, Pallas kernels: 3.19 us -> 2.35 us  [second_call(): pl.pallas_call(second_kernel, out_shape=(jax.ShapeDtypeStruct(fetched.sha...]
    pallas_call x1, Pallas kernels: 2.08 us -> 2.65 us  [third_call(): pl.pallas_call(third_kernel, out_shape=jax.ShapeDtypeStruct(total.shape,...]
    ppermute x7, waiting for transfers between devices: 9.34 us -> 8.99 us  [swapped(): return lax.ppermute(value, axis, pairs)]
  transfers between devices with their start and end apart: 7 -> 7, of which waited for: 3 -> 3; matrix products, arithmetic and copies ran while one was open for 15% -> 5% of each run, Pallas kernels for 22% -> 29%
where the time goes in v4:
time: 34 us; the launch traced here: 33.8 us
  Pallas kernels  11.6 us (34%)
  waiting for transfers between devices  8.99 us (26%)
  starting transfers between devices  6.81 us (20%)
  local copies, waits for them, and re-layouts  3.16 us (9%)
  matrix products  1.85 us (5%)
  between operations  0.95 us (3%)
  other arithmetic  0.41 us (1%)
    ppermute x7, waiting for transfers between devices, swapped(): return lax.ppermute(value, axis, pairs)  8.99 us
    ppermute x7, starting transfers between devices, swapped(): return lax.ppermute(value, axis, pairs)  6.81 us
    pallas_call x2, Pallas kernels, expand_call(): pl.pallas_call(functools.partial(expand_kernel, 'tgt', flip), out_shape=j...  3.97 us
    pallas_call x1, Pallas kernels, first_call(): pl.pallas_call(first_kernel, out_shape=(jax.ShapeDtypeStruct((clusters, r...  2.65 us
    pallas_call x1, Pallas kernels, third_call(): pl.pallas_call(third_kernel, out_shape=jax.ShapeDtypeStruct(total.shape,...  2.65 us
    pallas_call x1, Pallas kernels, second_call(): pl.pallas_call(second_kernel, out_shape=(jax.ShapeDtypeStruct(fetched.sha...  2.35 us
    unnamed x11, local copies, waits for them, and re-layouts  2.25 us
    transpose x1, local copies, waits for them, and re-layouts, shards(): matrix = expand.transpose(1, 0, 2).reshape(2 * rank, points)  0.88 us
  transfers between devices with their start and end apart: 7, of which 3 were waited for; matrix products, arithmetic and copies ran while one was open for 5% of the time, Pallas kernels for 29%

profile of v4, /device:TPU:25, one launch (start us, length us, event | category | flops | bytes accessed | tf_op | source)
XLA Modules:
  0.0 33.8 jit_solution(15840822747168290407)
XLA Ops:
  0.0 2.1 %copy.18 = bf16[256,8,2,256]{3,1,2,0:T(8,128)(2,1)S(1)} copy(bf16[256,8,2,256]{3,2,1,0:T(2,128)(2,1)} %bitcast.30) | data formatting | bytes 4194304
  2.1 0.0 copy-start.2
  2.2 0.0 copy-start.3
  2.2 0.7 %fusion.62 = f32[256,512]{1,0:T(8,128)S(1)} fusion(bf16[256,2048]{1,0:T(8,128)(2,1)S(1)} %copy-done, bf16[2048,512]{1,0:T(8,128)(2,1)S(1)} %bitcast.32), kind=kOutput, calls=%fused_computation.94 | convolution fusion | flops 536870912 | bytes 3670016 | tf_op jit(solution)/shard_map/dot_general | solution.py:379
  3.0 0.7 %collective-permute-start = (bf16[128,256]{1,0:T(8,128)(2,1)S(1)}, bf16[128,256]{1,0:T(8,128)(2,1)S(1)}, u32[]{:S(2)}, u32[]{:S(2)}) collective-permute-start(bf16[128,256]{1,0:T(8,128)(2,1)S(1)} %pad_maximum_fusion.2), channel_id=1, source_target_pairs={{0,1},{1,0},{2,3},{3,2},{4,5},{5,4},{6,7},{7,6},{8,9},{9,8},{10,11... | collective-permute-start | bytes 196616 | tf_op jit(solution)/shard_map/ppermute | solution.py:31
  3.7 0.1 copy.22
  3.8 0.2 collective-permute-start.1
  3.9 0.1 copy.21
  4.0 0.5 %collective-permute-start.3 = (bf16[3,2,256,128]{3,2,1,0:T(8,128)(2,1)S(1)}, bf16[3,2,256,128]{3,2,1,0:T(8,128)(2,1)S(1)}, u32[]{:S(2)}, u32[]{:S(2)}) collective-permute-start(bf16[3,2,256,128]{3,2,1,0:T(8,128)(2,1)S(1)} %bitcast.33), channel_id=1, source_target_pairs={{0,1},{1,0},{2,3},{3,2},{4,5},{5,4},{6,7},{7,6},{8,9},{9,8},{10,11... | collective-permute-start | bytes 1179656 | tf_op jit(solution)/shard_map/ppermute | solution.py:31
  5.1 0.0 copy-start.1
  5.1 2.7 %near0.1 = (bf16[16,256,256]{2,1,0:T(8,128)(2,1)S(1)}, bf16[64,256,128]{2,1,0:T(8,128)(2,1)S(1)}, f32[256,2176]{1,0:T(8,128)S(1)}) custom-call(s32[2,64]{1,0:T(2,128)} %bitcast.43, s32[1]{0:T(128)S(6)} %copy.27.count_hbm, s32[1,16]{1,0:T(1,128)} %order_hbm.9, bf16[256,2048]{1,0:T(8,128)(2,1)S(1)} %copy-done, bf16[64,256,128]{2,1,0:T(8,128)(2,1)} %bitcast.28), custom_call_target="tpu_custom_call" | custom-call | flops 536870912 | tf_op jit(solution)/shard_map/near0/pallas_call | solution.py:181
  7.8 0.9 %copy.17 = bf16[2,256,2048]{2,1,0:T(8,128)(2,1)S(1)} copy(bf16[2,256,2048]{2,0,1:T(2,128)(2,1)S(1)} %bitcast.31) | data formatting | bytes 4194304 | tf_op jit(solution)/shard_map/transpose | solution.py:420
  8.7 2.4 %near1.1 = (bf16[64,256,128]{2,1,0:T(8,128)(2,1)S(1)}, f32[256,2176]{1,0:T(8,128)S(1)}) custom-call(s32[2,64]{1,0:T(2,128)} %bitcast.44, s32[1]{0:T(128)S(6)} %copy.27.count_hbm, s32[1,16]{1,0:T(1,128)} %order_hbm.9, bf16[16,256,256]{2,1,0:T(8,128)(2,1)S(1)} %get-tuple-element.10.mixed_ref, ...), custom_call_target="tpu_custom_call", output_to_operand_aliasing={{0}: (5, {}), {1}: (6, {})} | custom-call | flops 536870912 | tf_op jit(solution)/shard_map/near1/pallas_call | solution.py:234
  11.1 0.0 collective-permute-done
  11.1 1.3 %collective-permute-start.2 = (bf16[128,256]{1,0:T(8,128)(2,1)S(1)}, bf16[128,256]{1,0:T(8,128)(2,1)S(1)}, u32[]{:S(2)}, u32[]{:S(2)}) collective-permute-start(bf16[128,256]{1,0:T(8,128)(2,1)S(1)} %fusion.6), channel_id=1, source_target_pairs={{0,2},{2,0},{4,6},{6,4},{8,10},{10,8},{12,14},{14,12},{1,3},{3,1},... | collective-permute-start | bytes 196616 | tf_op jit(solution)/shard_map/ppermute | solution.py:31
  12.4 1.9 %collective-permute-done.2 = bf16[128,256]{1,0:T(8,128)(2,1)S(1)} collective-permute-done((bf16[128,256]{1,0:T(8,128)(2,1)S(1)}, bf16[128,256]{1,0:T(8,128)(2,1)S(1)}, u32[]{:S(2)}, u32[]{:S(2)}) %collective-permute-start.2) | collective-permute-done | bytes 65568 | tf_op jit(solution)/shard_map/ppermute | solution.py:31
  14.3 0.1 fusion.5
  14.4 0.2 fusion.7
  14.6 0.1 pad_maximum_fusion
  14.7 0.2 fusion
  15.0 0.2 collective-permute-start.4
  15.2 0.2 fusion.22
  15.4 2.8 %collective-permute-done.4 = bf16[128,256]{1,0:T(8,128)(2,1)S(1)} collective-permute-done((bf16[128,256]{1,0:T(8,128)(2,1)S(1)}, bf16[128,256]{1,0:T(8,128)(2,1)S(1)}, u32[]{:S(2)}, u32[]{:S(2)}) %collective-permute-start.4) | collective-permute-done | bytes 65568 | tf_op jit(solution)/shard_map/ppermute | solution.py:31
  18.2 0.2 fusion.1
  18.4 0.1 collective-permute-start.5
  18.5 0.2 fusion.37
  18.7 4.3 %collective-permute-done.5 = bf16[128,256]{1,0:T(8,128)(2,1)S(1)} collective-permute-done((bf16[128,256]{1,0:T(8,128)(2,1)S(1)}, bf16[128,256]{1,0:T(8,128)(2,1)S(1)}, u32[]{:S(2)}, u32[]{:S(2)}) %collective-permute-start.5) | collective-permute-done | bytes 65568 | tf_op jit(solution)/shard_map/ppermute | solution.py:31
  23.1 0.2 fusion.45
  23.3 3.8 %collective-permute-start.6 = (bf16[128,256]{1,0:T(8,128)(2,1)S(1)}, bf16[128,256]{1,0:T(8,128)(2,1)S(1)}, u32[]{:S(2)}, u32[]{:S(2)}) collective-permute-start(bf16[128,256]{1,0:T(8,128)(2,1)S(1)} %maximum_select_fusion.2.coeff_ref), channel_id=1, source_target_pairs={{0,1},{1,0},{2,3},{3,2},{4,5},{5,4},{6,7},{7,6},{8,9},{9,8},{10,11... | collective-permute-start | bytes 196616 | tf_op jit(solution)/shard_map/ppermute | solution.py:31
  27.1 2.6 %near2.1.near_ref = f32[256,2176]{1,0:T(8,128)S(1)} custom-call(s32[2,64]{1,0:T(2,128)} %bitcast.45, s32[1]{0:T(128)S(6)} %copy.27.count_hbm, s32[1,16]{1,0:T(1,128)} %order_hbm.9, bf16[16,256,256]{2,1,0:T(8,128)(2,1)S(1)} %get-tuple-element.10.mixed_ref, bf16[64,256,128]{2,1,0:T(8,128)(2,1)S(1)} %get-tuple-element.13.tiles_ref, ...), custom_call_target="tpu_custom_call", output_to_operand_aliasing={{}: (5, {})} | custom-call | flops 536870912 | tf_op jit(solution)/shard_map/near2/pallas_call | solution.py:280
  29.8 2.0 %expand0.1.refs_0_ = bf16[256,2048]{1,0:T(8,128)(2,1)} custom-call(s32[1,16]{1,0:T(1,128)} %order_hbm.9, bf16[128,256]{1,0:T(8,128)(2,1)S(1)} %maximum_select_fusion.2.coeff_ref, bf16[512,2048]{1,0:T(8,128)(2,1)S(1)} %bitcast.26, f32[256,2176]{1,0:T(8,128)S(1)} %near2.1.near_ref), custom_call_target="tpu_custom_call" | custom-call | flops 268435456 | tf_op jit(solution)/shard_map/expand0/pallas_call | solution.py:345
  31.8 2.0 %expand1.1 = bf16[256,2048]{1,0:T(8,128)(2,1)} custom-call(s32[1,16]{1,0:T(1,128)} %order_hbm.9, bf16[128,256]{1,0:T(8,128)(2,1)S(1)} %collective-permute-done.6.coeff_ref, bf16[512,2048]{1,0:T(8,128)(2,1)S(1)} %bitcast.27, f32[256,2176]{1,0:T(8,128)S(1)} %near2.1.near_ref, bf16[256,2048]{1,0:T(8,128)(2,1)} %expand0.1.refs_0_), custom_call_target="tpu_custom_call", output_to_operand_aliasing={{}: (4, {})} | custom-call | flops 268435456 | tf_op jit(solution)/shard_map/expand1/pallas_call | solution.py:345
  (26 shorter events, 0.3 us)
Async XLA Ops:
  0.0 2.1 %copy-start = (bf16[256,2048]{1,0:T(8,128)(2,1)S(1)}, bf16[256,2048]{1,0:T(8,128)(2,1)}, u32[]{:S(2)}) copy-start(bf16[256,2048]{1,0:T(8,128)(2,1)} %dens_ref.1) | copy-start | bytes 3145732
  2.1 1.6 %copy-start.2 = (bf16[3,256,2,128]{3,2,1,0:T(2,128)(2,1)S(1)}, bf16[3,256,2,128]{3,2,1,0:T(2,128)(2,1)}, u32[]{:S(2)}) copy-start(bf16[3,256,2,128]{3,2,1,0:T(2,128)(2,1)} %param.11) | copy-start | bytes 1179652
  2.2 1.8 %copy-start.3 = (bf16[3,256,2,128]{3,2,1,0:T(2,128)(2,1)S(1)}, bf16[3,256,2,128]{3,2,1,0:T(2,128)(2,1)}, u32[]{:S(2)}) copy-start(bf16[3,256,2,128]{3,2,1,0:T(2,128)(2,1)} %param.12) | copy-start | bytes 1179652
  3.0 8.1 %collective-permute-start = (bf16[128,256]{1,0:T(8,128)(2,1)S(1)}, bf16[128,256]{1,0:T(8,128)(2,1)S(1)}, u32[]{:S(2)}, u32[]{:S(2)}) collective-permute-start(bf16[128,256]{1,0:T(8,128)(2,1)S(1)} %pad_maximum_fusion.2), channel_id=1, source_target_pairs={{0,1},{1,0},{2,3},{3,2},{4,5},{5,4},{6,7},{7,6},{8,9},{9,8},{10,11... | collective-permute-start | bytes 196616 | tf_op jit(solution)/shard_map/ppermute | solution.py:31
  3.8 10.5 %collective-permute-start.1 = (bf16[3,2,256,128]{3,2,1,0:T(8,128)(2,1)S(1)}, bf16[3,2,256,128]{3,2,1,0:T(8,128)(2,1)S(1)}, u32[]{:S(2)}, u32[]{:S(2)}) collective-permute-start(bf16[3,2,256,128]{3,2,1,0:T(8,128)(2,1)S(1)} %bitcast.35), channel_id=1, source_target_pairs={{0,1},{1,0},{2,3},{3,2},{4,5},{5,4},{6,7},{7,6},{8,9},{9,8},{10,11... | collective-permute-start | bytes 1179656 | tf_op jit(solution)/shard_map/ppermute | solution.py:31
  4.0 10.6 %collective-permute-start.3 = (bf16[3,2,256,128]{3,2,1,0:T(8,128)(2,1)S(1)}, bf16[3,2,256,128]{3,2,1,0:T(8,128)(2,1)S(1)}, u32[]{:S(2)}, u32[]{:S(2)}) collective-permute-start(bf16[3,2,256,128]{3,2,1,0:T(8,128)(2,1)S(1)} %bitcast.33), channel_id=1, source_target_pairs={{0,1},{1,0},{2,3},{3,2},{4,5},{5,4},{6,7},{7,6},{8,9},{9,8},{10,11... | collective-permute-start | bytes 1179656 | tf_op jit(solution)/shard_map/ppermute | solution.py:31
  5.1 2.7 %copy-start.1 = (bf16[256,2,2048]{2,1,0:T(2,128)(2,1)S(1)}, bf16[256,2,2048]{2,1,0:T(2,128)(2,1)}, u32[]{:S(2)}) copy-start(bf16[256,2,2048]{2,1,0:T(2,128)(2,1)} %param.13) | copy-start | bytes 6291460
  11.1 3.2 %collective-permute-start.2 = (bf16[128,256]{1,0:T(8,128)(2,1)S(1)}, bf16[128,256]{1,0:T(8,128)(2,1)S(1)}, u32[]{:S(2)}, u32[]{:S(2)}) collective-permute-start(bf16[128,256]{1,0:T(8,128)(2,1)S(1)} %fusion.6), channel_id=1, source_target_pairs={{0,2},{2,0},{4,6},{6,4},{8,10},{10,8},{12,14},{14,12},{1,3},{3,1},... | collective-permute-start | bytes 196616 | tf_op jit(solution)/shard_map/ppermute | solution.py:31
  15.0 3.2 %collective-permute-start.4 = (bf16[128,256]{1,0:T(8,128)(2,1)S(1)}, bf16[128,256]{1,0:T(8,128)(2,1)S(1)}, u32[]{:S(2)}, u32[]{:S(2)}) collective-permute-start(bf16[128,256]{1,0:T(8,128)(2,1)S(1)} %maximum_select_fusion), channel_id=1, source_target_pairs={{0,4},{2,6},{4,0},{6,2},{8,12},{10,14},{12,8},{14,10},{1,5},{3,7},... | collective-permute-start | bytes 196616 | tf_op jit(solution)/shard_map/ppermute | solution.py:31
  18.4 4.6 %collective-permute-start.5 = (bf16[128,256]{1,0:T(8,128)(2,1)S(1)}, bf16[128,256]{1,0:T(8,128)(2,1)S(1)}, u32[]{:S(2)}, u32[]{:S(2)}) collective-permute-start(bf16[128,256]{1,0:T(8,128)(2,1)S(1)} %maximum_select_fusion.1), channel_id=1, source_target_pairs={{0,8},{2,10},{4,12},{6,14},{8,0},{10,2},{12,4},{14,6},{1,9},{3,11}... | collective-permute-start | bytes 196616 | tf_op jit(solution)/shard_map/ppermute | solution.py:31
  23.3 8.5 %collective-permute-start.6 = (bf16[128,256]{1,0:T(8,128)(2,1)S(1)}, bf16[128,256]{1,0:T(8,128)(2,1)S(1)}, u32[]{:S(2)}, u32[]{:S(2)}) collective-permute-start(bf16[128,256]{1,0:T(8,128)(2,1)S(1)} %maximum_select_fusion.2.coeff_ref), channel_id=1, source_target_pairs={{0,1},{1,0},{2,3},{3,2},{4,5},{5,4},{6,7},{7,6},{8,9},{9,8},{10,11... | collective-permute-start | bytes 196616 | tf_op jit(solution)/shard_map/ppermute | solution.py:31

commit v5 on v4

--- a/solution.py
+++ b/solution.py
@@ -1,5 +1,3 @@
-import functools
-
 import jax
 import jax.numpy as jnp
 from jax import lax
@@ -8,7 +6,8 @@
 from jax.sharding import PartitionSpec as P
 
 
-NEAR_SHARES = (0, 1, 4, 8)
+NEAR_SHARES = (0, 0, 3, 8)
+FETCH_SHARES = (0, 5, 8)
 EXPAND_CHUNKS = 4
 UNROLL = 8
 
@@ -55,9 +54,9 @@
         mixed_ref[cluster] = woven.astype(jnp.bfloat16)
 
 
-def bounds(count, call):
+def bounds(count, shares, call):
     trips = (count + UNROLL - 1) // UNROLL
-    return (trips * NEAR_SHARES[call]) // NEAR_SHARES[-1]
+    return (trips * shares[call] + shares[-1] - 1) // shares[-1]
 
 
 def tile_copy(tiles_hbm, tiles_ref, sems, trip):
@@ -89,12 +88,11 @@
     lax.fori_loop(0, order_ref.shape[1], body, 0)
 
 
-def add_tiles(first, last, pairs_ref, inverse_ref, count, mixed_ref, tiles_ref, total, ready):
+def add_tiles(first, last, pairs_ref, inverse_ref, count, mixed_ref, tiles_ref, total):
     clusters = mixed_ref.shape[0]
     width = tiles_ref.shape[2]
 
     def body(trip, carry):
-        ready(trip)
         for lane in range(UNROLL):
             slot = trip * UNROLL + lane
             target = jnp.where(slot < count, inverse_ref[pairs_ref[0, slot]], clusters)
@@ -122,41 +120,20 @@
 
 
 def first_kernel(
-    pairs_hbm,
-    count_hbm,
-    order_hbm,
-    dens_ref,
-    tiles_hbm,
-    mixed_ref,
-    tiles_ref,
-    total,
-    weave,
-    pairs_ref,
-    count_ref,
-    order_ref,
-    inverse_ref,
-    table_sems,
-    tile_sems,
+    count_hbm, dens_ref, tiles_hbm, mixed_ref, tiles_ref, total, weave, count_ref, table_sem, tile_sems
 ):
-    finish = fetch(
-        (pairs_hbm, count_hbm, order_hbm), (pairs_ref, count_ref, order_ref), table_sems
-    )
+    finish = fetch((count_hbm,), (count_ref,), table_sem)
     clusters = mixed_ref.shape[0]
     prepare_weave(weave)
     weave_into(mixed_ref, dens_ref, weave, 0, clusters // 2)
     finish()
     count = count_ref[0]
-    middle, last = bounds(count, 1), bounds(count, 2)
+    last = bounds(count, FETCH_SHARES, 1)
     start_tiles(tiles_hbm, tiles_ref, tile_sems, 0, last)
-    invert(order_ref, inverse_ref)
     weave_into(mixed_ref, dens_ref, weave, clusters // 2, clusters)
     total[...] = jnp.zeros_like(total)
 
-    def ready(trip):
-        tile_copy(tiles_hbm, tiles_ref, tile_sems, trip).wait()
-
-    add_tiles(0, middle, pairs_ref, inverse_ref, count, mixed_ref, tiles_ref, total, ready)
-    wait_tiles(tiles_hbm, tiles_ref, tile_sems, middle, last)
+    wait_tiles(tiles_hbm, tiles_ref, tile_sems, 0, last)
 
 
 def in_place(value):
@@ -174,9 +151,8 @@
     return [pltpu.SMEM(array.shape, array.dtype) for array in arrays]
 
 
-def first_call(pairs, count, order, densities, tiles):
+def first_call(count, densities, tiles, clusters):
     rows = densities.shape[0]
-    clusters = order.shape[1]
     slots, depth, width = tiles.shape
     return pl.pallas_call(
         first_kernel,
@@ -185,19 +161,18 @@
             jax.ShapeDtypeStruct(tiles.shape, tiles.dtype),
             jax.ShapeDtypeStruct((rows, (clusters + 1) * width), jnp.float32),
         ),
-        in_specs=[in_hbm(), anywhere(), in_hbm(), in_vmem(), in_hbm()],
+        in_specs=[anywhere(), in_vmem(), in_hbm()],
         out_specs=(in_vmem(), in_vmem(), in_vmem()),
         scratch_shapes=[
             pltpu.VMEM((depth, depth), jnp.bfloat16),
-            *tables(pairs, count, order),
-            pltpu.SMEM((clusters,), jnp.int32),
-            pltpu.SemaphoreType.DMA((3,)),
+            *tables(count),
+            pltpu.SemaphoreType.DMA((1,)),
             pltpu.SemaphoreType.DMA((slots // UNROLL,)),
         ],
         cost_estimate=near_cost(rows, tiles),
         compiler_params=pltpu.CompilerParams(vmem_limit_bytes=16 << 20),
         name="near0",
-    )(in_place(pairs), count, in_place(order), densities, in_place(tiles))
+    )(count, densities, in_place(tiles))
 
 
 def second_kernel(
@@ -219,13 +194,12 @@
 ):
     fetch((pairs_hbm, count_hbm, order_hbm), (pairs_ref, count_ref, order_ref), table_sems)()
     count = count_ref[0]
-    first, middle, last = bounds(count, 1), bounds(count, 2), bounds(count, 3)
-    start_tiles(tiles_hbm, tiles_ref, tile_sems, middle, last)
+    first, last = bounds(count, FETCH_SHARES, 1), bounds(count, FETCH_SHARES, 2)
+    start_tiles(tiles_hbm, tiles_ref, tile_sems, first, last)
     invert(order_ref, inverse_ref)
-    add_tiles(
-        first, middle, pairs_ref, inverse_ref, count, mixed_ref, tiles_ref, total, lambda trip: None
-    )
-    wait_tiles(tiles_hbm, tiles_ref, tile_sems, middle, last)
+    end = bounds(count, NEAR_SHARES, 2)
+    add_tiles(0, end, pairs_ref, inverse_ref, count, mixed_ref, tiles_ref, total)
+    wait_tiles(tiles_hbm, tiles_ref, tile_sems, first, last)
 
 
 def second_call(pairs, count, order, mixed, tiles, fetched, total):
@@ -268,11 +242,9 @@
 ):
     fetch((pairs_hbm, count_hbm, order_hbm), (pairs_ref, count_ref, order_ref), table_sems)()
     count = count_ref[0]
-    first, last = bounds(count, 2), bounds(count, 3)
     invert(order_ref, inverse_ref)
-    add_tiles(
-        first, last, pairs_ref, inverse_ref, count, mixed_ref, tiles_ref, total, lambda trip: None
-    )
+    first, last = bounds(count, NEAR_SHARES, 2), bounds(count, NEAR_SHARES, 3)
+    add_tiles(first, last, pairs_ref, inverse_ref, count, mixed_ref, tiles_ref, total)
 
 
 def third_call(pairs, count, order, mixed, fetched, total):
@@ -294,72 +266,95 @@
     )(in_place(pairs), count, in_place(order), mixed, fetched, total)
 
 
-def expand_kernel(axis, flip, order_hbm, coeff_ref, matrix_ref, near_ref, *refs):
-    out_hbm, rows_out, order_ref, table_sem, sems = refs[-5:]
-    rows = near_ref.shape[0]
-    quarter = rows // 4
+def far_rows(half, coeff_ref, matrix_ref, near_ref, rows_ref, columns):
+    quarter = near_ref.shape[0] // 4
+    far = jnp.dot(
+        paired(coeff_ref[...]), matrix_ref[:, columns], preferred_element_type=jnp.float32
+    )
+    for part in range(2):
+        source = pl.ds(pl.multiple_of((2 * part + half) * quarter, quarter), quarter)
+        inner = slice(part * quarter, (part + 1) * quarter)
+        rows_ref[inner, columns] = (far[inner] + near_ref[source, columns]).astype(jnp.bfloat16)
+
+
+def own_kernel(coeff_ref, matrix_ref, near_ref, rows_ref):
+    span = matrix_ref.shape[1] // EXPAND_CHUNKS
+    for chunk in range(EXPAND_CHUNKS):
+        columns = slice(chunk * span, (chunk + 1) * span)
+        far_rows(lax.axis_index("tgt"), coeff_ref, matrix_ref, near_ref, rows_ref, columns)
+
+
+def expand_cost(coefficients, matrix):
+    return pl.CostEstimate(
+        flops=4 * coefficients.size * matrix.shape[1], bytes_accessed=0, transcendentals=0
+    )
+
+
+def own_call(coefficients, matrix, near):
+    return pl.pallas_call(
+        own_kernel,
+        out_shape=jax.ShapeDtypeStruct((coefficients.shape[0], matrix.shape[1]), jnp.bfloat16),
+        in_specs=[in_vmem(), in_vmem(), in_vmem()],
+        out_specs=in_vmem(),
+        cost_estimate=expand_cost(coefficients, matrix),
+        compiler_params=pltpu.CompilerParams(vmem_limit_bytes=16 << 20),
+        name="expand0",
+    )(coefficients, matrix, near)
+
+
+def last_kernel(order_ref, early_ref, coeff_ref, matrix_ref, near_ref, out_hbm, rows_ref, sems):
+    quarter = near_ref.shape[0] // 4
     points = matrix_ref.shape[1]
     clusters = order_ref.shape[1]
     width = points // clusters
-    finish = fetch((order_hbm,), (order_ref,), table_sem)
-    core = lax.axis_index(axis)
-    half = 1 - core if flip else core
-    left = paired(coeff_ref[...])
+    core = lax.axis_index("tgt")
+    order = order_ref[...]
+    copies = []
+
+    def send(buffer, half, cluster, sem):
+        place = pl.multiple_of(order[0, cluster] * width, width)
+        for part in range(2):
+            target = pl.ds(pl.multiple_of((2 * part + half) * quarter, quarter), quarter)
+            copy = pltpu.make_async_copy(
+                buffer.at[
+                    part * quarter : (part + 1) * quarter, cluster * width : (cluster + 1) * width
+                ],
+                out_hbm.at[target, pl.ds(place, width)],
+                sems.at[sem + 2 * cluster + part],
+            )
+            copy.start()
+            copies.append(copy)
+
+    for cluster in range(clusters):
+        send(early_ref, core, cluster, 0)
     span = points // EXPAND_CHUNKS
-    copies = []
     for chunk in range(EXPAND_CHUNKS):
         columns = slice(chunk * span, (chunk + 1) * span)
-        far = jnp.dot(left, matrix_ref[:, columns], preferred_element_type=jnp.float32)
-        for part in range(2):
-            source = pl.ds(pl.multiple_of((2 * part + half) * quarter, quarter), quarter)
-            inner = slice(part * quarter, (part + 1) * quarter)
-            rows_out[inner, columns] = (far[inner] + near_ref[source, columns]).astype(jnp.bfloat16)
-        if chunk == 0:
-            finish()
-        for cluster in range(chunk * clusters // EXPAND_CHUNKS, (chunk + 1) * clusters // EXPAND_CHUNKS):
-            place = pl.multiple_of(order_ref[0, cluster] * width, width)
-            for part in range(2):
-                target = pl.ds(pl.multiple_of((2 * part + half) * quarter, quarter), quarter)
-                copy = pltpu.make_async_copy(
-                    rows_out.at[part * quarter : (part + 1) * quarter, cluster * width : (cluster + 1) * width],
-                    out_hbm.at[target, pl.ds(place, width)],
-                    sems.at[2 * cluster + part],
-                )
-                copy.start()
-                copies.append(copy)
+        far_rows(1 - core, coeff_ref, matrix_ref, near_ref, rows_ref, columns)
+        for cluster in range(
+            chunk * clusters // EXPAND_CHUNKS, (chunk + 1) * clusters // EXPAND_CHUNKS
+        ):
+            send(rows_ref, 1 - core, cluster, 2 * clusters)
     for copy in copies:
         copy.wait()
 
 
-def expand_call(flip, order, coefficients, matrix, near, result):
-    clusters = order.shape[1]
+def last_call(order, early, coefficients, matrix, near):
     rows = near.shape[0]
     points = matrix.shape[1]
-    operands = [in_place(order), coefficients, matrix, near]
-    specs = [in_hbm(), in_vmem(), in_vmem(), in_vmem()]
-    aliases = {}
-    if result is not None:
-        operands.append(result)
-        specs.append(in_hbm())
-        aliases = {4: 0}
     return pl.pallas_call(
-        functools.partial(expand_kernel, "tgt", flip),
+        last_kernel,
         out_shape=jax.ShapeDtypeStruct((rows, points), jnp.bfloat16),
-        in_specs=specs,
+        in_specs=[in_vmem()] * 5,
         out_specs=in_hbm(),
-        input_output_aliases=aliases,
         scratch_shapes=[
             pltpu.VMEM((rows // 2, points), jnp.bfloat16),
-            pltpu.SMEM(order.shape, order.dtype),
-            pltpu.SemaphoreType.DMA((1,)),
-            pltpu.SemaphoreType.DMA((2 * clusters,)),
+            pltpu.SemaphoreType.DMA((4 * order.shape[1],)),
         ],
-        cost_estimate=pl.CostEstimate(
-            flops=4 * rows * matrix.shape[0] * points // 4, bytes_accessed=0, transcendentals=0
-        ),
+        cost_estimate=expand_cost(coefficients, matrix),
         compiler_params=pltpu.CompilerParams(vmem_limit_bytes=16 << 20),
-        name="expand1" if flip else "expand0",
-    )(*operands)
+        name="expand1",
+    )(order, early, coefficients, matrix, near)
 
 
 def shards(
@@ -401,7 +396,7 @@
     for section in range(sections):
         partner = swapped(coefficients, "src", section)
         if section == 0:
-            mixed, fetched, near = first_call(pairs, count, cluster_order, densities, tiles)
+            mixed, fetched, near = first_call(count, densities, tiles, clusters)
         elif section == 1:
             fetched, near = second_call(pairs, count, cluster_order, mixed, tiles, fetched, near)
         elif section == 2:
@@ -418,8 +413,8 @@
         coefficients = jnp.where(first_core, updated, turned)
     others = swapped(coefficients, "tgt", 0)
     matrix = expand.transpose(1, 0, 2).reshape(2 * rank, points)
-    result = expand_call(False, cluster_order, coefficients, matrix, near, None)
-    return expand_call(True, cluster_order, others, matrix, near, result)
+    early = own_call(coefficients, matrix, near)
+    return last_call(cluster_order, early, others, matrix, near)
 
 
 def solution(mesh):

time: 34 us -> 32.2 us (0.947)
  the two profiles are of different devices: /device:TPU:25 before, /device:TPU:29 now
where the time goes in v5:
time: 32.2 us; the launch traced here: 32 us
  waiting for transfers between devices  10.4 us (32%)
  Pallas kernels  9.81 us (30%)
  starting transfers between devices  5.21 us (16%)
  local copies, waits for them, and re-layouts  3.33 us (10%)
  matrix products  1.85 us (6%)
  between operations  0.98 us (3%)
  other arithmetic  0.42 us (1%)
    ppermute x7, waiting for transfers between devices, swapped(): return lax.ppermute(value, axis, pairs)  10.4 us
    ppermute x7, starting transfers between devices, swapped(): return lax.ppermute(value, axis, pairs)  5.21 us
    pallas_call x1, Pallas kernels, first_call(): pl.pallas_call(first_kernel, out_shape=(jax.ShapeDtypeStruct((clusters, r...  2.69 us
    pallas_call x1, Pallas kernels, third_call(): pl.pallas_call(third_kernel, out_shape=jax.ShapeDtypeStruct(total.shape,...  2.64 us
    unnamed x13, local copies, waits for them, and re-layouts  2.43 us
    pallas_call x1, Pallas kernels, second_call(): pl.pallas_call(second_kernel, out_shape=(jax.ShapeDtypeStruct(fetched.sha...  2.32 us
    pallas_call x1, Pallas kernels, last_call(): pl.pallas_call(last_kernel, out_shape=jax.ShapeDtypeStruct((rows, points)...  1.7 us
    transpose x1, local copies, waits for them, and re-layouts, shards(): matrix = expand.transpose(1, 0, 2).reshape(2 * rank, points)  0.88 us
  transfers between devices with their start and end apart: 7, of which 3 were waited for; matrix products, arithmetic and copies ran while one was open for 5% of the time, Pallas kernels for 25%

profile of v5, /device:TPU:29, one launch (start us, length us, event | category | flops | bytes accessed | tf_op | source)
XLA Modules:
  0.0 32.0 jit_solution(11206237069991093566)
XLA Ops:
  0.0 2.1 %copy.17 = bf16[256,8,2,256]{3,1,2,0:T(8,128)(2,1)S(1)} copy(bf16[256,8,2,256]{3,2,1,0:T(2,128)(2,1)} %bitcast.30) | data formatting | bytes 4194304
  2.1 0.0 copy-start.3
  2.2 0.0 copy-start.4
  2.2 0.7 %fusion.62 = f32[256,512]{1,0:T(8,128)S(1)} fusion(bf16[256,2048]{1,0:T(8,128)(2,1)S(1)} %copy-done, bf16[2048,512]{1,0:T(8,128)(2,1)S(1)} %bitcast.32), kind=kOutput, calls=%fused_computation.94 | convolution fusion | flops 536870912 | bytes 3670016 | tf_op jit(solution)/shard_map/dot_general | solution.py:374
  3.0 0.7 %collective-permute-start = (bf16[128,256]{1,0:T(8,128)(2,1)S(1)}, bf16[128,256]{1,0:T(8,128)(2,1)S(1)}, u32[]{:S(2)}, u32[]{:S(2)}) collective-permute-start(bf16[128,256]{1,0:T(8,128)(2,1)S(1)} %pad_maximum_fusion.2), channel_id=1, source_target_pairs={{0,1},{1,0},{2,3},{3,2},{4,5},{5,4},{6,7},{7,6},{8,9},{9,8},{10,11... | collective-permute-start | bytes 196616 | tf_op jit(solution)/shard_map/ppermute | solution.py:30
  3.7 0.1 copy.21
  3.8 0.2 collective-permute-start.1
  3.9 0.1 copy.20
  4.0 0.5 %collective-permute-start.3 = (bf16[3,2,256,128]{3,2,1,0:T(8,128)(2,1)S(1)}, bf16[3,2,256,128]{3,2,1,0:T(8,128)(2,1)S(1)}, u32[]{:S(2)}, u32[]{:S(2)}) collective-permute-start(bf16[3,2,256,128]{3,2,1,0:T(8,128)(2,1)S(1)} %bitcast.33), channel_id=1, source_target_pairs={{0,1},{1,0},{2,3},{3,2},{4,5},{5,4},{6,7},{7,6},{8,9},{9,8},{10,11... | collective-permute-start | bytes 1179656 | tf_op jit(solution)/shard_map/ppermute | solution.py:30
  5.1 2.7 %near0.1 = (bf16[16,256,256]{2,1,0:T(8,128)(2,1)S(1)}, bf16[64,256,128]{2,1,0:T(8,128)(2,1)S(1)}, f32[256,2176]{1,0:T(8,128)S(1)}) custom-call(s32[1]{0:T(128)S(6)} %copy.25.count_hbm, bf16[256,2048]{1,0:T(8,128)(2,1)S(1)} %copy-done, bf16[64,256,128]{2,1,0:T(8,128)(2,1)} %bitcast.28), custom_call_target="tpu_custom_call" | custom-call | flops 536870912 | tf_op jit(solution)/shard_map/near0/pallas_call | solution.py:157
  7.8 0.9 %copy.16 = bf16[2,256,2048]{2,1,0:T(8,128)(2,1)S(1)} copy(bf16[2,256,2048]{2,0,1:T(2,128)(2,1)S(1)} %bitcast.31) | data formatting | bytes 4194304 | tf_op jit(solution)/shard_map/transpose | solution.py:415
  8.7 2.3 %near1.1 = (bf16[64,256,128]{2,1,0:T(8,128)(2,1)S(1)}, f32[256,2176]{1,0:T(8,128)S(1)}) custom-call(s32[2,64]{1,0:T(2,128)} %bitcast.43, s32[1]{0:T(128)S(6)} %copy.25.count_hbm, s32[1,16]{1,0:T(1,128)} %order_ref.1, bf16[16,256,256]{2,1,0:T(8,128)(2,1)S(1)} %get-tuple-element.10.mixed_ref, ...), custom_call_target="tpu_custom_call", output_to_operand_aliasing={{0}: (5, {}), {1}: (6, {})} | custom-call | flops 536870912 | tf_op jit(solution)/shard_map/near1/pallas_call | solution.py:208
  11.1 0.3 collective-permute-start.2
  11.4 3.3 %collective-permute-done.2 = bf16[128,256]{1,0:T(8,128)(2,1)S(1)} collective-permute-done((bf16[128,256]{1,0:T(8,128)(2,1)S(1)}, bf16[128,256]{1,0:T(8,128)(2,1)S(1)}, u32[]{:S(2)}, u32[]{:S(2)}) %collective-permute-start.2) | collective-permute-done | bytes 65568 | tf_op jit(solution)/shard_map/ppermute | solution.py:30
  14.7 0.1 fusion.5
  14.8 0.2 fusion.7
  15.0 0.1 pad_maximum_fusion
  15.1 0.2 fusion
  15.4 0.1 collective-permute-start.4
  15.5 0.2 fusion.22
  15.7 2.9 %collective-permute-done.4 = bf16[128,256]{1,0:T(8,128)(2,1)S(1)} collective-permute-done((bf16[128,256]{1,0:T(8,128)(2,1)S(1)}, bf16[128,256]{1,0:T(8,128)(2,1)S(1)}, u32[]{:S(2)}, u32[]{:S(2)}) %collective-permute-start.4) | collective-permute-done | bytes 65568 | tf_op jit(solution)/shard_map/ppermute | solution.py:30
  18.6 0.2 fusion.1
  18.8 0.1 collective-permute-start.5
  18.9 0.2 fusion.37
  19.1 4.2 %collective-permute-done.5 = bf16[128,256]{1,0:T(8,128)(2,1)S(1)} collective-permute-done((bf16[128,256]{1,0:T(8,128)(2,1)S(1)}, bf16[128,256]{1,0:T(8,128)(2,1)S(1)}, u32[]{:S(2)}, u32[]{:S(2)}) %collective-permute-start.5) | collective-permute-done | bytes 65568 | tf_op jit(solution)/shard_map/ppermute | solution.py:30
  23.3 0.2 fusion.45
  23.6 3.4 %collective-permute-start.6 = (bf16[128,256]{1,0:T(8,128)(2,1)S(1)}, bf16[128,256]{1,0:T(8,128)(2,1)S(1)}, u32[]{:S(2)}, u32[]{:S(2)}) collective-permute-start(bf16[128,256]{1,0:T(8,128)(2,1)S(1)} %maximum_select_fusion.2.coeff_ref), channel_id=1, source_target_pairs={{0,1},{1,0},{2,3},{3,2},{4,5},{5,4},{6,7},{7,6},{8,9},{9,8},{10,11... | collective-permute-start | bytes 196616 | tf_op jit(solution)/shard_map/ppermute | solution.py:30
  27.0 2.6 %near2.1.near_ref = f32[256,2176]{1,0:T(8,128)S(1)} custom-call(s32[2,64]{1,0:T(2,128)} %bitcast.44, s32[1]{0:T(128)S(6)} %copy.25.count_hbm, s32[1,16]{1,0:T(1,128)} %order_ref.1, bf16[16,256,256]{2,1,0:T(8,128)(2,1)S(1)} %get-tuple-element.10.mixed_ref, bf16[64,256,128]{2,1,0:T(8,128)(2,1)S(1)} %get-tuple-element.13.tiles_ref, ...), custom_call_target="tpu_custom_call", output_to_operand_aliasing={{}: (5, {})} | custom-call | flops 536870912 | tf_op jit(solution)/shard_map/near2/pallas_call | solution.py:252
  29.6 0.0 copy-start.1
  29.7 0.5 %expand0.1.early_ref = bf16[128,2048]{1,0:T(8,128)(2,1)S(1)} custom-call(bf16[128,256]{1,0:T(8,128)(2,1)S(1)} %maximum_select_fusion.2.coeff_ref, bf16[512,2048]{1,0:T(8,128)(2,1)S(1)} %bitcast.26, f32[256,2176]{1,0:T(8,128)S(1)} %near2.1.near_ref), custom_call_target="tpu_custom_call" | custom-call | flops 268435456 | tf_op jit(solution)/shard_map/expand0/pallas_call | solution.py:294
  30.1 0.2 copy-done.1
  30.3 1.7 %expand1.1 = bf16[256,2048]{1,0:T(8,128)(2,1)} custom-call(s32[1,16]{1,0:T(1,128)S(1)} %copy-done.1, bf16[128,2048]{1,0:T(8,128)(2,1)S(1)} %expand0.1.early_ref, bf16[128,256]{1,0:T(8,128)(2,1)S(1)} %collective-permute-done.6.coeff_ref, bf16[512,2048]{1,0:T(8,128)(2,1)S(1)} %bitcast.27, f32[256,2176]{1,0:T(8,128)S(1)} %near2.1.near_ref), custom_call_target="tpu_custom_call" | custom-call | flops 268435456 | tf_op jit(solution)/shard_map/expand1/pallas_call | solution.py:345
  (28 shorter events, 0.3 us)
Async XLA Ops:
  0.0 2.1 %copy-start = (bf16[256,2048]{1,0:T(8,128)(2,1)S(1)}, bf16[256,2048]{1,0:T(8,128)(2,1)}, u32[]{:S(2)}) copy-start(bf16[256,2048]{1,0:T(8,128)(2,1)} %dens_ref.1) | copy-start | bytes 3145732
  2.1 1.6 %copy-start.3 = (bf16[3,256,2,128]{3,2,1,0:T(2,128)(2,1)S(1)}, bf16[3,256,2,128]{3,2,1,0:T(2,128)(2,1)}, u32[]{:S(2)}) copy-start(bf16[3,256,2,128]{3,2,1,0:T(2,128)(2,1)} %param.11) | copy-start | bytes 1179652
  2.2 1.8 %copy-start.4 = (bf16[3,256,2,128]{3,2,1,0:T(2,128)(2,1)S(1)}, bf16[3,256,2,128]{3,2,1,0:T(2,128)(2,1)}, u32[]{:S(2)}) copy-start(bf16[3,256,2,128]{3,2,1,0:T(2,128)(2,1)} %param.12) | copy-start | bytes 1179652
  3.0 8.1 %collective-permute-start = (bf16[128,256]{1,0:T(8,128)(2,1)S(1)}, bf16[128,256]{1,0:T(8,128)(2,1)S(1)}, u32[]{:S(2)}, u32[]{:S(2)}) collective-permute-start(bf16[128,256]{1,0:T(8,128)(2,1)S(1)} %pad_maximum_fusion.2), channel_id=1, source_target_pairs={{0,1},{1,0},{2,3},{3,2},{4,5},{5,4},{6,7},{7,6},{8,9},{9,8},{10,11... | collective-permute-start | bytes 196616 | tf_op jit(solution)/shard_map/ppermute | solution.py:30
  3.8 10.9 %collective-permute-start.1 = (bf16[3,2,256,128]{3,2,1,0:T(8,128)(2,1)S(1)}, bf16[3,2,256,128]{3,2,1,0:T(8,128)(2,1)S(1)}, u32[]{:S(2)}, u32[]{:S(2)}) collective-permute-start(bf16[3,2,256,128]{3,2,1,0:T(8,128)(2,1)S(1)} %bitcast.35), channel_id=1, source_target_pairs={{0,1},{1,0},{2,3},{3,2},{4,5},{5,4},{6,7},{7,6},{8,9},{9,8},{10,11... | collective-permute-start | bytes 1179656 | tf_op jit(solution)/shard_map/ppermute | solution.py:30
  4.0 11.0 %collective-permute-start.3 = (bf16[3,2,256,128]{3,2,1,0:T(8,128)(2,1)S(1)}, bf16[3,2,256,128]{3,2,1,0:T(8,128)(2,1)S(1)}, u32[]{:S(2)}, u32[]{:S(2)}) collective-permute-start(bf16[3,2,256,128]{3,2,1,0:T(8,128)(2,1)S(1)} %bitcast.33), channel_id=1, source_target_pairs={{0,1},{1,0},{2,3},{3,2},{4,5},{5,4},{6,7},{7,6},{8,9},{9,8},{10,11... | collective-permute-start | bytes 1179656 | tf_op jit(solution)/shard_map/ppermute | solution.py:30
  5.1 2.7 %copy-start.2 = (bf16[256,2,2048]{2,1,0:T(2,128)(2,1)S(1)}, bf16[256,2,2048]{2,1,0:T(2,128)(2,1)}, u32[]{:S(2)}) copy-start(bf16[256,2,2048]{2,1,0:T(2,128)(2,1)} %param.13) | copy-start | bytes 6291460
  11.1 3.6 %collective-permute-start.2 = (bf16[128,256]{1,0:T(8,128)(2,1)S(1)}, bf16[128,256]{1,0:T(8,128)(2,1)S(1)}, u32[]{:S(2)}, u32[]{:S(2)}) collective-permute-start(bf16[128,256]{1,0:T(8,128)(2,1)S(1)} %fusion.6), channel_id=1, source_target_pairs={{0,2},{2,0},{4,6},{6,4},{8,10},{10,8},{12,14},{14,12},{1,3},{3,1},... | collective-permute-start | bytes 196616 | tf_op jit(solution)/shard_map/ppermute | solution.py:30
  15.4 3.2 %collective-permute-start.4 = (bf16[128,256]{1,0:T(8,128)(2,1)S(1)}, bf16[128,256]{1,0:T(8,128)(2,1)S(1)}, u32[]{:S(2)}, u32[]{:S(2)}) collective-permute-start(bf16[128,256]{1,0:T(8,128)(2,1)S(1)} %maximum_select_fusion), channel_id=1, source_target_pairs={{0,4},{2,6},{4,0},{6,2},{8,12},{10,14},{12,8},{14,10},{1,5},{3,7},... | collective-permute-start | bytes 196616 | tf_op jit(solution)/shard_map/ppermute | solution.py:30
  18.8 4.5 %collective-permute-start.5 = (bf16[128,256]{1,0:T(8,128)(2,1)S(1)}, bf16[128,256]{1,0:T(8,128)(2,1)S(1)}, u32[]{:S(2)}, u32[]{:S(2)}) collective-permute-start(bf16[128,256]{1,0:T(8,128)(2,1)S(1)} %maximum_select_fusion.1), channel_id=1, source_target_pairs={{0,8},{2,10},{4,12},{6,14},{8,0},{10,2},{12,4},{14,6},{1,9},{3,11}... | collective-permute-start | bytes 196616 | tf_op jit(solution)/shard_map/ppermute | solution.py:30
  23.6 6.5 %collective-permute-start.6 = (bf16[128,256]{1,0:T(8,128)(2,1)S(1)}, bf16[128,256]{1,0:T(8,128)(2,1)S(1)}, u32[]{:S(2)}, u32[]{:S(2)}) collective-permute-start(bf16[128,256]{1,0:T(8,128)(2,1)S(1)} %maximum_select_fusion.2.coeff_ref), channel_id=1, source_target_pairs={{0,1},{1,0},{2,3},{3,2},{4,5},{5,4},{6,7},{7,6},{8,9},{9,8},{10,11... | collective-permute-start | bytes 196616 | tf_op jit(solution)/shard_map/ppermute | solution.py:30
  29.6 0.7 %copy-start.1 = (s32[1,16]{1,0:T(1,128)S(1)}, s32[1,16]{1,0:T(1,128)}, u32[]{:S(2)}) copy-start(s32[1,16]{1,0:T(1,128)} %order_ref.1) | copy-start | bytes 196

commit v6 on v0

v6 whole, which is shorter than its diff:
```python
import functools

import jax
import jax.numpy as jnp
from jax import lax
from jax.experimental import pallas as pl
from jax.experimental.pallas import tpu as pltpu
from jax.sharding import PartitionSpec as P


EXPAND_CHUNKS = 4
UNROLL = 16


def in_vmem():
    return pl.BlockSpec(memory_space=pltpu.VMEM)


def in_smem():
    return pl.BlockSpec(memory_space=pltpu.SMEM)


def in_hbm():
    return pl.BlockSpec(memory_space=pltpu.HBM)


def swapped(value, axis, bit):
    mask = 2**bit
    pairs = [(source, source ^ mask) for source in range(lax.axis_size(axis))]
    return lax.ppermute(value, axis, pairs)


def paired(block):
    half = block.shape[0] // 2
    upper, lower = block[:half], block[half:]
    return jnp.concatenate(
        [jnp.concatenate([upper, -lower], axis=1), jnp.concatenate([lower, upper], axis=1)], axis=0
    )


def first_kernel(dens_ref, mixed_ref, total, weave):
    clusters = mixed_ref.shape[0]
    width = dens_ref.shape[1] // clusters
    row_id = lax.broadcasted_iota(jnp.int32, weave.shape, 0)
    col_id = lax.broadcasted_iota(jnp.int32, weave.shape, 1)
    goal = jnp.where(row_id < width, 2 * row_id, 2 * (row_id - width) + 1)
    weave[...] = jnp.where(col_id == goal, 1.0, 0.0).astype(jnp.bfloat16)
    for cluster in range(clusters):
        block = paired(dens_ref[:, cluster * width : (cluster + 1) * width])
        woven = jnp.dot(block, weave[...], preferred_element_type=jnp.float32)
        mixed_ref[cluster] = woven.astype(jnp.bfloat16)
    total[...] = jnp.zeros_like(total)


def tiles_kernel(first, last, table_ref, count_ref, mixed_ref, tiles_ref, before, total):
    clusters = mixed_ref.shape[0]
    width = tiles_ref.shape[2]
    count = count_ref[0]
    for start in range(first, last, UNROLL):

        @pl.when(start < count)
        def _():
            table = table_ref[...]
            for slot in range(start, min(start + UNROLL, last)):
                target = jnp.where(slot < count, table[0, slot], clusters)
                columns = pl.ds(pl.multiple_of(target * width, width), width)
                total[:, columns] += jnp.dot(
                    mixed_ref[table[1, slot]], tiles_ref[slot], preferred_element_type=jnp.float32
                )


def first_call(densities, clusters):
    rows, points = densities.shape
    width = points // clusters
    return pl.pallas_call(
        first_kernel,
        out_shape=(
            jax.ShapeDtypeStruct((clusters, rows, 2 * width), jnp.bfloat16),
            jax.ShapeDtypeStruct((rows, points + width), jnp.float32),
        ),
        in_specs=[in_vmem()],
        out_specs=(in_vmem(), in_vmem()),
        scratch_shapes=[pltpu.VMEM((2 * width, 2 * width), jnp.bfloat16)],
        cost_estimate=pl.CostEstimate(
            flops=4 * rows * points * width, bytes_accessed=0, transcendentals=0
        ),
        compiler_params=pltpu.CompilerParams(vmem_limit_bytes=16 << 20),
        name="weave",
    )(densities)


def tiles_call(first, last, table, count, mixed, tiles, total):
    depth, width = tiles.shape[1:]
    return pl.pallas_call(
        functools.partial(tiles_kernel, first, last),
        out_shape=jax.ShapeDtypeStruct(total.shape, total.dtype),
        in_specs=[in_vmem(), in_smem(), in_vmem(), in_vmem(), in_vmem()],
        out_specs=in_vmem(),
        input_output_aliases={4: 0},
        cost_estimate=pl.CostEstimate(
            flops=2 * total.shape[0] * depth * width * (last - first),
            bytes_accessed=0,
            transcendentals=0,
        ),
        compiler_params=pltpu.CompilerParams(vmem_limit_bytes=16 << 20),
        name="tiles",
    )(table, count, mixed, tiles, total)


def far_rows(half, coeff_ref, matrix_ref, near_ref, rows_ref, columns):
    quarter = near_ref.shape[0] // 4
    far = jnp.dot(
        paired(coeff_ref[...]), matrix_ref[:, columns], preferred_element_type=jnp.float32
    )
    for part in range(2):
        source = pl.ds(pl.multiple_of((2 * part + half) * quarter, quarter), quarter)
        inner = slice(part * quarter, (part + 1) * quarter)
        rows_ref[inner, columns] = (far[inner] + near_ref[source, columns]).astype(jnp.bfloat16)


def own_kernel(coeff_ref, matrix_ref, near_ref, rows_ref):
    span = matrix_ref.shape[1] // EXPAND_CHUNKS
    for chunk in range(EXPAND_CHUNKS):
        columns = slice(chunk * span, (chunk + 1) * span)
        far_rows(lax.axis_index("tgt"), coeff_ref, matrix_ref, near_ref, rows_ref, columns)


def expand_cost(coefficients, matrix):
    return pl.CostEstimate(
        flops=4 * coefficients.size * matrix.shape[1], bytes_accessed=0, transcendentals=0
    )


def own_call(coefficients, matrix, near):
    return pl.pallas_call(
        own_kernel,
        out_shape=jax.ShapeDtypeStruct((coefficients.shape[0], matrix.shape[1]), jnp.bfloat16),
        in_specs=[in_vmem(), in_vmem(), in_vmem()],
        out_specs=in_vmem(),
        cost_estimate=expand_cost(coefficients, matrix),
        compiler_params=pltpu.CompilerParams(vmem_limit_bytes=16 << 20),
        name="expand0",
    )(coefficients, matrix, near)


def last_kernel(order_ref, early_ref, coeff_ref, matrix_ref, near_ref, out_hbm, rows_ref, sems):
    quarter = near_ref.shape[0] // 4
    points = matrix_ref.shape[1]
    clusters = order_ref.shape[1]
    width = points // clusters
    core = lax.axis_index("tgt")
    order = order_ref[...]

    def send(buffer, half, cluster, sem):
        place = pl.multiple_of(order[0, cluster] * width, width)
        for part in range(2):
            target = pl.ds(pl.multiple_of((2 * part + half) * quarter, quarter), quarter)
            pltpu.make_async_copy(
                buffer.at[
                    part * quarter : (part + 1) * quarter, cluster * width : (cluster + 1) * width
                ],
                out_hbm.at[target, pl.ds(place, width)],
                sem,
            ).start()

    for cluster in range(clusters):
        send(early_ref, core, cluster, sems.at[0])
    span = points // EXPAND_CHUNKS
    for chunk in range(EXPAND_CHUNKS):
        columns = slice(chunk * span, (chunk + 1) * span)
        far_rows(1 - core, coeff_ref, matrix_ref, near_ref, rows_ref, columns)
        for cluster in range(
            chunk * clusters // EXPAND_CHUNKS, (chunk + 1) * clusters // EXPAND_CHUNKS
        ):
            send(rows_ref, 1 - core, cluster, sems.at[1])
    whole = out_hbm.at[0 : 2 * quarter, :]
    pltpu.make_async_copy(early_ref, whole, sems.at[0]).wait()
    pltpu.make_async_copy(rows_ref, whole, sems.at[1]).wait()


def last_call(order, early, coefficients, matrix, near):
    rows = near.shape[0]
    points = matrix.shape[1]
    return pl.pallas_call(
        last_kernel,
        out_shape=jax.ShapeDtypeStruct((rows, points), jnp.bfloat16),
        in_specs=[in_vmem()] * 5,
        out_specs=in_hbm(),
        scratch_shapes=[
            pltpu.VMEM((rows // 2, points), jnp.bfloat16),
            pltpu.SemaphoreType.DMA((2,)),
        ],
        cost_estimate=expand_cost(coefficients, matrix),
        compiler_params=pltpu.CompilerParams(vmem_limit_bytes=16 << 20),
        name="expand1",
    )(order, early, coefficients, matrix, near)


def shards(
    densities, compress, level_a, level_b, expand, near_tiles, tile_pairs, tile_count, cluster_order
):
    rows, points = densities.shape
    rank = compress.shape[2]
    sections = level_a.shape[0]
    clusters = cluster_order.shape[1]
    width = points // clusters
    slots = near_tiles.shape[0]
    core = lax.axis_index("tgt").astype(jnp.int32)
    tiles = near_tiles.reshape(slots, 2 * width, width)
    ids = jnp.arange(clusters, dtype=jnp.int32)
    found = cluster_order[0][None, :] == tile_pairs[:, 0][:, None]
    places = jnp.sum(jnp.where(found, ids[None, :], 0), axis=1)
    table = jnp.stack([places, tile_pairs[:, 1]])
    cut = slots // UNROLL // 2 * UNROLL
    half_rows = rows // 2

    product = jnp.dot(
        densities, compress.reshape(points, 2 * rank), preferred_element_type=jnp.float32
    )
    upper, lower = product[:half_rows], product[half_rows:]
    quarter = half_rows // 2
    first_core = core == 0
    keep, send = [], []
    for value in (upper[:, :rank] - lower[:, rank:], upper[:, rank:] + lower[:, :rank]):
        keep.append(jnp.where(first_core, value[:quarter], value[quarter:]))
        send.append(jnp.where(first_core, value[quarter:], value[:quarter]))
    keep = jnp.concatenate(keep, axis=0)
    arrived = swapped(jnp.concatenate(send, axis=0).astype(jnp.bfloat16), "tgt", 0)
    coefficients = (keep + arrived.astype(jnp.float32)).astype(jnp.bfloat16)

    def both(matrix):
        planes = matrix.transpose(0, 2, 1, 3)
        other = swapped(planes, "tgt", 0)
        joined = jnp.concatenate([planes, other], axis=3)
        return joined.reshape(sections, 2 * rank, rank)

    own_matrices, partner_matrices = both(level_a), both(level_b)
    for section in range(sections):
        partner = swapped(coefficients, "src", section)
        if section == 0:
            mixed, near = first_call(densities, clusters)
        elif section == 1:
            near = tiles_call(0, cut, table, tile_count, mixed, tiles, near)
        elif section == 2:
            near = tiles_call(cut, slots, table, tile_count, mixed, tiles, near)
        own = jnp.dot(
            paired(coefficients), own_matrices[section], preferred_element_type=jnp.float32
        )
        own = lax.optimization_barrier(own)
        updated = own + jnp.dot(
            paired(partner), partner_matrices[section], preferred_element_type=jnp.float32
        )
        updated = updated.astype(jnp.bfloat16)
        turned = jnp.concatenate([updated[:, rank // 2 :], updated[:, : rank // 2]], axis=1)
        coefficients = jnp.where(first_core, updated, turned)
    others = swapped(coefficients, "tgt", 0)
    matrix = expand.transpose(1, 0, 2).reshape(2 * rank, points)
    early = own_call(coefficients, matrix, near)
    return last_call(cluster_order, early, others, matrix, near)


def solution(mesh):
    placed = (
        P("grp", ("src", "tgt")),
        P(("grp", "src", "tgt"), None, None),
        P("grp", "src", None, "tgt"),
        P("grp", "src", None, "tgt"),
        P(("grp", "src"), None, "tgt"),
        P(("grp", "src", "tgt"), None, None, None),
        P(("grp", "src", "tgt"), None),
        P(("grp", "src", "tgt")),
        P(("grp", "src", "tgt"), None),
    )
    return jax.shard_map(
        shards, mesh=mesh, in_specs=placed, out_specs=P("grp", ("src", "tgt")), check_vma=False
    )
```

time: 93.8 us -> 30.7 us (0.33)
  the two profiles are of different devices: /device:TPU:0 before, /device:TPU:25 now
where the time goes in v6:
time: 30.7 us; the launch traced here: 30.5 us
  waiting for transfers between devices  9.4 us (31%)
  starting transfers between devices  6.36 us (21%)
  Pallas kernels  5.83 us (19%)
  local copies, waits for them, and re-layouts  5.52 us (18%)
  matrix products  1.84 us (6%)
  between operations  0.99 us (3%)
  other arithmetic  0.51 us (2%)
    ppermute x7, waiting for transfers between devices, swapped(): return lax.ppermute(value, axis, pairs)  9.4 us
    ppermute x7, starting transfers between devices, swapped(): return lax.ppermute(value, axis, pairs)  6.36 us
    unnamed x13, local copies, waits for them, and re-layouts  4.6 us
    pallas_call x2, Pallas kernels, tiles_call(): pl.pallas_call(functools.partial(tiles_kernel, first, last), out_shape=ja...  3.4 us
    pallas_call x1, Pallas kernels, last_call(): pl.pallas_call(last_kernel, out_shape=jax.ShapeDtypeStruct((rows, points)...  1.15 us
    transpose x1, local copies, waits for them, and re-layouts, shards(): matrix = expand.transpose(1, 0, 2).reshape(2 * rank, points)  0.89 us
    pallas_call x1, Pallas kernels, first_call(): pl.pallas_call(first_kernel, out_shape=(jax.ShapeDtypeStruct((clusters, r...  0.81 us
    dot_general x1, matrix products, shards(): jnp.dot(densities, compress.reshape(points, 2 * rank), preferred_element_...  0.7 us
  transfers between devices with their start and end apart: 7, of which 3 were waited for; matrix products, arithmetic and copies ran while one was open for 12% of the time, Pallas kernels for 15%

profile of v6, /device:TPU:25, one launch (start us, length us, event | category | flops | bytes accessed | tf_op | source)
XLA Modules:
  0.0 30.5 jit_solution(5478533540323125952)
XLA Ops:
  0.0 2.1 %copy.19 = bf16[256,8,2,256]{3,1,2,0:T(8,128)(2,1)S(1)} copy(bf16[256,8,2,256]{3,2,1,0:T(2,128)(2,1)} %bitcast.36) | data formatting | bytes 4194304
  2.1 0.7 %fusion.62 = f32[256,512]{1,0:T(8,128)S(1)} fusion(bf16[256,2048]{1,0:T(8,128)(2,1)S(1)} %copy-done.1, bf16[2048,512]{1,0:T(8,128)(2,1)S(1)} %bitcast.38), kind=kOutput, calls=%fused_computation.98 | convolution fusion | flops 536870912 | bytes 3670016 | tf_op jit(solution)/shard_map/dot_general | solution.py:217
  2.8 0.0 copy-start.4
  2.9 0.0 copy-start.3
  3.0 0.7 %collective-permute-start = (bf16[128,256]{1,0:T(8,128)(2,1)S(1)}, bf16[128,256]{1,0:T(8,128)(2,1)S(1)}, u32[]{:S(2)}, u32[]{:S(2)}) collective-permute-start(bf16[128,256]{1,0:T(8,128)(2,1)S(1)} %pad_maximum_fusion.2), channel_id=1, source_target_pairs={{0,1},{1,0},{2,3},{3,2},{4,5},{5,4},{6,7},{7,6},{8,9},{9,8},{10,11... | collective-permute-start | bytes 196616 | tf_op jit(solution)/shard_map/ppermute | solution.py:30
  3.7 1.0 %copy.23 = bf16[3,256,2,128]{3,1,2,0:T(8,128)(2,1)S(1)} copy(bf16[3,256,2,128]{3,2,1,0:T(2,128)(2,1)} %param.11) | data formatting | bytes 786432 | tf_op args[2]
  4.8 0.2 collective-permute-start.1
  4.9 1.0 %copy.22 = bf16[3,256,2,128]{3,1,2,0:T(8,128)(2,1)S(1)} copy(bf16[3,256,2,128]{3,2,1,0:T(2,128)(2,1)} %param.12) | data formatting | bytes 786432 | tf_op args[3]
  6.0 0.4 %collective-permute-start.3 = (bf16[3,2,256,128]{3,2,1,0:T(8,128)(2,1)S(1)}, bf16[3,2,256,128]{3,2,1,0:T(8,128)(2,1)S(1)}, u32[]{:S(2)}, u32[]{:S(2)}) collective-permute-start(bf16[3,2,256,128]{3,2,1,0:T(8,128)(2,1)S(1)} %bitcast.39), channel_id=1, source_target_pairs={{0,1},{1,0},{2,3},{3,2},{4,5},{5,4},{6,7},{7,6},{8,9},{9,8},{10,11... | collective-permute-start | bytes 1179656 | tf_op jit(solution)/shard_map/ppermute | solution.py:30
  7.2 0.9 %copy.18 = bf16[2,256,2048]{2,1,0:T(8,128)(2,1)S(1)} copy(bf16[2,256,2048]{2,0,1:T(2,128)(2,1)S(1)} %bitcast.37) | data formatting | bytes 4194304 | tf_op jit(solution)/shard_map/transpose | solution.py:257
  8.1 0.1 select_reduce_fusion
  8.2 0.8 %weave.1 = (bf16[16,256,256]{2,1,0:T(8,128)(2,1)S(1)}, f32[256,2176]{1,0:T(8,128)S(1)}) custom-call(bf16[256,2048]{1,0:T(8,128)(2,1)S(1)} %copy-done.1), custom_call_target="tpu_custom_call" | custom-call | flops 268435456 | tf_op jit(solution)/shard_map/weave/pallas_call | solution.py:75
  9.0 0.4 %copy-done = bf16[64,128,2,128]{3,2,1,0:T(2,128)(2,1)S(1)} copy-done((bf16[64,128,2,128]{3,2,1,0:T(2,128)(2,1)S(1)}, bf16[64,128,2,128]{3,2,1,0:T(2,128)(2,1)}, u32[]{:S(2)}) %copy-start) | copy-done | bytes 4194328
  9.3 1.7 %tiles.2.before = f32[256,2176]{1,0:T(8,128)S(1)} custom-call(s32[2,64]{1,0:T(2,128)S(1)} %pad_add_fusion.table_ref, s32[1]{0:T(128)S(6)} %copy.26.count_ref, bf16[16,256,256]{2,1,0:T(8,128)(2,1)S(1)} %get-tuple-element.7.mixed_ref, bf16[64,256,128]{2,1,0:T(8,128)(2,1)S(1)} %bitcast.33, ...), custom_call_target="tpu_custom_call", output_to_operand_aliasing={{}: (4, {})} | custom-call | flops 536870912 | tf_op jit(solution)/shard_map/tiles/pallas_call | solution.py:94
  11.1 1.3 %collective-permute-start.2 = (bf16[128,256]{1,0:T(8,128)(2,1)S(1)}, bf16[128,256]{1,0:T(8,128)(2,1)S(1)}, u32[]{:S(2)}, u32[]{:S(2)}) collective-permute-start(bf16[128,256]{1,0:T(8,128)(2,1)S(1)} %fusion.6), channel_id=1, source_target_pairs={{0,2},{2,0},{4,6},{6,4},{8,10},{10,8},{12,14},{14,12},{1,3},{3,1},... | collective-permute-start | bytes 196616 | tf_op jit(solution)/shard_map/ppermute | solution.py:30
  12.4 2.3 %collective-permute-done.2 = bf16[128,256]{1,0:T(8,128)(2,1)S(1)} collective-permute-done((bf16[128,256]{1,0:T(8,128)(2,1)S(1)}, bf16[128,256]{1,0:T(8,128)(2,1)S(1)}, u32[]{:S(2)}, u32[]{:S(2)}) %collective-permute-start.2) | collective-permute-done | bytes 65568 | tf_op jit(solution)/shard_map/ppermute | solution.py:30
  14.7 0.1 fusion.5
  14.8 0.2 fusion.7
  15.0 0.1 pad_maximum_fusion
  15.1 0.2 fusion
  15.4 0.2 collective-permute-start.4
  15.6 0.2 fusion.22
  15.8 2.7 %collective-permute-done.4 = bf16[128,256]{1,0:T(8,128)(2,1)S(1)} collective-permute-done((bf16[128,256]{1,0:T(8,128)(2,1)S(1)}, bf16[128,256]{1,0:T(8,128)(2,1)S(1)}, u32[]{:S(2)}, u32[]{:S(2)}) %collective-permute-start.4) | collective-permute-done | bytes 65568 | tf_op jit(solution)/shard_map/ppermute | solution.py:30
  18.5 0.2 fusion.1
  18.8 0.1 collective-permute-start.5
  18.9 0.2 fusion.37
  19.1 4.4 %collective-permute-done.5 = bf16[128,256]{1,0:T(8,128)(2,1)S(1)} collective-permute-done((bf16[128,256]{1,0:T(8,128)(2,1)S(1)}, bf16[128,256]{1,0:T(8,128)(2,1)S(1)}, u32[]{:S(2)}, u32[]{:S(2)}) %collective-permute-start.5) | collective-permute-done | bytes 65568 | tf_op jit(solution)/shard_map/ppermute | solution.py:30
  23.5 0.2 fusion.45
  23.7 3.4 %collective-permute-start.6 = (bf16[128,256]{1,0:T(8,128)(2,1)S(1)}, bf16[128,256]{1,0:T(8,128)(2,1)S(1)}, u32[]{:S(2)}, u32[]{:S(2)}) collective-permute-start(bf16[128,256]{1,0:T(8,128)(2,1)S(1)} %maximum_select_fusion.2.coeff_ref), channel_id=1, source_target_pairs={{0,1},{1,0},{2,3},{3,2},{4,5},{5,4},{6,7},{7,6},{8,9},{9,8},{10,11... | collective-permute-start | bytes 196616 | tf_op jit(solution)/shard_map/ppermute | solution.py:30
  27.1 1.7 %tiles.3.near_ref = f32[256,2176]{1,0:T(8,128)S(1)} custom-call(s32[2,64]{1,0:T(2,128)S(1)} %pad_add_fusion.table_ref, s32[1]{0:T(128)S(6)} %copy.26.count_ref, bf16[16,256,256]{2,1,0:T(8,128)(2,1)S(1)} %get-tuple-element.7.mixed_ref, bf16[64,256,128]{2,1,0:T(8,128)(2,1)S(1)} %bitcast.34, f32[256,2176]{1,0:T(8,128)S(1)} %tiles.2.before), custom_call_target="tpu_custom_call", output_to_operand_aliasing={{}: (4, {})} | custom-call | flops 536870912 | tf_op jit(solution)/shard_map/tiles/pallas_call | solution.py:94
  28.8 0.5 %expand0.1.early_ref = bf16[128,2048]{1,0:T(8,128)(2,1)S(1)} custom-call(bf16[128,256]{1,0:T(8,128)(2,1)S(1)} %maximum_select_fusion.2.coeff_ref, bf16[512,2048]{1,0:T(8,128)(2,1)S(1)} %bitcast.31, f32[256,2176]{1,0:T(8,128)S(1)} %tiles.3.near_ref), custom_call_target="tpu_custom_call" | custom-call | flops 268435456 | tf_op jit(solution)/shard_map/expand0/pallas_call | solution.py:135
  29.3 1.2 %expand1.1 = bf16[256,2048]{1,0:T(8,128)(2,1)} custom-call(s32[1,16]{1,0:T(1,128)S(1)} %copy-done.2, bf16[128,2048]{1,0:T(8,128)(2,1)S(1)} %expand0.1.early_ref, bf16[128,256]{1,0:T(8,128)(2,1)S(1)} %collective-permute-done.6.coeff_ref, bf16[512,2048]{1,0:T(8,128)(2,1)S(1)} %bitcast.32, f32[256,2176]{1,0:T(8,128)S(1)} %tiles.3.near_ref), custom_call_target="tpu_custom_call" | custom-call | flops 268435456 | tf_op jit(solution)/shard_map/expand1/pallas_call | solution.py:184
  (31 shorter events, 0.3 us)
Async XLA Ops:
  0.0 2.1 %copy-start.1 = (bf16[256,2048]{1,0:T(8,128)(2,1)S(1)}, bf16[256,2048]{1,0:T(8,128)(2,1)}, u32[]{:S(2)}) copy-start(bf16[256,2048]{1,0:T(8,128)(2,1)} %dens_ref.1) | copy-start | bytes 3145732
  2.8 3.6 %copy-start.4 = (s32[64,2]{0,1:T(2,128)S(1)}, s32[64,2]{0,1:T(2,128)}, u32[]{:S(2)}) copy-start(s32[64,2]{0,1:T(2,128)} %param.15) | copy-start | bytes 1540
  2.9 4.3 %copy-start.3 = (bf16[256,2,2048]{2,1,0:T(2,128)(2,1)S(1)}, bf16[256,2,2048]{2,1,0:T(2,128)(2,1)}, u32[]{:S(2)}) copy-start(bf16[256,2,2048]{2,1,0:T(2,128)(2,1)} %param.13) | copy-start | bytes 6291460
  3.0 8.1 %collective-permute-start = (bf16[128,256]{1,0:T(8,128)(2,1)S(1)}, bf16[128,256]{1,0:T(8,128)(2,1)S(1)}, u32[]{:S(2)}, u32[]{:S(2)}) collective-permute-start(bf16[128,256]{1,0:T(8,128)(2,1)S(1)} %pad_maximum_fusion.2), channel_id=1, source_target_pairs={{0,1},{1,0},{2,3},{3,2},{4,5},{5,4},{6,7},{7,6},{8,9},{9,8},{10,11... | collective-permute-start | bytes 196616 | tf_op jit(solution)/shard_map/ppermute | solution.py:30
  4.8 9.9 %collective-permute-start.1 = (bf16[3,2,256,128]{3,2,1,0:T(8,128)(2,1)S(1)}, bf16[3,2,256,128]{3,2,1,0:T(8,128)(2,1)S(1)}, u32[]{:S(2)}, u32[]{:S(2)}) collective-permute-start(bf16[3,2,256,128]{3,2,1,0:T(8,128)(2,1)S(1)} %bitcast.41), channel_id=1, source_target_pairs={{0,1},{1,0},{2,3},{3,2},{4,5},{5,4},{6,7},{7,6},{8,9},{9,8},{10,11... | collective-permute-start | bytes 1179656 | tf_op jit(solution)/shard_map/ppermute | solution.py:30
  6.0 9.0 %collective-permute-start.3 = (bf16[3,2,256,128]{3,2,1,0:T(8,128)(2,1)S(1)}, bf16[3,2,256,128]{3,2,1,0:T(8,128)(2,1)S(1)}, u32[]{:S(2)}, u32[]{:S(2)}) collective-permute-start(bf16[3,2,256,128]{3,2,1,0:T(8,128)(2,1)S(1)} %bitcast.39), channel_id=1, source_target_pairs={{0,1},{1,0},{2,3},{3,2},{4,5},{5,4},{6,7},{7,6},{8,9},{9,8},{10,11... | collective-permute-start | bytes 1179656 | tf_op jit(solution)/shard_map/ppermute | solution.py:30
  7.1 0.9 %copy-start.2 = (s32[1,16]{1,0:T(1,128)S(1)}, s32[1,16]{1,0:T(1,128)}, u32[]{:S(2)}) copy-start(s32[1,16]{1,0:T(1,128)} %order_ref.1) | copy-start | bytes 196
  7.2 2.2 %copy-start = (bf16[64,128,2,128]{3,2,1,0:T(2,128)(2,1)S(1)}, bf16[64,128,2,128]{3,2,1,0:T(2,128)(2,1)}, u32[]{:S(2)}) copy-start(bf16[64,128,2,128]{3,2,1,0:T(2,128)(2,1)} %param.14) | copy-start | bytes 12582916
  11.1 3.6 %collective-permute-start.2 = (bf16[128,256]{1,0:T(8,128)(2,1)S(1)}, bf16[128,256]{1,0:T(8,128)(2,1)S(1)}, u32[]{:S(2)}, u32[]{:S(2)}) collective-permute-start(bf16[128,256]{1,0:T(8,128)(2,1)S(1)} %fusion.6), channel_id=1, source_target_pairs={{0,2},{2,0},{4,6},{6,4},{8,10},{10,8},{12,14},{14,12},{1,3},{3,1},... | collective-permute-start | bytes 196616 | tf_op jit(solution)/shard_map/ppermute | solution.py:30
  15.4 3.2 %collective-permute-start.4 = (bf16[128,256]{1,0:T(8,128)(2,1)S(1)}, bf16[128,256]{1,0:T(8,128)(2,1)S(1)}, u32[]{:S(2)}, u32[]{:S(2)}) collective-permute-start(bf16[128,256]{1,0:T(8,128)(2,1)S(1)} %maximum_select_fusion), channel_id=1, source_target_pairs={{0,4},{2,6},{4,0},{6,2},{8,12},{10,14},{12,8},{14,10},{1,5},{3,7},... | collective-permute-start | bytes 196616 | tf_op jit(solution)/shard_map/ppermute | solution.py:30
  18.8 4.7 %collective-permute-start.5 = (bf16[128,256]{1,0:T(8,128)(2,1)S(1)}, bf16[128,256]{1,0:T(8,128)(2,1)S(1)}, u32[]{:S(2)}, u32[]{:S(2)}) collective-permute-start(bf16[128,256]{1,0:T(8,128)(2,1)S(1)} %maximum_select_fusion.1), channel_id=1, source_target_pairs={{0,8},{2,10},{4,12},{6,14},{8,0},{10,2},{12,4},{14,6},{1,9},{3,11}... | collective-permute-start | bytes 196616 | tf_op jit(solution)/shard_map/ppermute | solution.py:30
  23.7 5.5 %collective-permute-start.6 = (bf16[128,256]{1,0:T(8,128)(2,1)S(1)}, bf16[128,256]{1,0:T(8,128)(2,1)S(1)}, u32[]{:S(2)}, u32[]{:S(2)}) collective-permute-start(bf16[128,256]{1,0:T(8,128)(2,1)S(1)} %maximum_select_fusion.2.coeff_ref), channel_id=1, source_target_pairs={{0,1},{1,0},{2,3},{3,2},{4,5},{5,4},{6,7},{7,6},{8,9},{9,8},{10,11... | collective-permute-start | bytes 196616 | tf_op jit(solution)/shard_map/ppermute | solution.py:30
